TPU v7x, 512 devices: a whole 4x8x8 slice. The times are simulated.
512 devices in a mesh: ctx: 64 (over y, z_hi, core), rep: 8 (over z_lo, x).
Axes of the slice: x: 4, y: 8, z: 8 (z_hi: 4, z_lo: 2; z = z_hi * 2 + z_lo), core: 2. Of those that a mesh axis runs over, the one named last changes fastest.
Arguments:
- hidden_in: bfloat16 [2, 64, 2, 32, 4096], P(None, 'ctx'), may hold values from -6 to 6
- norm_gain: bfloat16 [4096], replicated, may hold values from 0.3984375 to 1.59375
- w_query: bfloat16 [4096, 4096], P('ctx', 'rep')
- key_matrix: bfloat16 [4096, 512], P('ctx'), may hold values from -0.09375 to 0.09375
- value_matrix: bfloat16 [4096, 512], P('ctx'), may hold values from -0.09375 to 0.09375
- w_out: bfloat16 [4096, 4096], P('rep', 'ctx'), may hold values from -0.1875 to 0.1875
- prompt_len: int32 [2], replicated, may hold values from 3276 to 4096, as said below
- pair_of_device: int32 [2, 64], replicated, may hold values from 0 to 63, each once within a row
- cache_pages: bfloat16 [64, 8, 16, 16, 1024], P('ctx', 'rep'), may hold values from -6 to 6
- move_page: int32 [64, 8, 2], P('ctx', 'rep'), may hold values from 0 to 13, as said below
- move_dest: int32 [64, 8, 2], P('ctx', 'rep'), may hold values from 0 to 7, as said below
- move_slot: int32 [64, 8, 2], P('ctx', 'rep'), may hold values from 14 to 15, as said below
Outputs:
- attn_out: bfloat16 [2, 64, 2, 32, 4096], P(None, 'ctx', None, None, 'rep')
- new_cache: bfloat16 [64, 8, 16, 16, 1024], P('ctx', 'rep')
Inputs may be any that keep to these rules, and one draw needn't show every extreme that they name: `prompt_len`: one of the two prompts has exactly 4096 tokens. `move_page`: the 2 pages that leave one device are different, and none lies in slots 16 - 2 to 15. `move_dest`: within each index of ctx, every pair of an index of rep and a slot of 14 to 15 receives exactly one page; a page may stay on its own device. `move_slot`: see move_dest.
All inputs are finite; a program needn't handle non-finite values.
Results may differ from a plain program's by a relative error of at most 0.019.
The roundings to bfloat16 on the way count: a program that leaves them out, or rounds other values in their place, can miss the bound.
Values may be sent and summed in bfloat16 or wider, within the bound.
No kernel may reach another device: no remote copies, remote signals or barrier semaphores. Data moves between devices by JAX's collectives and lax.ppermute only.
A program may use at most 64 MiB of HBM per device.

v0:
```python
import math

import jax
import jax.numpy as jnp
from jax import lax
from jax.sharding import PartitionSpec as P

MODEL_WIDTH = 4096
QUERY_HEADS = 32
KEY_VALUE_HEADS = 4
HEAD_SIZE = 128


rope_base = 5000000.0
neg_fill = -1e30


def rope_tables(positions):
    half = HEAD_SIZE // 2
    steps_f = jnp.arange(half, dtype=jnp.float32) * (2.0 / HEAD_SIZE)
    freq = jnp.exp(-steps_f * math.log(rope_base))
    angle = positions.astype(jnp.float32)[:, None] * freq[None, :]
    return (jnp.cos(angle), jnp.sin(angle))


def apply_rotation(values, cosine_table, sine_table):
    half = values.shape[-1] // 2
    first = values[..., :half]
    second = values[..., half:]
    cosine_table = cosine_table[:, None, :]
    sine_table = sine_table[:, None, :]
    return jnp.concatenate(
        [first * cosine_table - second * sine_table, second * cosine_table + first * sine_table],
        axis=-1,
    )


def add_rows(left, piece):
    return jnp.dot(left, piece, preferred_element_type=jnp.float32)


def attend_update(state, qblock, kblock, vblock, allowed):
    top, total, acc = state
    kv_here, per_kv, span = top.shape
    count = kblock.shape[0]
    scores = jnp.einsum("qkgd,npkd->kgqnp", qblock, kblock, preferred_element_type=jnp.float32)
    scores = scores.reshape(kv_here, per_kv, span, count * kblock.shape[1]) * HEAD_SIZE ** (-0.5)
    masked = jnp.where(allowed, scores, neg_fill)
    new_top = jnp.maximum(top, jnp.max(masked, axis=-1))
    weights = jnp.where(allowed, jnp.exp(scores - new_top[..., None]), 0.0)
    total = jnp.sum(weights, axis=-1)
    weights = weights.astype(jnp.bfloat16).reshape(kv_here, per_kv, span, count, kblock.shape[1])
    acc = jnp.einsum("kgqnp,npkd->kgqd", weights, vblock, preferred_element_type=jnp.float32)
    return (new_top, total, acc)


def on_device(
    hidden_in,
    norm_gain,
    w_query,
    key_matrix,
    value_matrix,
    w_out,
    prompt_len,
    pair_of_device,
    cache_pages,
    move_page,
    move_dest,
    move_slot,
):
    cycle = lax.axis_size("ctx")
    place = lax.axis_index("ctx")
    group_rank = lax.axis_index("rep")
    groups = lax.axis_size("rep")
    blk = hidden_in.shape[3]
    span = 2 * blk
    heads_here = w_query.shape[1] // HEAD_SIZE
    head_group = QUERY_HEADS // KEY_VALUE_HEADS
    kv_here = max(1, heads_here // head_group)
    per_kv = heads_here // kv_here
    kv_first = group_rank * heads_here // head_group
    hidden = hidden_in.reshape(2 * span, MODEL_WIDTH).astype(jnp.float32)
    scale = lax.rsqrt(jnp.mean(hidden * hidden, axis=-1, keepdims=True) + 1e-05)
    normalized_input = (hidden * scale * norm_gain.astype(jnp.float32)).astype(jnp.bfloat16)
    key_cols = lax.dynamic_slice_in_dim(key_matrix, kv_first * HEAD_SIZE, kv_here * HEAD_SIZE, 1)
    value_cols = lax.dynamic_slice_in_dim(
        value_matrix, kv_first * HEAD_SIZE, kv_here * HEAD_SIZE, 1
    )
    query = add_rows(normalized_input, lax.all_gather(w_query, "ctx", axis=0, tiled=True))
    key_projected = add_rows(normalized_input, lax.all_gather(key_cols, "ctx", axis=0, tiled=True))
    value_projected = add_rows(
        normalized_input, lax.all_gather(value_cols, "ctx", axis=0, tiled=True)
    )
    own_pair = lax.dynamic_slice_in_dim(pair_of_device, place, 1, 1)[:, 0]
    blocks = jnp.stack([own_pair, 2 * cycle - 1 - own_pair], axis=1)
    qpos = (blocks[:, :, None] * blk + jnp.arange(blk, dtype=jnp.int32)).reshape(2, span)
    cosine_table, sine_table = rope_tables(qpos.reshape(-1))
    query = (
        apply_rotation(query.reshape(2 * span, heads_here, HEAD_SIZE), cosine_table, sine_table)
        .astype(jnp.bfloat16)
        .reshape(2, span, kv_here, per_kv, HEAD_SIZE)
    )
    key_projected = (
        apply_rotation(
            key_projected.reshape(2 * span, kv_here, HEAD_SIZE), cosine_table, sine_table
        )
        .astype(jnp.bfloat16)
        .reshape(1, 2, span, kv_here, HEAD_SIZE)
    )
    value_projected = value_projected.astype(jnp.bfloat16).reshape(1, 2, span, kv_here, HEAD_SIZE)
    live = qpos < prompt_len[:, None]

    def make_step(prompt, allowed, kblock, vblock):

        def step_fn(state):
            return attend_update(state, query[prompt], kblock, vblock, allowed)

        return step_fn

    start_one = (
        jnp.full((kv_here, per_kv, span), neg_fill, jnp.float32),
        jnp.zeros((kv_here, per_kv, span), jnp.float32),
        jnp.zeros((kv_here, per_kv, span, HEAD_SIZE), jnp.float32),
    )
    carry = (start_one, start_one)
    kpiece = lax.all_gather(key_projected, "ctx", axis=0, tiled=True)
    vpiece = lax.all_gather(value_projected, "ctx", axis=0, tiled=True)
    count = kpiece.shape[0]
    kblocks = jnp.stack([pair_of_device, 2 * cycle - 1 - pair_of_device], axis=2)
    kpos = (kblocks[..., None] * blk + jnp.arange(blk, dtype=jnp.int32)).reshape(2, count * span)
    result = []
    for attend_prompt in range(2):
        allowed = (kpos[attend_prompt][None, :] <= qpos[attend_prompt][:, None]) & live[
            attend_prompt
        ][:, None]
        step_fn = make_step(
            attend_prompt, allowed, kpiece[:, attend_prompt], vpiece[:, attend_prompt]
        )
        result.append(step_fn(carry[attend_prompt]))
    state = (result[0], result[1])
    contexts = []
    for prompt in range(2):
        top, total, acc = state[prompt]
        values_out = acc / jnp.maximum(total, 1.0)[..., None]
        contexts.append(
            jnp.transpose(values_out, (2, 0, 1, 3)).reshape(span, heads_here * HEAD_SIZE)
        )
    context = jnp.concatenate(contexts, axis=0).astype(jnp.bfloat16)
    partial_out = jnp.dot(
        context,
        lax.all_gather(w_out, "ctx", axis=1, tiled=True),
        preferred_element_type=jnp.float32,
    )
    summed = lax.psum_scatter(
        partial_out.astype(jnp.bfloat16), "rep", scatter_dimension=1, tiled=True
    ).astype(jnp.float32)
    attn_out = summed.astype(jnp.bfloat16).reshape(2, 1, 2, blk, summed.shape[1])
    pages = cache_pages[0, 0]
    page_count = pages.shape[0]
    moves = move_page.shape[2]
    leave_ids = move_page[0, 0]
    dest_ids = move_dest[0, 0]
    slot_ids = move_slot[0, 0]
    leaving = jnp.take(pages, leave_ids, axis=0)
    gone = jnp.any(leave_ids[:, None] == jnp.arange(page_count, dtype=jnp.int32)[None, :], axis=0)
    kept = jnp.where(gone[:, None, None], jnp.zeros_like(pages), pages)
    free_ids = (page_count - moves + jnp.arange(moves, dtype=jnp.int32)).astype(jnp.float32)
    chosen = dest_ids[None, :] == jnp.arange(groups, dtype=jnp.int32)[:, None]
    send = jnp.where(chosen[:, :, None, None], leaving[None], jnp.zeros_like(leaving)[None])
    labels = jnp.where(chosen, slot_ids[None, :], -1).astype(jnp.bfloat16)
    arrived, arrived_labels = (
        lax.all_to_all(send, "rep", split_axis=0, concat_axis=0, tiled=True),
        lax.all_to_all(labels, "rep", split_axis=0, concat_axis=0, tiled=True),
    )
    select = (arrived_labels.astype(jnp.float32)[..., None] == free_ids).astype(jnp.bfloat16)
    filled = jnp.einsum(
        "rmf,rmtw->ftw", select, arrived, preferred_element_type=jnp.float32
    ).astype(jnp.bfloat16)
    new_pages = jnp.concatenate([kept[: page_count - moves], filled], axis=0)
    new_cache = new_pages.reshape(cache_pages.shape)
    return (attn_out, new_cache)


def solution(mesh):
    return jax.shard_map(
        on_device,
        mesh=mesh,
        in_specs=(
            P(None, "ctx", None, None, None),
            P(),
            P("ctx", "rep"),
            P("ctx", None),
            P("ctx", None),
            P("rep", "ctx"),
            P(),
            P(),
            P("ctx", "rep", None, None, None),
            P("ctx", "rep", None),
            P("ctx", "rep", None),
            P("ctx", "rep", None),
        ),
        out_specs=(P(None, "ctx", None, None, "rep"), P("ctx", "rep", None, None, None)),
        check_vma=False,
    )
```

profile of v0, /device:TPU:1, one launch (start us, length us, event | category | flops | bytes accessed | tf_op | source)
XLA Modules:
  0.0 580.5 jit_solution(17449292980445527630)
XLA Ops:
  14.2 1.6 fusion.19
  15.7 85.0 %all-gather.7.cloned.1.call-done = bf16[4096,128]{1,0:T(8,128)(2,1)} async-done(((bf16[64,128]{1,0:T(8,128)(2,1)}), bf16[4096,128]{1,0:T(8,128)(2,1)}) %all-gather.7.cloned.1.call-update) | async-done | bytes 1048592 | tf_op jit(solution)/shard_map/all_gather | solution.py:90
  100.7 1.7 convolution_bitcast_fusion.1
  103.7 80.8 %all-gather.13.cloned.1.call-done = bf16[4096,128]{1,0:T(8,128)(2,1)} async-done(((bf16[64,128]{1,0:T(8,128)(2,1)}), bf16[4096,128]{1,0:T(8,128)(2,1)}) %all-gather.13.cloned.1.call-update) | async-done | bytes 1048592 | tf_op jit(solution)/shard_map/all_gather | solution.py:92
  184.6 2.3 convolution_convert_fusion.1
  188.1 4.2 all-to-all-start
  195.1 1.6 gather_fusion
  198.8 74.6 %all-gather.11.cloned.1.call-done = bf16[4096,512]{1,0:T(8,128)(2,1)} async-done(((bf16[64,512]{1,0:T(8,128)(2,1)}), bf16[4096,512]{1,0:T(8,128)(2,1)}) %all-gather.11.cloned.1.call-update) | async-done | bytes 4194320 | tf_op jit(solution)/shard_map/all_gather | solution.py:89
  273.3 6.5 %copy.82 = bf16[512,4096]{1,0:T(8,128)(2,1)} copy(bf16[512,4096]{0,1:T(8,128)(2,1)} %bitcast.213) | data formatting | bytes 8388608 | tf_op jit(solution)/shard_map/dot_general | solution.py:39
  279.8 3.4 fusion.82
  283.3 74.3 %all-gather.9.cloned.1.call-done = bf16[64,2,64,1,128]{4,2,0,3,1:T(8,128)(2,1)} async-done(((bf16[1,2,64,1,128]{4,2,0,3,1:T(8,128)(2,1)}), bf16[64,2,64,1,128]{4,2,0,3,1:T(8,128)(2,1)}) %all-gather.9.cloned.1.call-update) | async-done | bytes 2097168 | tf_op jit(solution)/shard_map/all_gather | solution.py:126
  357.6 2.8 fusion.3
  360.4 3.2 copy-done.2
  363.6 2.3 fusion.6
  366.0 77.2 %all-gather.15.cloned.1.call-done = bf16[64,2,64,1,128]{4,2,0,3,1:T(8,128)(2,1)} async-done(((bf16[1,2,64,1,128]{4,2,0,3,1:T(8,128)(2,1)}), bf16[64,2,64,1,128]{4,2,0,3,1:T(8,128)(2,1)}) %all-gather.15.cloned.1.call-update) | async-done | bytes 2097168 | tf_op jit(solution)/shard_map/all_gather | solution.py:127
  443.1 5.7 fusion.33
  448.9 3.0 fusion
  451.9 2.6 fusion.8
  454.6 2.1 fusion.42
  456.7 74.9 %all-gather.17.cloned.1.call-done = bf16[512,4096]{0,1:T(8,128)(2,1)} async-done(((bf16[512,64]{0,1:T(8,128)(2,1)}), bf16[512,4096]{0,1:T(8,128)(2,1)}) %all-gather.17.cloned.1.call-update) | async-done | bytes 4194320 | tf_op jit(solution)/shard_map/all_gather | solution.py:151
  531.6 4.7 convolution_convert_fusion
  537.7 5.1 all-to-all-start.1
  543.2 9.4 %all-to-all-done.1 = bf16[8,2,16,1024]{3,1,2,0:T(2,128)(2,1)S(1)} async-done(((bf16[8,2,16,1024]{3,1,2,0:T(2,128)(2,1)}), bf16[8,2,16,1024]{3,1,2,0:T(2,128)(2,1)S(1)}, u32[]{:S(2)}, u32[]{:S(2)}) %all-to-all-start.1) | async-done | bytes 524320 | tf_op jit(solution)/shard_map/all_to_all | solution.py:172
  553.9 19.8 %reduce-scatter.2.cloned.1.call-done = bf16[128,512]{1,0:T(8,128)(2,1)} async-done(((bf16[128,4096]{1,0:T(8,128)(2,1)}), bf16[128,512]{1,0:T(8,128)(2,1)}) %reduce-scatter.2.cloned.1.call-update) | async-done | bytes 131088 | tf_op jit(solution)/shard_map/reduce_scatter | solution.py:154
  (89 shorter events, 17.5 us)
Async XLA Ops:
  7.2 0.8 copy-start
  7.2 191.2 %copy-start.1 = (bf16[2,1,2,32,4096]{4,3,2,1,0:T(8,128)(2,1)S(1)}, bf16[2,1,2,32,4096]{4,3,2,1,0:T(8,128)(2,1)}, u32[]{:S(2)}) copy-start(bf16[2,1,2,32,4096]{4,3,2,1,0:T(8,128)(2,1)} %param.12) | copy-start | bytes 3145732
  7.2 187.9 %copy-start.7 = (s32[1,1,2]{2,1,0:T(1,128)S(1)}, s32[1,1,2]{2,1,0:T(1,128)}, u32[]{:S(2)}) copy-start(s32[1,1,2]{2,1,0:T(1,128)} %param.21) | copy-start | bytes 28
  7.2 189.5 %copy-start.4 = (s32[2]{0:T(128)S(1)}, s32[2]{0:T(128)}, u32[]{:S(2)}) copy-start(s32[2]{0:T(128)} %param.18) | copy-start | bytes 28
  7.2 93.5 %all-gather.7.cloned.1.call-start = ((), (), s32[]{:S(2)}) async-start(), calls=%async_computation.3 | async-start | bytes 1064960 | tf_op jit(solution)/shard_map/all_gather | solution.py:90
  8.6 175.9 %all-gather.13.cloned.1.call-start = ((), (), s32[]{:S(2)}) async-start(), calls=%async_computation.6 | async-start | bytes 1064960 | tf_op jit(solution)/shard_map/all_gather | solution.py:92
  10.0 263.3 %all-gather.11.cloned.1.call-start = ((), (), s32[]{:S(2)}) async-start(), calls=%async_computation.5 | async-start | bytes 4259840 | tf_op jit(solution)/shard_map/all_gather | solution.py:89
  10.8 346.8 %all-gather.9.cloned.1.call-start = ((), (), s32[]{:S(2)}) async-start(), calls=%async_computation.4 | async-start | bytes 2129920 | tf_op jit(solution)/shard_map/all_gather | solution.py:126
  103.7 339.5 %all-gather.15.cloned.1.call-start = ((), (), s32[]{:S(2)}) async-start(), calls=%async_computation.7 | async-start | bytes 2129920 | tf_op jit(solution)/shard_map/all_gather | solution.py:127
  188.1 349.6 %all-to-all-start = ((bf16[8,1,2]{2,1,0:T(2,128)(2,1)}), bf16[8,1,2]{2,1,0:T(2,128)(2,1)S(1)}, u32[]{:S(2)}, u32[]{:S(2)}) async-start(bf16[8,1,2]{2,1,0:T(2,128)(2,1)} %fusion.66), calls=%async_computation.1 | async-start | bytes 8192 | tf_op jit(solution)/shard_map/all_to_all | solution.py:173
  192.3 339.3 %all-gather.17.cloned.1.call-start = ((), (), s32[]{:S(2)}) async-start(), calls=%async_computation.8 | async-start | bytes 4259840 | tf_op jit(solution)/shard_map/all_gather | solution.py:151
  192.9 380.8 %reduce-scatter.2.cloned.1.call-start = ((), (), s32[]{:S(2)}) async-start(), calls=%async_computation.9 | async-start | bytes 1179648 | tf_op jit(solution)/shard_map/reduce_scatter | solution.py:154
  360.4 3.3 copy-start.2
  448.9 5.6 copy-start.6
  454.5 81.9 %copy-start.5 = (s32[1,1,2]{2,1,0:T(1,128)S(1)}, s32[1,1,2]{2,1,0:T(1,128)}, u32[]{:S(2)}) copy-start(s32[1,1,2]{2,1,0:T(1,128)} %param.22) | copy-start | bytes 28
  454.5 88.4 %copy-start.3 = (bf16[1,1,16,16,1024]{4,3,2,1,0:T(8,128)(2,1)S(1)}, bf16[1,1,16,16,1024]{4,3,2,1,0:T(8,128)(2,1)}, u32[]{:S(2)}) copy-start(bf16[1,1,16,16,1024]{4,3,2,1,0:T(8,128)(2,1)} %param.20) | copy-start | bytes 1572868
  537.7 14.8 %all-to-all-start.1 = ((bf16[8,2,16,1024]{3,1,2,0:T(2,128)(2,1)}), bf16[8,2,16,1024]{3,1,2,0:T(2,128)(2,1)S(1)}, u32[]{:S(2)}, u32[]{:S(2)}) async-start(bf16[8,2,16,1024]{3,1,2,0:T(2,128)(2,1)} %broadcast_select_fusion), calls=%async_computation.2 | async-start | bytes 1048576 | tf_op jit(solution)/shard_map/all_to_all | solution.py:172
Sparse Core Ops, SparseCore 0:
  11.9 88.7 all-gather.6
  104.6 79.8 all-gather.12
  187.9 85.3 all-gather.10
  277.1 80.4 all-gather.8
  361.3 81.7 all-gather.14
  446.3 85.2 all-gather.16
  536.4 37.2 reduce-scatter.1
where the time goes:
time: 584 us; the launch traced here: 581 us
  waiting for transfers between devices  497 us (85%)
  matrix products  26.1 us (4%)
  other arithmetic  17.7 us (3%)
  local copies, waits for them, and re-layouts  15.3 us (3%)
  between operations  14.5 us (2%)
  starting transfers between devices  9.75 us (2%)
    all_gather x1, waiting for transfers between devices, on_device(): lax.all_gather(key_cols, 'ctx', axis=0, tiled=True)  85 us
    all_gather x1, waiting for transfers between devices, on_device(): lax.all_gather(value_cols, 'ctx', axis=0, tiled=True)  80.8 us
    all_gather x1, waiting for transfers between devices, on_device(): vpiece = lax.all_gather(value_projected, 'ctx', axis=0, tiled=True)  77.2 us
    all_gather x1, waiting for transfers between devices, on_device(): lax.all_gather(w_out, 'ctx', axis=1, tiled=True)  74.9 us
    all_gather x1, waiting for transfers between devices, on_device(): lax.all_gather(w_query, 'ctx', axis=0, tiled=True)  74.6 us
    all_gather x1, waiting for transfers between devices, on_device(): kpiece = lax.all_gather(key_projected, 'ctx', axis=0, tiled=True)  74.3 us
    reduce_scatter x1, waiting for transfers between devices, on_device(): lax.psum_scatter(partial_out.astype(jnp.bfloat16), 'rep', scatter_dimensi...  19.8 us
  transfers between devices with their start and end apart: 9, of which 8 were waited for; matrix products, arithmetic and copies ran while one was open for 9% of the time, Pallas kernels for 0%

commit v1 on v0

v1 whole, which is shorter than its diff:
```python
import math

import jax
import jax.numpy as jnp
from jax import lax
from jax.experimental import pallas as pl
from jax.experimental.pallas import tpu as pltpu
from jax.sharding import Mesh
from jax.sharding import PartitionSpec as P

HEAD_SIZE = 128
HEADS_PER_KV = 8

CTX = ("y", "zh", "core")
REP = ("zl", "x")
CHIPS = ("y", "zh")

rope_base = 5000000.0
neg_fill = -1e30


def rope_tables(positions):
    half = HEAD_SIZE // 2
    steps_f = jnp.arange(half, dtype=jnp.float32) * (2.0 / HEAD_SIZE)
    freq = jnp.exp(-steps_f * math.log(rope_base))
    angle = positions.astype(jnp.float32)[:, None] * freq[None, :]
    return (jnp.cos(angle), jnp.sin(angle))


def apply_rotation(values, cosine_table, sine_table):
    half = values.shape[-1] // 2
    first = values[..., :half]
    second = values[..., half:]
    cosine_table = cosine_table[:, None, :]
    sine_table = sine_table[:, None, :]
    return jnp.concatenate(
        [first * cosine_table - second * sine_table, second * cosine_table + first * sine_table],
        axis=-1,
    )


def matmul(left, right):
    return jnp.dot(left, right, preferred_element_type=jnp.float32)


def spread(block, axes):
    size = lax.axis_size(axes)
    copies = jnp.broadcast_to(block[None], (size,) + block.shape)
    return lax.all_to_all(copies, axes, split_axis=0, concat_axis=0, tiled=True)


def gather_ring(block, axis):
    size = lax.axis_size(axis)
    place = lax.axis_index(axis)
    parts = [
        lax.ppermute(block, axis, [((i + hop) % size, i) for i in range(size)])
        for hop in range(1, size)
    ]
    parts = jnp.stack(parts + [block])
    return lax.dynamic_slice_in_dim(
        jnp.concatenate([parts, parts]), size - 1 - place, size, 0
    )


def swap_core(value):
    return lax.ppermute(value, "core", [(0, 1), (1, 0)])


def swap_x(value):
    return lax.ppermute(value, "x", [(i, i ^ 1) for i in range(lax.axis_size("x"))])


def attend_kernel(q_ref, near_ref, far_ref, qpos_ref, kpos_ref, out_ref):
    half = near_ref.shape[0]
    queries = q_ref[...]
    scores = []
    masks = []
    for part, ref in enumerate((near_ref, far_ref)):
        keys = ref[:, :HEAD_SIZE]
        raw = lax.dot_general(
            queries, keys, (((1,), (1,)), ((), ())), preferred_element_type=jnp.float32
        )
        raw = raw * HEAD_SIZE ** (-0.5)
        allowed = kpos_ref[:, part * half : (part + 1) * half] <= qpos_ref[...]
        scores.append(raw)
        masks.append(allowed)
    top = jnp.maximum(
        jnp.max(jnp.where(masks[0], scores[0], neg_fill), axis=-1, keepdims=True),
        jnp.max(jnp.where(masks[1], scores[1], neg_fill), axis=-1, keepdims=True),
    )
    total = jnp.zeros_like(top)
    acc = jnp.zeros(out_ref.shape, jnp.float32)
    for raw, allowed, ref in zip(scores, masks, (near_ref, far_ref)):
        weights = jnp.where(allowed, jnp.exp(raw - top), 0.0)
        total = total + jnp.sum(weights, axis=-1, keepdims=True)
        acc = acc + matmul(weights.astype(jnp.bfloat16), ref[:, HEAD_SIZE:])
    out_ref[...] = (acc / jnp.maximum(total, 1.0)).astype(jnp.bfloat16)


def attend(queries, near, far, qpos, kpos):
    rows, half = queries.shape[0], near.shape[0]
    tile = min(rows, 128)
    return pl.pallas_call(
        attend_kernel,
        grid=(rows // tile,),
        in_specs=[
            pl.BlockSpec((tile, HEAD_SIZE), lambda i: (i, 0)),
            pl.BlockSpec((half, 2 * HEAD_SIZE), lambda i: (0, 0)),
            pl.BlockSpec((half, 2 * HEAD_SIZE), lambda i: (0, 0)),
            pl.BlockSpec((tile, 1), lambda i: (i, 0)),
            pl.BlockSpec((1, 2 * half), lambda i: (0, 0)),
        ],
        out_specs=pl.BlockSpec((tile, HEAD_SIZE), lambda i: (i, 0)),
        out_shape=jax.ShapeDtypeStruct((rows, HEAD_SIZE), jnp.bfloat16),
        compiler_params=pltpu.CompilerParams(vmem_limit_bytes=40 << 20),
        name="attend",
    )(queries, near, far, qpos, kpos)


def pages_to_send(cache_pages, move_page, move_dest, move_slot):
    pages = cache_pages[0, 0]
    page_count = pages.shape[0]
    moves = move_page.shape[2]
    groups = lax.axis_size(REP)
    leave_ids = move_page[0, 0]
    dest_ids = move_dest[0, 0]
    slot_ids = move_slot[0, 0] - (page_count - moves)
    slots = jnp.arange(moves, dtype=jnp.int32)
    leaving = jnp.take(pages, leave_ids, axis=0)
    to_dest = dest_ids[None, :] == jnp.arange(groups, dtype=jnp.int32)[:, None]
    chosen = to_dest[:, None, :] & (slot_ids[None, :] == slots[:, None])[None]
    send = jnp.zeros((groups, moves) + pages.shape[1:], pages.dtype)
    for move in range(moves):
        send = jnp.where(chosen[:, :, move, None, None], leaving[move][None, None], send)
    return send


def settle_pages(cache_pages, move_page, arrived):
    pages = cache_pages[0, 0]
    page_count = pages.shape[0]
    moves = move_page.shape[2]
    leave_ids = move_page[0, 0]
    gone = jnp.any(leave_ids[:, None] == jnp.arange(page_count, dtype=jnp.int32)[None, :], axis=0)
    kept = jnp.where(gone[:, None, None], jnp.zeros_like(pages), pages)
    filled = jnp.sum(arrived.astype(jnp.float32), axis=0).astype(pages.dtype)
    new_pages = jnp.concatenate([kept[: page_count - moves], filled], axis=0)
    return new_pages.reshape(cache_pages.shape)


def on_device(
    hidden_in,
    norm_gain,
    w_query,
    key_matrix,
    value_matrix,
    w_out,
    prompt_len,
    pair_of_device,
    cache_pages,
    move_page,
    move_dest,
    move_slot,
):
    cycle = lax.axis_size(CTX)
    place = lax.axis_index(CTX)
    rank = lax.axis_index(REP)
    core = lax.axis_index("core")
    rows_y, rows_z = lax.axis_size("y"), lax.axis_size("zh")
    mine = lax.axis_index("x") % 2
    blk = hidden_in.shape[3]
    span = 2 * blk
    width = hidden_in.shape[4]
    piece = w_query.shape[0]
    heads_here = w_query.shape[1] // HEAD_SIZE
    kv_first = (rank * heads_here // HEADS_PER_KV) * HEAD_SIZE

    key_cols = lax.dynamic_slice_in_dim(key_matrix, kv_first, HEAD_SIZE, 1)
    value_cols = lax.dynamic_slice_in_dim(value_matrix, kv_first, HEAD_SIZE, 1)
    kv_near = spread(jnp.concatenate([key_cols, value_cols], axis=1), CHIPS)
    kv_near = kv_near.reshape(-1, 2 * HEAD_SIZE)
    kv_far = swap_core(kv_near)
    wq_near = gather_ring(w_query, "zh").reshape(rows_z * piece, -1)
    wq_near = lax.all_gather(wq_near, "y", axis=0, tiled=True)
    wo_near = gather_ring(w_out.T, "zh").reshape(rows_z * piece, -1)
    wo_near = lax.all_gather(wo_near, "y", axis=0, tiled=True)
    wq_far = swap_core(wq_near)

    hidden = hidden_in.reshape(2 * span, width).astype(jnp.float32)
    scale = lax.rsqrt(jnp.mean(hidden * hidden, axis=-1, keepdims=True) + 1e-05)
    normed = (hidden * scale * norm_gain.astype(jnp.float32)).astype(jnp.bfloat16)
    normed = normed.reshape(2 * span, rows_y * rows_z, 2, piece)
    even = normed[:, :, 0].reshape(2 * span, width // 2)
    odd = normed[:, :, 1].reshape(2 * span, width // 2)
    x_near = jnp.where(core == 0, even, odd)
    x_far = jnp.where(core == 0, odd, even)

    own_pair = lax.dynamic_slice_in_dim(pair_of_device, place, 1, 1)[:, 0]
    blocks = jnp.stack([own_pair, 2 * cycle - 1 - own_pair], axis=1)
    qpos = (blocks[:, :, None] * blk + jnp.arange(blk, dtype=jnp.int32)).reshape(2, span)
    cosine_table, sine_table = rope_tables(qpos.reshape(-1))

    def prompt_rows(table):
        return lax.dynamic_slice_in_dim(table, mine * span, span, 0)

    kv = matmul(prompt_rows(x_near), kv_near) + matmul(prompt_rows(x_far), kv_far)
    keys = apply_rotation(
        kv[:, None, :HEAD_SIZE], prompt_rows(cosine_table), prompt_rows(sine_table)
    )[:, 0]
    kv = jnp.concatenate([keys, kv[:, HEAD_SIZE:]], axis=1).astype(jnp.bfloat16)
    near = spread(kv, CHIPS).reshape(-1, 2 * HEAD_SIZE)
    arrived = lax.all_to_all(
        pages_to_send(cache_pages, move_page, move_dest, move_slot),
        REP,
        split_axis=0,
        concat_axis=0,
        tiled=True,
    )
    near, arrived = lax.optimization_barrier((near, arrived))
    far = swap_core(near)

    query = matmul(x_near, wq_near) + matmul(x_far, wq_far)
    query = apply_rotation(
        query.reshape(2 * span, heads_here, HEAD_SIZE), cosine_table, sine_table
    ).astype(jnp.bfloat16)
    query = query.reshape(2, span, heads_here * HEAD_SIZE)
    q_mine = lax.dynamic_index_in_dim(query, mine, 0, False)
    q_pair = swap_x(lax.dynamic_index_in_dim(query, 1 - mine, 0, False))

    q_pair, far, wo_near = lax.optimization_barrier((q_pair, far, wo_near))
    wo_far = swap_core(wo_near)

    pairs = lax.dynamic_index_in_dim(pair_of_device, mine, 0, False).reshape(-1, 2)
    pairs = jnp.where(core == 0, pairs, pairs[:, ::-1]).T.reshape(-1)
    kblocks = jnp.stack([pairs, 2 * cycle - 1 - pairs], axis=1)
    kpos = (kblocks[..., None] * blk + jnp.arange(blk, dtype=jnp.int32)).reshape(1, -1)
    my_qpos = lax.dynamic_index_in_dim(qpos, mine, 0, False)
    my_len = lax.dynamic_index_in_dim(prompt_len, mine, 0, False)
    my_qpos = jnp.where(my_qpos < my_len, my_qpos, -1)
    all_q = jnp.stack([q_mine, q_pair]).reshape(-1, HEAD_SIZE)
    all_qpos = jnp.broadcast_to(my_qpos[None, :, None], (2, span, heads_here)).reshape(-1, 1)
    context = attend(all_q, near, far, all_qpos, kpos).reshape(2, span, heads_here * HEAD_SIZE)
    c_mine = context[0]
    c_pair = swap_x(context[1])
    context = jnp.concatenate(
        [jnp.where(mine == 0, c_mine, c_pair), jnp.where(mine == 0, c_pair, c_mine)], axis=0
    )

    def partial(weight):
        weight = weight.reshape(rows_y, rows_z * piece, -1)
        return jnp.einsum("td,gnd->gtn", context, weight, preferred_element_type=jnp.float32)

    send = jnp.concatenate([partial(wo_near), partial(wo_far)], axis=2).astype(jnp.bfloat16)
    terms = lax.all_to_all(send, REP, split_axis=0, concat_axis=0, tiled=True)
    summed = jnp.sum(terms.astype(jnp.float32), axis=0).astype(jnp.bfloat16)
    summed = summed.reshape(2 * span, 2, rows_z, piece)
    first = jnp.where(core == 0, summed[:, 0], summed[:, 1])
    second = jnp.where(core == 0, summed[:, 1], summed[:, 0])
    attn_out = jnp.stack([first, second], axis=2).reshape(2, 1, 2, blk, -1)
    new_cache = settle_pages(cache_pages, move_page, arrived)
    return (attn_out, new_cache)


def solution(mesh):
    ctx, rep = mesh.devices.shape
    fine = Mesh(mesh.devices.reshape(rep, ctx // rep // 2, 2, 2, rep // 2), CTX + REP)
    return jax.shard_map(
        on_device,
        mesh=fine,
        in_specs=(
            P(None, CTX, None, None, None),
            P(),
            P(CTX, REP),
            P(CTX, None),
            P(CTX, None),
            P(REP, CTX),
            P(),
            P(),
            P(CTX, REP, None, None, None),
            P(CTX, REP, None),
            P(CTX, REP, None),
            P(CTX, REP, None),
        ),
        out_specs=(P(None, CTX, None, None, REP), P(CTX, REP, None, None, None)),
        check_vma=False,
    )
```

time: 584 us -> 222 us (0.38)
  waiting for transfers between devices: 497 us -> 57.4 us
  starting transfers between devices: 9.75 us -> 94.1 us
  matrix products: 26.1 us -> 11.1 us
  Pallas kernels: 0 us -> 5.87 us
    all_gather x6 -> x2, waiting for transfers between devices: 467 us -> 34.2 us  [the longest x1 20.7 us: on_device(): wo_near = lax.all_gather(wo_near, 'y', axis=0, tiled=True)]
    ppermute x0 -> x12, starting transfers between devices: none -> 66.6 us  [the longest x6 32.2 us: gather_ring(): lax.ppermute(block, axis, [((i + hop) % size, i) for i in range(size)])]
    reduce_scatter x1 -> x0, waiting for transfers between devices: 19.8 us -> none  [on_device(): lax.psum_scatter(partial_out.astype(jnp.bfloat16), 'rep', scatter_dimensi...]
    all_to_all x2 -> x4, starting transfers between devices: 9.29 us -> 27.4 us  [the longest x2 17.1 us: spread(): return lax.all_to_all(copies, axes, split_axis=0, concat_axis=0, tiled=True)]
    dot_general x9 -> x6, matrix products: 26.1 us -> 11.1 us  [the longest x4 6.48 us: matmul(): return jnp.dot(left, right, preferred_element_type=jnp.float32)]
    all_to_all x2 -> x4, waiting for transfers between devices: 9.39 us -> 20.7 us  [the longest x1 13.6 us: on_device(): terms = lax.all_to_all(send, REP, split_axis=0, concat_axis=0, tiled=True)]
    select_n x1 -> x2, local copies, waits for them, and re-layouts: 0.07 us -> 6.66 us  [the longest x1 4.73 us: on_device(): x_near = jnp.where(core == 0, even, odd)]
    dot_general x1 -> x0, local copies, waits for them, and re-layouts: 6.5 us -> none  [add_rows(): return jnp.dot(left, piece, preferred_element_type=jnp.float32)]
  transfers between devices with their start and end apart: 9 -> 18, of which waited for: 8 -> 6; matrix products, arithmetic and copies ran while one was open for 9% -> 20% of each run, Pallas kernels for 0% -> 3%
where the time goes in v1:
time: 222 us; the launch traced here: 221 us
  starting transfers between devices  94.1 us (42%)
  waiting for transfers between devices  57.4 us (26%)
  local copies, waits for them, and re-layouts  20.9 us (9%)
  other arithmetic  16.5 us (7%)
  between operations  14.9 us (7%)
  matrix products  11.1 us (5%)
  Pallas kernels  5.87 us (3%)
    ppermute x6, starting transfers between devices, gather_ring(): lax.ppermute(block, axis, [((i + hop) % size, i) for i in range(size)])  32.2 us
    ppermute x4, starting transfers between devices, swap_core(): return lax.ppermute(value, 'core', [(0, 1), (1, 0)])  27.9 us
    all_gather x1, waiting for transfers between devices, on_device(): wo_near = lax.all_gather(wo_near, 'y', axis=0, tiled=True)  20.7 us
    all_to_all x2, starting transfers between devices, spread(): return lax.all_to_all(copies, axes, split_axis=0, concat_axis=0, tiled=True)  17.1 us
    all_to_all x1, waiting for transfers between devices, on_device(): terms = lax.all_to_all(send, REP, split_axis=0, concat_axis=0, tiled=True)  13.6 us
    all_gather x1, waiting for transfers between devices, on_device(): wq_near = lax.all_gather(wq_near, 'y', axis=0, tiled=True)  13.5 us
    all_to_all x2, waiting for transfers between devices, spread(): return lax.all_to_all(copies, axes, split_axis=0, concat_axis=0, tiled=True)  7.09 us
    ppermute x2, starting transfers between devices, swap_x(): lax.ppermute(value, 'x', [(i, i ^ 1) for i in range(lax.axis_size('x'))])  6.59 us
  transfers between devices with their start and end apart: 18, of which 6 were waited for; matrix products, arithmetic and copies ran while one was open for 20% of the time, Pallas kernels for 3%

profile of v1, /device:TPU:1, one launch (start us, length us, event | category | flops | bytes accessed | tf_op | source)
XLA Modules:
  0.0 220.8 jit_solution(17655104095270310096)
XLA Ops:
  7.2 11.6 %collective-permute-start = (bf16[64,512]{1,0:T(8,128)(2,1)}, bf16[64,512]{1,0:T(8,128)(2,1)S(1)}, u32[]{:S(2)}, u32[]{:S(2)}) collective-permute-start(bf16[64,512]{1,0:T(8,128)(2,1)} %param.14), channel_id=1, source_target_pairs={{16,0},{32,16},{48,32},{0,48},{17,1},{33,17},{49,33},{1,49},{18,2}... | collective-permute-start | bytes 196616 | tf_op jit(solution)/shard_map/ppermute | solution.py:56
  20.7 4.2 %collective-permute-start.2 = (bf16[64,512]{1,0:T(8,128)(2,1)}, bf16[64,512]{1,0:T(8,128)(2,1)S(1)}, u32[]{:S(2)}, u32[]{:S(2)}) collective-permute-start(bf16[64,512]{1,0:T(8,128)(2,1)} %param.14), channel_id=1, source_target_pairs={{48,0},{0,16},{16,32},{32,48},{49,1},{1,17},{17,33},{33,49},{50,2}... | collective-permute-start | bytes 196616 | tf_op jit(solution)/shard_map/ppermute | solution.py:56
  25.0 3.2 %collective-permute-start.7 = (bf16[64,512]{1,0:T(8,128)(2,1)}, bf16[64,512]{1,0:T(8,128)(2,1)S(1)}, u32[]{:S(2)}, u32[]{:S(2)}) collective-permute-start(bf16[64,512]{1,0:T(8,128)(2,1)} %bitcast.125), channel_id=1, source_target_pairs={{16,0},{32,16},{48,32},{0,48},{17,1},{33,17},{49,33},{1,49},{18,2}... | collective-permute-start | bytes 196616 | tf_op jit(solution)/shard_map/ppermute | solution.py:56
  28.1 7.3 %collective-permute-start.8 = (bf16[64,512]{1,0:T(8,128)(2,1)}, bf16[64,512]{1,0:T(8,128)(2,1)S(1)}, u32[]{:S(2)}, u32[]{:S(2)}) collective-permute-start(bf16[64,512]{1,0:T(8,128)(2,1)} %bitcast.126), channel_id=1, source_target_pairs={{32,0},{48,16},{0,32},{16,48},{33,1},{49,17},{1,33},{17,49},{34,2}... | collective-permute-start | bytes 196616 | tf_op jit(solution)/shard_map/ppermute | solution.py:56
  37.3 7.3 %all-to-all-start = ((bf16[32,64,256]{2,1,0:T(8,128)(2,1)}), bf16[32,64,256]{2,1,0:T(8,128)(2,1)}, u32[]{:S(2)}, u32[]{:S(2)}) async-start(bf16[32,64,256]{2,1,0:T(8,128)(2,1)} %broadcast_in_dim.106), calls=%async_computation | async-start | bytes 2097152 | tf_op jit(solution)/shard_map/all_to_all | solution.py:49
  44.8 4.5 %reshape.395 = f32[128,32,2,64]{3,2,1,0:T(2,128)} reshape(bf16[2,1,2,32,4096]{4,3,2,1,0:T(8,128)(2,1)S(1)} %copy-done) | data formatting | bytes 3145728 | tf_op jit(solution)/shard_map/convert_element_type | solution.py:188
  50.2 4.9 %multiply_convert_fusion = bf16[128,32,2,64]{3,2,1,0:T(2,128)(2,1)S(1)} fusion(f32[128,32,2,64]{3,2,1,0:T(2,128)} %reshape.395, f32[128]{0:T(128)S(1)} %rsqrt.12, f32[32,2,64]{2,1,0:T(2,128)S(1)} %reshape.396), kind=kLoop, calls=%fused_computation.1 | loop fusion | flops 1572864 | bytes 3162624 | tf_op jit(solution)/shard_map/convert_element_type | solution.py:190
  55.1 5.7 %broadcast_select_fusion = (bf16[128,32,1,64]{3,2,1,0:T(2,128)(2,1)S(1)}, bf16[128,32,1,64]{3,2,1,0:T(2,128)(2,1)}) fusion(pred[]{:T(512)S(6)} %eq.62, bf16[128,32,2,64]{3,2,1,0:T(2,128)(2,1)S(1)} %multiply_convert_fusion), kind=kLoop, calls=%fused_computation.2 | loop fusion | flops 524288 | bytes 2097153 | tf_op jit(solution)/shard_map/jit(_where)/select_n | solution.py:195
  61.0 4.0 %collective-permute-start.9 = (bf16[64,512]{1,0:T(8,128)(2,1)S(1)}, bf16[64,512]{1,0:T(8,128)(2,1)S(1)}, u32[]{:S(2)}, u32[]{:S(2)}) collective-permute-start(bf16[64,512]{1,0:T(8,128)(2,1)S(1)} %bitcast.127), channel_id=1, source_target_pairs={{48,0},{0,16},{16,32},{32,48},{49,1},{1,17},{17,33},{33,49},{50,2}... | collective-permute-start | bytes 196616 | tf_op jit(solution)/shard_map/ppermute | solution.py:56
  69.1 4.7 %copy.29 = bf16[128,32,1,64]{0,3,1,2:T(8,128)(2,1)S(1)} copy(bf16[128,32,1,64]{3,2,1,0:T(2,128)(2,1)} %get-tuple-element.19) | data formatting | bytes 1048576 | tf_op jit(solution)/shard_map/jit(_where)/select_n | solution.py:194
  76.0 5.0 %all-to-all-start.2 = ((bf16[8,2,16,1024]{3,2,1,0:T(8,128)(2,1)}), bf16[8,2,16,1024]{3,2,1,0:T(8,128)(2,1)S(1)}, u32[]{:S(2)}, u32[]{:S(2)}) async-start(bf16[8,2,16,1024]{3,2,1,0:T(8,128)(2,1)} %select_select_fusion), calls=%async_computation.2 | async-start | bytes 1048576 | tf_op jit(solution)/shard_map/all_to_all | solution.py:211
  81.0 4.9 %collective-permute-start.5 = (bf16[2048,256]{1,0:T(8,128)(2,1)}, bf16[2048,256]{1,0:T(8,128)(2,1)S(1)}, u32[]{:S(2)}, u32[]{:S(2)}) collective-permute-start(bf16[2048,256]{1,0:T(8,128)(2,1)} %bitcast.8), channel_id=1, source_target_pairs={{0,8},{8,0},{1,9},{9,1},{2,10},{10,2},{3,11},{11,3},{4,12},{12,4},... | collective-permute-start | bytes 3145736 | tf_op jit(solution)/shard_map/ppermute | solution.py:66
  90.5 9.8 %all-to-all-start.1 = ((bf16[32,64,256]{2,1,0:T(8,128)(2,1)}), bf16[32,64,256]{2,1,0:T(8,128)(2,1)S(1)}, u32[]{:S(2)}, u32[]{:S(2)}) async-start(bf16[32,64,256]{2,1,0:T(8,128)(2,1)} %broadcast_in_dim.110), calls=%async_computation.1 | async-start | bytes 2097152 | tf_op jit(solution)/shard_map/all_to_all | solution.py:49
  100.2 13.5 %all-gather.3.cloned.1.call-done = bf16[2048,512]{1,0:T(8,128)(2,1)} async-done(((bf16[256,512]{1,0:T(8,128)(2,1)}), bf16[2048,512]{1,0:T(8,128)(2,1)}) %all-gather.3.cloned.1.call-update) | async-done | bytes 2097168 | tf_op jit(solution)/shard_map/all_gather | solution.py:183
  113.7 11.6 %collective-permute-start.3 = (bf16[2048,512]{1,0:T(8,128)(2,1)}, bf16[2048,512]{1,0:T(8,128)(2,1)}, u32[]{:S(2)}, u32[]{:S(2)}) collective-permute-start(bf16[2048,512]{1,0:T(8,128)(2,1)} %all-gather.3.cloned.1.call-done), channel_id=1, source_target_pairs={{0,8},{8,0},{1,9},{9,1},{2,10},{10,2},{3,11},{11,3},{4,12},{12,4},... | collective-permute-start | bytes 6291464 | tf_op jit(solution)/shard_map/ppermute | solution.py:66
  125.4 7.1 %all-to-all-done.1 = bf16[32,64,256]{2,1,0:T(8,128)(2,1)S(1)} async-done(((bf16[32,64,256]{2,1,0:T(8,128)(2,1)}), bf16[32,64,256]{2,1,0:T(8,128)(2,1)S(1)}, u32[]{:S(2)}, u32[]{:S(2)}) %all-to-all-start.1) | async-done | bytes 1048608 | tf_op jit(solution)/shard_map/all_to_all | solution.py:49
  132.4 5.1 %collective-permute-start.6 = (bf16[2048,256]{1,0:T(8,128)(2,1)S(1)}, bf16[2048,256]{1,0:T(8,128)(2,1)S(1)}, u32[]{:S(2)}, u32[]{:S(2)}) collective-permute-start(bf16[2048,256]{1,0:T(8,128)(2,1)S(1)} %bitcast.113), channel_id=1, source_target_pairs={{0,8},{8,0},{1,9},{9,1},{2,10},{10,2},{3,11},{11,3},{4,12},{12,4},... | collective-permute-start | bytes 3145736 | tf_op jit(solution)/shard_map/ppermute | solution.py:66
  142.5 3.4 %collective-permute-start.4 = (bf16[64,512]{1,0:T(8,128)(2,1)S(1)}, bf16[64,512]{1,0:T(8,128)(2,1)S(1)}, u32[]{:S(2)}, u32[]{:S(2)}) collective-permute-start(bf16[64,512]{1,0:T(8,128)(2,1)S(1)} %get-tuple-element.31), channel_id=1, source_target_pairs={{0,1},{1,0},{2,3},{3,2},{4,5},{5,4},{6,7},{7,6},{8,9},{9,8},{10,11... | collective-permute-start | bytes 196616 | tf_op jit(solution)/shard_map/ppermute | solution.py:70
  145.9 20.7 %all-gather.5.cloned.1.call-done = bf16[2048,512]{1,0:T(8,128)(2,1)} async-done(((bf16[256,512]{1,0:T(8,128)(2,1)}), bf16[2048,512]{1,0:T(8,128)(2,1)}) %all-gather.5.cloned.1.call-update) | async-done | bytes 2097168 | tf_op jit(solution)/shard_map/all_gather | solution.py:185
  166.6 6.2 %collective-permute-start.11 = (bf16[2048,512]{1,0:T(8,128)(2,1)}, bf16[2048,512]{1,0:T(8,128)(2,1)}, u32[]{:S(2)}, u32[]{:S(2)}) collective-permute-start(bf16[2048,512]{1,0:T(8,128)(2,1)} %all-gather.5.cloned.1.call-done), channel_id=1, source_target_pairs={{0,8},{8,0},{1,9},{9,1},{2,10},{10,2},{3,11},{11,3},{4,12},{12,4},... | collective-permute-start | bytes 6291464 | tf_op jit(solution)/shard_map/ppermute | solution.py:66
  175.4 5.9 %attend.1 = bf16[512,128]{1,0:T(8,128)(2,1)S(1)} custom-call(bf16[512,128]{1,0:T(8,128)(2,1)S(1)} %reshape.388.q_ref, bf16[2048,256]{1,0:T(8,128)(2,1)S(1)} %bitcast.114, bf16[2048,256]{1,0:T(8,128)(2,1)S(1)} %collective-permute-done.6.far_ref, s32[512,1]{1,0:T(8,128)S(1)} %reshape.406.qpos_ref, s32[1,4096]{1,0:T(1,128)S(1)} %add.172.kpos_ref), custom_call_target="tpu_custom_call" | custom-call | tf_op jit(solution)/shard_map/attend/pallas_call | solution.py:103
  181.3 3.2 %collective-permute-start.10 = (bf16[64,512]{1,0:T(8,128)(2,1)S(1)}, bf16[64,512]{1,0:T(8,128)(2,1)S(1)}, u32[]{:S(2)}, u32[]{:S(2)}) collective-permute-start(bf16[64,512]{1,0:T(8,128)(2,1)S(1)} %squeeze.43), channel_id=1, source_target_pairs={{0,1},{1,0},{2,3},{3,2},{4,5},{5,4},{6,7},{7,6},{8,9},{9,8},{10,11... | collective-permute-start | bytes 196616 | tf_op jit(solution)/shard_map/ppermute | solution.py:70
  192.6 5.3 %all-to-all-start.3 = ((bf16[8,128,512]{1,2,0:T(8,128)(2,1)}), bf16[8,128,512]{1,2,0:T(8,128)(2,1)S(1)}, u32[]{:S(2)}, u32[]{:S(2)}) async-start(bf16[8,128,512]{1,2,0:T(8,128)(2,1)} %pad_maximum_fusion), calls=%async_computation.3 | async-start | bytes 2097152 | tf_op jit(solution)/shard_map/all_to_all | solution.py:253
  199.1 13.6 %all-to-all-done.3 = bf16[8,128,512]{1,2,0:T(8,128)(2,1)S(1)} async-done(((bf16[8,128,512]{1,2,0:T(8,128)(2,1)}), bf16[8,128,512]{1,2,0:T(8,128)(2,1)S(1)}, u32[]{:S(2)}, u32[]{:S(2)}) %all-to-all-start.3) | async-done | bytes 1048608 | tf_op jit(solution)/shard_map/all_to_all | solution.py:253
  (142 shorter events, 33.3 us)
Async XLA Ops:
  7.2 37.6 %copy-start = (bf16[2,1,2,32,4096]{4,3,2,1,0:T(8,128)(2,1)S(1)}, bf16[2,1,2,32,4096]{4,3,2,1,0:T(8,128)(2,1)}, u32[]{:S(2)}) copy-start(bf16[2,1,2,32,4096]{4,3,2,1,0:T(8,128)(2,1)} %param.12) | copy-start | bytes 3145732
  7.2 53.8 %collective-permute-start = (bf16[64,512]{1,0:T(8,128)(2,1)}, bf16[64,512]{1,0:T(8,128)(2,1)S(1)}, u32[]{:S(2)}, u32[]{:S(2)}) collective-permute-start(bf16[64,512]{1,0:T(8,128)(2,1)} %param.14), channel_id=1, source_target_pairs={{16,0},{32,16},{48,32},{0,48},{17,1},{33,17},{49,33},{1,49},{18,2}... | collective-permute-start | bytes 196616 | tf_op jit(solution)/shard_map/ppermute | solution.py:56
  18.8 46.2 %collective-permute-start.1 = (bf16[64,512]{1,0:T(8,128)(2,1)}, bf16[64,512]{1,0:T(8,128)(2,1)S(1)}, u32[]{:S(2)}, u32[]{:S(2)}) collective-permute-start(bf16[64,512]{1,0:T(8,128)(2,1)} %param.14), channel_id=1, source_target_pairs={{32,0},{48,16},{0,32},{16,48},{33,1},{49,17},{1,33},{17,49},{34,2}... | collective-permute-start | bytes 196616 | tf_op jit(solution)/shard_map/ppermute | solution.py:56
  20.7 44.2 %collective-permute-start.2 = (bf16[64,512]{1,0:T(8,128)(2,1)}, bf16[64,512]{1,0:T(8,128)(2,1)S(1)}, u32[]{:S(2)}, u32[]{:S(2)}) collective-permute-start(bf16[64,512]{1,0:T(8,128)(2,1)} %param.14), channel_id=1, source_target_pairs={{48,0},{0,16},{16,32},{32,48},{49,1},{1,17},{17,33},{33,49},{50,2}... | collective-permute-start | bytes 196616 | tf_op jit(solution)/shard_map/ppermute | solution.py:56
  25.0 50.8 %collective-permute-start.7 = (bf16[64,512]{1,0:T(8,128)(2,1)}, bf16[64,512]{1,0:T(8,128)(2,1)S(1)}, u32[]{:S(2)}, u32[]{:S(2)}) collective-permute-start(bf16[64,512]{1,0:T(8,128)(2,1)} %bitcast.125), channel_id=1, source_target_pairs={{16,0},{32,16},{48,32},{0,48},{17,1},{33,17},{49,33},{1,49},{18,2}... | collective-permute-start | bytes 196616 | tf_op jit(solution)/shard_map/ppermute | solution.py:56
  28.1 47.6 %collective-permute-start.8 = (bf16[64,512]{1,0:T(8,128)(2,1)}, bf16[64,512]{1,0:T(8,128)(2,1)S(1)}, u32[]{:S(2)}, u32[]{:S(2)}) collective-permute-start(bf16[64,512]{1,0:T(8,128)(2,1)} %bitcast.126), channel_id=1, source_target_pairs={{32,0},{48,16},{0,32},{16,48},{33,1},{49,17},{1,33},{17,49},{34,2}... | collective-permute-start | bytes 196616 | tf_op jit(solution)/shard_map/ppermute | solution.py:56
  37.3 38.7 %all-to-all-start = ((bf16[32,64,256]{2,1,0:T(8,128)(2,1)}), bf16[32,64,256]{2,1,0:T(8,128)(2,1)}, u32[]{:S(2)}, u32[]{:S(2)}) async-start(bf16[32,64,256]{2,1,0:T(8,128)(2,1)} %broadcast_in_dim.106), calls=%async_computation | async-start | bytes 2097152 | tf_op jit(solution)/shard_map/all_to_all | solution.py:49
  44.7 69.1 %all-gather.3.cloned.1.call-start = ((), (), s32[]{:S(2)}) async-start(), calls=%async_computation.4 | async-start | bytes 2359296 | tf_op jit(solution)/shard_map/all_gather | solution.py:183
  55.0 10.0 %copy-start.4 = (bf16[64,512]{1,0:T(8,128)(2,1)S(1)}, bf16[64,512]{1,0:T(8,128)(2,1)}, u32[]{:S(2)}) copy-start(bf16[64,512]{1,0:T(8,128)(2,1)} %param.14) | copy-start | bytes 196612
  55.1 11.0 %copy-start.11 = (s32[1,1,2]{2,1,0:T(1,128)S(1)}, s32[1,1,2]{2,1,0:T(1,128)}, u32[]{:S(2)}) copy-start(s32[1,1,2]{2,1,0:T(1,128)} %param.21) | copy-start | bytes 28
  61.0 15.0 %collective-permute-start.9 = (bf16[64,512]{1,0:T(8,128)(2,1)S(1)}, bf16[64,512]{1,0:T(8,128)(2,1)S(1)}, u32[]{:S(2)}, u32[]{:S(2)}) collective-permute-start(bf16[64,512]{1,0:T(8,128)(2,1)S(1)} %bitcast.127), channel_id=1, source_target_pairs={{48,0},{0,16},{16,32},{32,48},{49,1},{1,17},{17,33},{33,49},{50,2}... | collective-permute-start | bytes 196616 | tf_op jit(solution)/shard_map/ppermute | solution.py:56
  76.0 13.3 %all-to-all-start.2 = ((bf16[8,2,16,1024]{3,2,1,0:T(8,128)(2,1)}), bf16[8,2,16,1024]{3,2,1,0:T(8,128)(2,1)S(1)}, u32[]{:S(2)}, u32[]{:S(2)}) async-start(bf16[8,2,16,1024]{3,2,1,0:T(8,128)(2,1)} %select_select_fusion), calls=%async_computation.2 | async-start | bytes 1048576 | tf_op jit(solution)/shard_map/all_to_all | solution.py:211
  81.0 85.6 %all-gather.5.cloned.1.call-start = ((), (), s32[]{:S(2)}) async-start(), calls=%async_computation.5 | async-start | bytes 2359296 | tf_op jit(solution)/shard_map/all_gather | solution.py:185
  81.0 7.5 %collective-permute-start.5 = (bf16[2048,256]{1,0:T(8,128)(2,1)}, bf16[2048,256]{1,0:T(8,128)(2,1)S(1)}, u32[]{:S(2)}, u32[]{:S(2)}) collective-permute-start(bf16[2048,256]{1,0:T(8,128)(2,1)} %bitcast.8), channel_id=1, source_target_pairs={{0,8},{8,0},{1,9},{9,1},{2,10},{10,2},{3,11},{11,3},{4,12},{12,4},... | collective-permute-start | bytes 3145736 | tf_op jit(solution)/shard_map/ppermute | solution.py:66
  90.5 42.0 %all-to-all-start.1 = ((bf16[32,64,256]{2,1,0:T(8,128)(2,1)}), bf16[32,64,256]{2,1,0:T(8,128)(2,1)S(1)}, u32[]{:S(2)}, u32[]{:S(2)}) async-start(bf16[32,64,256]{2,1,0:T(8,128)(2,1)} %broadcast_in_dim.110), calls=%async_computation.1 | async-start | bytes 2097152 | tf_op jit(solution)/shard_map/all_to_all | solution.py:49
  113.7 25.9 %collective-permute-start.3 = (bf16[2048,512]{1,0:T(8,128)(2,1)}, bf16[2048,512]{1,0:T(8,128)(2,1)}, u32[]{:S(2)}, u32[]{:S(2)}) collective-permute-start(bf16[2048,512]{1,0:T(8,128)(2,1)} %all-gather.3.cloned.1.call-done), channel_id=1, source_target_pairs={{0,8},{8,0},{1,9},{9,1},{2,10},{10,2},{3,11},{11,3},{4,12},{12,4},... | collective-permute-start | bytes 6291464 | tf_op jit(solution)/shard_map/ppermute | solution.py:66
  132.4 34.1 %collective-permute-start.6 = (bf16[2048,256]{1,0:T(8,128)(2,1)S(1)}, bf16[2048,256]{1,0:T(8,128)(2,1)S(1)}, u32[]{:S(2)}, u32[]{:S(2)}) collective-permute-start(bf16[2048,256]{1,0:T(8,128)(2,1)S(1)} %bitcast.113), channel_id=1, source_target_pairs={{0,8},{8,0},{1,9},{9,1},{2,10},{10,2},{3,11},{11,3},{4,12},{12,4},... | collective-permute-start | bytes 3145736 | tf_op jit(solution)/shard_map/ppermute | solution.py:66
  139.7 33.4 %copy-start.10 = (s32[2]{0:T(128)S(1)}, s32[2]{0:T(128)}, u32[]{:S(2)}) copy-start(s32[2]{0:T(128)} %param.18) | copy-start | bytes 28
  142.5 24.1 %collective-permute-start.4 = (bf16[64,512]{1,0:T(8,128)(2,1)S(1)}, bf16[64,512]{1,0:T(8,128)(2,1)S(1)}, u32[]{:S(2)}, u32[]{:S(2)}) collective-permute-start(bf16[64,512]{1,0:T(8,128)(2,1)S(1)} %get-tuple-element.31), channel_id=1, source_target_pairs={{0,1},{1,0},{2,3},{3,2},{4,5},{5,4},{6,7},{7,6},{8,9},{9,8},{10,11... | collective-permute-start | bytes 196616 | tf_op jit(solution)/shard_map/ppermute | solution.py:70
  166.6 22.7 %collective-permute-start.11 = (bf16[2048,512]{1,0:T(8,128)(2,1)}, bf16[2048,512]{1,0:T(8,128)(2,1)}, u32[]{:S(2)}, u32[]{:S(2)}) collective-permute-start(bf16[2048,512]{1,0:T(8,128)(2,1)} %all-gather.5.cloned.1.call-done), channel_id=1, source_target_pairs={{0,8},{8,0},{1,9},{9,1},{2,10},{10,2},{3,11},{11,3},{4,12},{12,4},... | collective-permute-start | bytes 6291464 | tf_op jit(solution)/shard_map/ppermute | solution.py:66
  181.3 5.6 %collective-permute-start.10 = (bf16[64,512]{1,0:T(8,128)(2,1)S(1)}, bf16[64,512]{1,0:T(8,128)(2,1)S(1)}, u32[]{:S(2)}, u32[]{:S(2)}) collective-permute-start(bf16[64,512]{1,0:T(8,128)(2,1)S(1)} %squeeze.43), channel_id=1, source_target_pairs={{0,1},{1,0},{2,3},{3,2},{4,5},{5,4},{6,7},{7,6},{8,9},{9,8},{10,11... | collective-permute-start | bytes 196616 | tf_op jit(solution)/shard_map/ppermute | solution.py:70
  191.5 6.5 %copy-start.3 = (bf16[1,1,16,16,1024]{4,3,2,1,0:T(8,128)(2,1)S(1)}, bf16[1,1,16,16,1024]{4,3,2,1,0:T(8,128)(2,1)}, u32[]{:S(2)}) copy-start(bf16[1,1,16,16,1024]{4,3,2,1,0:T(8,128)(2,1)} %param.20) | copy-start | bytes 1572868
  191.6 6.6 %copy-start.2 = (bf16[8,2,16,1024]{3,2,1,0:T(8,128)(2,1)S(1)}, bf16[8,2,16,1024]{3,2,1,0:T(8,128)(2,1)}, u32[]{:S(2)}) copy-start(bf16[8,2,16,1024]{3,2,1,0:T(8,128)(2,1)} %copy-done.1) | copy-start | bytes 1572868
  192.6 20.0 %all-to-all-start.3 = ((bf16[8,128,512]{1,2,0:T(8,128)(2,1)}), bf16[8,128,512]{1,2,0:T(8,128)(2,1)S(1)}, u32[]{:S(2)}, u32[]{:S(2)}) async-start(bf16[8,128,512]{1,2,0:T(8,128)(2,1)} %pad_maximum_fusion), calls=%async_computation.3 | async-start | bytes 2097152 | tf_op jit(solution)/shard_map/all_to_all | solution.py:253
  (6 other events, 27.6 us)
Sparse Core Ops, SparseCore 0:
  66.0 47.6 all-gather.2
  115.8 50.6 all-gather.4

commit v2 on v1

--- a/solution.py
+++ b/solution.py
@@ -49,25 +49,47 @@
     return lax.all_to_all(copies, axes, split_axis=0, concat_axis=0, tiled=True)
 
 
-def gather_ring(block, axis):
-    size = lax.axis_size(axis)
-    place = lax.axis_index(axis)
-    parts = [
-        lax.ppermute(block, axis, [((i + hop) % size, i) for i in range(size)])
-        for hop in range(1, size)
-    ]
-    parts = jnp.stack(parts + [block])
-    return lax.dynamic_slice_in_dim(
-        jnp.concatenate([parts, parts]), size - 1 - place, size, 0
-    )
-
-
 def swap_core(value):
     return lax.ppermute(value, "core", [(0, 1), (1, 0)])
 
 
 def swap_x(value):
     return lax.ppermute(value, "x", [(i, i ^ 1) for i in range(lax.axis_size("x"))])
+
+
+def norm_kernel(core_ref, hidden_ref, gain_ref, near_ref, far_ref):
+    hidden = hidden_ref[...].astype(jnp.float32)
+    scale = lax.rsqrt(jnp.mean(hidden * hidden, axis=-1, keepdims=True) + 1e-05)
+    normed = hidden * scale * gain_ref[...].astype(jnp.float32)
+    core = core_ref[0]
+    lane = lax.broadcasted_iota(jnp.int32, (hidden.shape[0], 128), 1)
+    for pair in range(hidden.shape[1] // 256):
+        left = normed[:, 256 * pair : 256 * pair + 128]
+        right = normed[:, 256 * pair + 128 : 256 * pair + 256]
+        even = jnp.where(lane < 64, left, pltpu.roll(right, 64, 1)).astype(jnp.bfloat16)
+        odd = jnp.where(lane < 64, pltpu.roll(left, 64, 1), right).astype(jnp.bfloat16)
+        span = slice(128 * pair, 128 * pair + 128)
+        near_ref[:, span] = jnp.where(core == 0, even, odd)
+        far_ref[:, span] = jnp.where(core == 0, odd, even)
+
+
+def split_norm(hidden, gain, core):
+    rows, width = hidden.shape
+    tile = 32
+    half = jax.ShapeDtypeStruct((rows, width // 2), jnp.bfloat16)
+    half_spec = pl.BlockSpec((tile, width // 2), lambda i: (i, 0))
+    return pl.pallas_call(
+        norm_kernel,
+        grid=(rows // tile,),
+        in_specs=[
+            pl.BlockSpec(memory_space=pltpu.SMEM),
+            pl.BlockSpec((tile, width), lambda i: (i, 0)),
+            pl.BlockSpec((1, width), lambda i: (0, 0)),
+        ],
+        out_specs=(half_spec, half_spec),
+        out_shape=(half, half),
+        name="split_norm",
+    )(core.reshape(1), hidden, gain[None])
 
 
 def attend_kernel(q_ref, near_ref, far_ref, qpos_ref, kpos_ref, out_ref):
@@ -142,8 +164,7 @@
     leave_ids = move_page[0, 0]
     gone = jnp.any(leave_ids[:, None] == jnp.arange(page_count, dtype=jnp.int32)[None, :], axis=0)
     kept = jnp.where(gone[:, None, None], jnp.zeros_like(pages), pages)
-    filled = jnp.sum(arrived.astype(jnp.float32), axis=0).astype(pages.dtype)
-    new_pages = jnp.concatenate([kept[: page_count - moves], filled], axis=0)
+    new_pages = jnp.concatenate([kept[: page_count - moves], arrived[0]], axis=0)
     return new_pages.reshape(cache_pages.shape)
 
 
@@ -176,46 +197,38 @@
 
     key_cols = lax.dynamic_slice_in_dim(key_matrix, kv_first, HEAD_SIZE, 1)
     value_cols = lax.dynamic_slice_in_dim(value_matrix, kv_first, HEAD_SIZE, 1)
-    kv_near = spread(jnp.concatenate([key_cols, value_cols], axis=1), CHIPS)
-    kv_near = kv_near.reshape(-1, 2 * HEAD_SIZE)
-    kv_far = swap_core(kv_near)
-    wq_near = gather_ring(w_query, "zh").reshape(rows_z * piece, -1)
-    wq_near = lax.all_gather(wq_near, "y", axis=0, tiled=True)
-    wo_near = gather_ring(w_out.T, "zh").reshape(rows_z * piece, -1)
-    wo_near = lax.all_gather(wo_near, "y", axis=0, tiled=True)
+    half_near = spread(jnp.where(mine == 0, key_cols, value_cols), CHIPS).reshape(-1, HEAD_SIZE)
+    weights = jnp.stack([w_query, w_out.T])
+    weights = lax.all_gather(weights, "zh", axis=0)
+    weights, leave = lax.optimization_barrier((weights, move_page))
+    weights = lax.all_gather(weights, "y", axis=0)
+    send_pages = pages_to_send(cache_pages, leave, move_dest, move_slot)
+    arrived = lax.psum_scatter(send_pages, REP, scatter_dimension=0, tiled=True)
+    weights, arrived = lax.optimization_barrier((weights, arrived))
+    wq_near = weights[:, :, 0].reshape(rows_y * rows_z * piece, -1)
+    wo_near = weights[:, :, 1].reshape(rows_y * rows_z * piece, -1)
     wq_far = swap_core(wq_near)
 
-    hidden = hidden_in.reshape(2 * span, width).astype(jnp.float32)
-    scale = lax.rsqrt(jnp.mean(hidden * hidden, axis=-1, keepdims=True) + 1e-05)
-    normed = (hidden * scale * norm_gain.astype(jnp.float32)).astype(jnp.bfloat16)
-    normed = normed.reshape(2 * span, rows_y * rows_z, 2, piece)
-    even = normed[:, :, 0].reshape(2 * span, width // 2)
-    odd = normed[:, :, 1].reshape(2 * span, width // 2)
-    x_near = jnp.where(core == 0, even, odd)
-    x_far = jnp.where(core == 0, odd, even)
+    x_near, x_far = split_norm(hidden_in.reshape(2 * span, width), norm_gain, core)
+    half_near, x_near, x_far = lax.optimization_barrier((half_near, x_near, x_far))
+    half_far = swap_core(half_near)
 
     own_pair = lax.dynamic_slice_in_dim(pair_of_device, place, 1, 1)[:, 0]
     blocks = jnp.stack([own_pair, 2 * cycle - 1 - own_pair], axis=1)
     qpos = (blocks[:, :, None] * blk + jnp.arange(blk, dtype=jnp.int32)).reshape(2, span)
     cosine_table, sine_table = rope_tables(qpos.reshape(-1))
 
-    def prompt_rows(table):
-        return lax.dynamic_slice_in_dim(table, mine * span, span, 0)
-
-    kv = matmul(prompt_rows(x_near), kv_near) + matmul(prompt_rows(x_far), kv_far)
-    keys = apply_rotation(
-        kv[:, None, :HEAD_SIZE], prompt_rows(cosine_table), prompt_rows(sine_table)
-    )[:, 0]
-    kv = jnp.concatenate([keys, kv[:, HEAD_SIZE:]], axis=1).astype(jnp.bfloat16)
+    half = matmul(x_near, half_near) + matmul(x_far, half_far)
+    keys = apply_rotation(half[:, None, :], cosine_table, sine_table)[:, 0]
+    half = jnp.where(mine == 0, keys, half).astype(jnp.bfloat16).reshape(2, span, HEAD_SIZE)
+    kept = lax.dynamic_index_in_dim(half, mine, 0, False)
+    other = swap_x(lax.dynamic_index_in_dim(half, 1 - mine, 0, False))
+    kv = jnp.where(
+        mine == 0,
+        jnp.concatenate([kept, other], axis=1),
+        jnp.concatenate([other, kept], axis=1),
+    )
     near = spread(kv, CHIPS).reshape(-1, 2 * HEAD_SIZE)
-    arrived = lax.all_to_all(
-        pages_to_send(cache_pages, move_page, move_dest, move_slot),
-        REP,
-        split_axis=0,
-        concat_axis=0,
-        tiled=True,
-    )
-    near, arrived = lax.optimization_barrier((near, arrived))
     far = swap_core(near)
 
     query = matmul(x_near, wq_near) + matmul(x_far, wq_far)
@@ -226,7 +239,6 @@
     q_mine = lax.dynamic_index_in_dim(query, mine, 0, False)
     q_pair = swap_x(lax.dynamic_index_in_dim(query, 1 - mine, 0, False))
 
-    q_pair, far, wo_near = lax.optimization_barrier((q_pair, far, wo_near))
     wo_far = swap_core(wo_near)
 
     pairs = lax.dynamic_index_in_dim(pair_of_device, mine, 0, False).reshape(-1, 2)

time: 222 us -> 196 us (0.88)
  the two profiles are of different devices: /device:TPU:1 before, /device:TPU:24 now
where the time goes in v2:
time: 196 us; the launch traced here: 195 us
  waiting for transfers between devices  66.7 us (34%)
  starting transfers between devices  43.8 us (22%)
  blocking collectives  22.3 us (11%)
  between operations  16 us (8%)
  local copies, waits for them, and re-layouts  15.2 us (8%)
  matrix products  11.4 us (6%)
  other arithmetic  9.89 us (5%)
  Pallas kernels  9.79 us (5%)
    all_gather x1, waiting for transfers between devices, on_device(): weights = lax.all_gather(weights, 'y', axis=0)  34 us
    all_gather x1, blocking collectives, on_device(): weights = lax.all_gather(weights, 'zh', axis=0)  22.3 us
    all_to_all x2, starting transfers between devices, spread(): return lax.all_to_all(copies, axes, split_axis=0, concat_axis=0, tiled=True)  19.8 us
    all_to_all x1, waiting for transfers between devices, on_device(): terms = lax.all_to_all(send, REP, split_axis=0, concat_axis=0, tiled=True)  12.4 us
    all_to_all x2, waiting for transfers between devices, spread(): return lax.all_to_all(copies, axes, split_axis=0, concat_axis=0, tiled=True)  12.3 us
    ppermute x3, starting transfers between devices, swap_x(): lax.ppermute(value, 'x', [(i, i ^ 1) for i in range(lax.axis_size('x'))])  10.1 us
    ppermute x4, starting transfers between devices, swap_core(): return lax.ppermute(value, 'core', [(0, 1), (1, 0)])  8.31 us
    ppermute x3, waiting for transfers between devices, swap_x(): lax.ppermute(value, 'x', [(i, i ^ 1) for i in range(lax.axis_size('x'))])  7.06 us
  transfers between devices with their start and end apart: 12, of which 7 were waited for; matrix products, arithmetic and copies ran while one was open for 13% of the time, Pallas kernels for 5%

profile of v2, /device:TPU:24, one launch (start us, length us, event | category | flops | bytes accessed | tf_op | source)
XLA Modules:
  0.0 195.1 jit_solution(2338383276800140117)
XLA Ops:
  8.9 22.3 %all-gather = bf16[8,64,512]{2,1,0:T(8,128)(2,1)} all-gather(bf16[2,64,512]{2,1,0:T(8,128)(2,1)S(1)} %pad_maximum_fusion.1), channel_id=2, replica_groups=mesh['y'=8,'zh'=4,'core'=2,'zl'=2,'x'=4] {'zh'}, dimensions={0}, use_global_device_ids=true | all-gather | bytes 655360 | tf_op jit(solution)/shard_map/all_gather | solution.py:202
  39.2 11.4 %all-to-all-start = ((bf16[32,64,128]{2,1,0:T(8,128)(2,1)}), bf16[32,64,128]{2,1,0:T(8,128)(2,1)S(1)}, u32[]{:S(2)}, u32[]{:S(2)}) async-start(bf16[32,64,128]{2,1,0:T(8,128)(2,1)} %broadcast_in_dim.114), calls=%async_computation.1 | async-start | bytes 1048576 | tf_op jit(solution)/shard_map/all_to_all | solution.py:49
  51.3 3.9 %split_norm.1 = (bf16[128,2048]{1,0:T(8,128)(2,1)}, bf16[128,2048]{1,0:T(8,128)(2,1)}) custom-call(s32[1]{0:T(128)} %bitcast.17.core_ref, bf16[128,4096]{1,0:T(8,128)(2,1)} %bitcast.92, bf16[1,4096]{1,0:T(2,128)(2,1)} %broadcast_in_dim.115.gain_ref), custom_call_target="tpu_custom_call" | custom-call | tf_op jit(solution)/shard_map/split_norm/pallas_call | solution.py:81
  55.4 12.3 %all-to-all-done = bf16[32,64,128]{2,1,0:T(8,128)(2,1)S(1)} async-done(((bf16[32,64,128]{2,1,0:T(8,128)(2,1)}), bf16[32,64,128]{2,1,0:T(8,128)(2,1)S(1)}, u32[]{:S(2)}, u32[]{:S(2)}) %all-to-all-start) | async-done | bytes 524320 | tf_op jit(solution)/shard_map/all_to_all | solution.py:49
  73.3 3.4 %collective-permute-start.3 = (bf16[64,128]{1,0:T(8,128)(2,1)S(1)}, bf16[64,128]{1,0:T(8,128)(2,1)S(1)}, u32[]{:S(2)}, u32[]{:S(2)}) collective-permute-start(bf16[64,128]{1,0:T(8,128)(2,1)S(1)} %get-tuple-element.43), channel_id=1, source_target_pairs={{0,1},{1,0},{2,3},{3,2},{4,5},{5,4},{6,7},{7,6},{8,9},{9,8},{10,11... | collective-permute-start | bytes 49160 | tf_op jit(solution)/shard_map/ppermute | solution.py:57
  76.7 2.2 %collective-permute-done.3 = bf16[64,128]{1,0:T(8,128)(2,1)S(1)} collective-permute-done((bf16[64,128]{1,0:T(8,128)(2,1)S(1)}, bf16[64,128]{1,0:T(8,128)(2,1)S(1)}, u32[]{:S(2)}, u32[]{:S(2)}) %collective-permute-start.3) | collective-permute-done | bytes 16416 | tf_op jit(solution)/shard_map/ppermute | solution.py:57
  80.1 8.4 %all-to-all-start.1 = ((bf16[32,64,256]{2,1,0:T(8,128)(2,1)}), bf16[32,64,256]{2,1,0:T(8,128)(2,1)S(1)}, u32[]{:S(2)}, u32[]{:S(2)}) async-start(bf16[32,64,256]{2,1,0:T(8,128)(2,1)} %broadcast_in_dim.117), calls=%async_computation.2 | async-start | bytes 2097152 | tf_op jit(solution)/shard_map/all_to_all | solution.py:49
  88.5 34.0 %all-gather.4.cloned.1.call-done = bf16[32,2,64,512]{3,2,1,0:T(8,128)(2,1)} async-done(((bf16[4,2,64,512]{3,2,1,0:T(8,128)(2,1)}), bf16[32,2,64,512]{3,2,1,0:T(8,128)(2,1)}) %all-gather.4.cloned.1.call-update) | async-done | bytes 4194320 | tf_op jit(solution)/shard_map/all_gather | solution.py:204
  122.5 3.2 %slice.54 = bf16[8,4,1,64,512]{4,3,2,1,0:T(8,128)(2,1)} slice(bf16[8,4,2,64,512]{4,3,2,1,0:T(8,128)(2,1)} %bitcast.87), slice={[0:8], [0:4], [0:1], [0:64], [0:512]} | slice | bytes 4194304 | tf_op jit(solution)/shard_map/slice | solution.py:208
  125.7 2.0 %collective-permute-start = (bf16[2048,512]{1,0:T(8,128)(2,1)}, bf16[2048,512]{1,0:T(8,128)(2,1)}, u32[]{:S(2)}, u32[]{:S(2)}) collective-permute-start(bf16[2048,512]{1,0:T(8,128)(2,1)} %bitcast.19), channel_id=1, source_target_pairs={{0,8},{8,0},{1,9},{9,1},{2,10},{10,2},{3,11},{11,3},{4,12},{12,4},... | collective-permute-start | bytes 6291464 | tf_op jit(solution)/shard_map/ppermute | solution.py:53
  129.6 2.4 %collective-permute-start.4 = (bf16[2048,256]{1,0:T(8,128)(2,1)S(1)}, bf16[2048,256]{1,0:T(8,128)(2,1)S(1)}, u32[]{:S(2)}, u32[]{:S(2)}) collective-permute-start(bf16[2048,256]{1,0:T(8,128)(2,1)S(1)} %bitcast.85), channel_id=1, source_target_pairs={{0,8},{8,0},{1,9},{9,1},{2,10},{10,2},{3,11},{11,3},{4,12},{12,4},... | collective-permute-start | bytes 3145736 | tf_op jit(solution)/shard_map/ppermute | solution.py:53
  132.0 2.7 %copy.42 = bf16[8,4,2,64,512]{4,3,1,0,2:T(8,128)(2,1)S(1)} copy(bf16[8,4,2,64,512]{4,3,2,1,0:T(8,128)(2,1)} %bitcast.88) | data formatting | bytes 8388608 | tf_op jit(solution)/shard_map/optimization_barrier | solution.py:207
  136.3 2.1 %collective-permute-start.6 = (bf16[2048,512]{1,0:T(8,128)(2,1)}, bf16[2048,512]{1,0:T(8,128)(2,1)}, u32[]{:S(2)}, u32[]{:S(2)}) collective-permute-start(bf16[2048,512]{1,0:T(8,128)(2,1)} %bitcast.33), channel_id=1, source_target_pairs={{0,8},{8,0},{1,9},{9,1},{2,10},{10,2},{3,11},{11,3},{4,12},{12,4},... | collective-permute-start | bytes 6291464 | tf_op jit(solution)/shard_map/ppermute | solution.py:53
  138.4 2.0 %fusion.16 = f32[128,512]{1,0:T(8,128)S(1)} fusion(bf16[128,2048]{1,0:T(8,128)(2,1)S(1)} %copy-done.1, bf16[2048,512]{1,0:T(8,128)(2,1)} %bitcast.19), kind=kOutput, calls=%fused_computation.74 | convolution fusion | flops 268435456 | bytes 2883584 | tf_op jit(solution)/shard_map/dot_general | solution.py:43
  140.4 2.0 %convolution_add_fusion = f32[128,512]{1,0:T(8,128)S(1)} fusion(f32[128,512]{1,0:T(8,128)S(1)} %fusion.16, bf16[128,2048]{1,0:T(8,128)(2,1)S(1)} %copy-done, bf16[2048,512]{1,0:T(8,128)(2,1)} %collective-permute-done), kind=kOutput, calls=%fused_computation.5 | convolution fusion | flops 268500992 | bytes 3145728 | tf_op jit(solution)/shard_map/dot_general | solution.py:43
  143.2 3.3 %collective-permute-start.1 = (bf16[64,512]{1,0:T(8,128)(2,1)S(1)}, bf16[64,512]{1,0:T(8,128)(2,1)S(1)}, u32[]{:S(2)}, u32[]{:S(2)}) collective-permute-start(bf16[64,512]{1,0:T(8,128)(2,1)S(1)} %get-tuple-element.37), channel_id=1, source_target_pairs={{0,1},{1,0},{2,3},{3,2},{4,5},{5,4},{6,7},{7,6},{8,9},{9,8},{10,11... | collective-permute-start | bytes 196616 | tf_op jit(solution)/shard_map/ppermute | solution.py:57
  147.4 2.1 %collective-permute-done.1 = bf16[64,512]{1,0:T(8,128)(2,1)S(1)} collective-permute-done((bf16[64,512]{1,0:T(8,128)(2,1)S(1)}, bf16[64,512]{1,0:T(8,128)(2,1)S(1)}, u32[]{:S(2)}, u32[]{:S(2)}) %collective-permute-start.1) | collective-permute-done | bytes 65568 | tf_op jit(solution)/shard_map/ppermute | solution.py:57
  149.6 5.9 %attend.1 = bf16[512,128]{1,0:T(8,128)(2,1)S(1)} custom-call(bf16[512,128]{1,0:T(8,128)(2,1)S(1)} %reshape.404.q_ref, bf16[2048,256]{1,0:T(8,128)(2,1)S(1)} %bitcast.86, bf16[2048,256]{1,0:T(8,128)(2,1)S(1)} %collective-permute-done.4.far_ref, s32[512,1]{1,0:T(8,128)S(1)} %reshape.424.qpos_ref, s32[1,4096]{1,0:T(1,128)S(1)} %add.150.kpos_ref), custom_call_target="tpu_custom_call" | custom-call | tf_op jit(solution)/shard_map/attend/pallas_call | solution.py:125
  155.6 3.4 %collective-permute-start.5 = (bf16[64,512]{1,0:T(8,128)(2,1)S(1)}, bf16[64,512]{1,0:T(8,128)(2,1)S(1)}, u32[]{:S(2)}, u32[]{:S(2)}) collective-permute-start(bf16[64,512]{1,0:T(8,128)(2,1)S(1)} %squeeze.55), channel_id=1, source_target_pairs={{0,1},{1,0},{2,3},{3,2},{4,5},{5,4},{6,7},{7,6},{8,9},{9,8},{10,11... | collective-permute-start | bytes 196616 | tf_op jit(solution)/shard_map/ppermute | solution.py:57
  159.0 2.7 %collective-permute-done.5 = bf16[64,512]{1,0:T(8,128)(2,1)S(1)} collective-permute-done((bf16[64,512]{1,0:T(8,128)(2,1)S(1)}, bf16[64,512]{1,0:T(8,128)(2,1)S(1)}, u32[]{:S(2)}, u32[]{:S(2)}) %collective-permute-start.5) | collective-permute-done | bytes 65568 | tf_op jit(solution)/shard_map/ppermute | solution.py:57
  161.7 2.3 %fusion = bf16[8,128,256]{1,2,0:T(8,128)(2,1)S(1)} fusion(bf16[8,256,512]{2,1,0:T(8,128)(2,1)} %bitcast.15, bf16[64,512]{1,0:T(8,128)(2,1)S(1)} %get-tuple-element.33, bf16[64,512]{1,0:T(8,128)(2,1)S(1)} %get-tuple-element.32), kind=kOutput, calls=%fused_computation.3 | convolution fusion | flops 268959744 | bytes 2752512 | tf_op jit(solution)/shard_map/td,gnd->gtn/dot_general | solution.py:262
  164.0 2.3 %fusion.1 = bf16[8,128,256]{1,2,0:T(8,128)(2,1)S(1)} fusion(bf16[8,256,512]{2,1,0:T(8,128)(2,1)} %bitcast.34, bf16[64,512]{1,0:T(8,128)(2,1)S(1)} %get-tuple-element.33, bf16[64,512]{1,0:T(8,128)(2,1)S(1)} %get-tuple-element.32), kind=kOutput, calls=%fused_computation.4 | convolution fusion | flops 268959744 | bytes 2752512 | tf_op jit(solution)/shard_map/td,gnd->gtn/dot_general | solution.py:262
  167.5 5.5 %all-to-all-start.2 = ((bf16[8,128,512]{1,2,0:T(8,128)(2,1)}), bf16[8,128,512]{1,2,0:T(8,128)(2,1)S(1)}, u32[]{:S(2)}, u32[]{:S(2)}) async-start(bf16[8,128,512]{1,2,0:T(8,128)(2,1)} %pad_maximum_fusion), calls=%async_computation.3 | async-start | bytes 2097152 | tf_op jit(solution)/shard_map/all_to_all | solution.py:265
  174.0 12.4 %all-to-all-done.2 = bf16[8,128,512]{1,2,0:T(8,128)(2,1)S(1)} async-done(((bf16[8,128,512]{1,2,0:T(8,128)(2,1)}), bf16[8,128,512]{1,2,0:T(8,128)(2,1)S(1)}, u32[]{:S(2)}, u32[]{:S(2)}) %all-to-all-start.2) | async-done | bytes 1048608 | tf_op jit(solution)/shard_map/all_to_all | solution.py:265
  (100 shorter events, 24.9 us)
Async XLA Ops:
  8.0 80.5 %reduce-scatter.2.cloned.1.call-start = ((), (), s32[]{:S(2)}) async-start(), calls=%async_computation.4 | async-start | bytes 589824 | tf_op jit(solution)/shard_map/reduce_scatter | solution.py:206
  8.9 41.7 %copy-start.4 = (bf16[4096]{0:T(1024)(128)(2,1)S(1)}, bf16[4096]{0:T(1024)(128)(2,1)}, u32[]{:S(2)}) copy-start(bf16[4096]{0:T(1024)(128)(2,1)} %param.13) | copy-start | bytes 24580
  36.9 18.3 %copy-start.5 = (s32[2,64]{1,0:T(2,128)S(1)}, s32[2,64]{1,0:T(2,128)}, u32[]{:S(2)}) copy-start(s32[2,64]{1,0:T(2,128)} %param.19) | copy-start | bytes 1540
  37.0 85.6 %all-gather.4.cloned.1.call-start = ((), (), s32[]{:S(2)}) async-start(), calls=%async_computation.5 | async-start | bytes 4718592 | tf_op jit(solution)/shard_map/all_gather | solution.py:204
  39.2 28.5 %all-to-all-start = ((bf16[32,64,128]{2,1,0:T(8,128)(2,1)}), bf16[32,64,128]{2,1,0:T(8,128)(2,1)S(1)}, u32[]{:S(2)}, u32[]{:S(2)}) async-start(bf16[32,64,128]{2,1,0:T(8,128)(2,1)} %broadcast_in_dim.114), calls=%async_computation.1 | async-start | bytes 1048576 | tf_op jit(solution)/shard_map/all_to_all | solution.py:49
  67.7 3.8 %collective-permute-start.2 = (bf16[2048,128]{1,0:T(8,128)(2,1)S(1)}, bf16[2048,128]{1,0:T(8,128)(2,1)S(1)}, u32[]{:S(2)}, u32[]{:S(2)}) collective-permute-start(bf16[2048,128]{1,0:T(8,128)(2,1)S(1)} %bitcast.90), channel_id=1, source_target_pairs={{0,8},{8,0},{1,9},{9,1},{2,10},{10,2},{3,11},{11,3},{4,12},{12,4},... | collective-permute-start | bytes 1572872 | tf_op jit(solution)/shard_map/ppermute | solution.py:53
  73.3 5.6 %collective-permute-start.3 = (bf16[64,128]{1,0:T(8,128)(2,1)S(1)}, bf16[64,128]{1,0:T(8,128)(2,1)S(1)}, u32[]{:S(2)}, u32[]{:S(2)}) collective-permute-start(bf16[64,128]{1,0:T(8,128)(2,1)S(1)} %get-tuple-element.43), channel_id=1, source_target_pairs={{0,1},{1,0},{2,3},{3,2},{4,5},{5,4},{6,7},{7,6},{8,9},{9,8},{10,11... | collective-permute-start | bytes 49160 | tf_op jit(solution)/shard_map/ppermute | solution.py:57
  80.1 49.5 %all-to-all-start.1 = ((bf16[32,64,256]{2,1,0:T(8,128)(2,1)}), bf16[32,64,256]{2,1,0:T(8,128)(2,1)S(1)}, u32[]{:S(2)}, u32[]{:S(2)}) async-start(bf16[32,64,256]{2,1,0:T(8,128)(2,1)} %broadcast_in_dim.117), calls=%async_computation.2 | async-start | bytes 2097152 | tf_op jit(solution)/shard_map/all_to_all | solution.py:49
  122.5 6.0 %copy-start.6 = (s32[2]{0:T(128)S(1)}, s32[2]{0:T(128)}, u32[]{:S(2)}) copy-start(s32[2]{0:T(128)} %param.18) | copy-start | bytes 28
  125.7 14.7 %collective-permute-start = (bf16[2048,512]{1,0:T(8,128)(2,1)}, bf16[2048,512]{1,0:T(8,128)(2,1)}, u32[]{:S(2)}, u32[]{:S(2)}) collective-permute-start(bf16[2048,512]{1,0:T(8,128)(2,1)} %bitcast.19), channel_id=1, source_target_pairs={{0,8},{8,0},{1,9},{9,1},{2,10},{10,2},{3,11},{11,3},{4,12},{12,4},... | collective-permute-start | bytes 6291464 | tf_op jit(solution)/shard_map/ppermute | solution.py:53
  129.6 20.0 %collective-permute-start.4 = (bf16[2048,256]{1,0:T(8,128)(2,1)S(1)}, bf16[2048,256]{1,0:T(8,128)(2,1)S(1)}, u32[]{:S(2)}, u32[]{:S(2)}) collective-permute-start(bf16[2048,256]{1,0:T(8,128)(2,1)S(1)} %bitcast.85), channel_id=1, source_target_pairs={{0,8},{8,0},{1,9},{9,1},{2,10},{10,2},{3,11},{11,3},{4,12},{12,4},... | collective-permute-start | bytes 3145736 | tf_op jit(solution)/shard_map/ppermute | solution.py:53
  134.7 3.7 %copy-start.1 = (bf16[128,2048]{1,0:T(8,128)(2,1)S(1)}, bf16[128,2048]{1,0:T(8,128)(2,1)}, u32[]{:S(2)}) copy-start(bf16[128,2048]{1,0:T(8,128)(2,1)} %get-tuple-element.16) | copy-start | bytes 1572868
  136.3 4.2 %copy-start = (bf16[128,2048]{1,0:T(8,128)(2,1)S(1)}, bf16[128,2048]{1,0:T(8,128)(2,1)}, u32[]{:S(2)}) copy-start(bf16[128,2048]{1,0:T(8,128)(2,1)} %get-tuple-element.17) | copy-start | bytes 1572868
  136.3 27.8 %collective-permute-start.6 = (bf16[2048,512]{1,0:T(8,128)(2,1)}, bf16[2048,512]{1,0:T(8,128)(2,1)}, u32[]{:S(2)}, u32[]{:S(2)}) collective-permute-start(bf16[2048,512]{1,0:T(8,128)(2,1)} %bitcast.33), channel_id=1, source_target_pairs={{0,8},{8,0},{1,9},{9,1},{2,10},{10,2},{3,11},{11,3},{4,12},{12,4},... | collective-permute-start | bytes 6291464 | tf_op jit(solution)/shard_map/ppermute | solution.py:53
  143.2 6.3 %collective-permute-start.1 = (bf16[64,512]{1,0:T(8,128)(2,1)S(1)}, bf16[64,512]{1,0:T(8,128)(2,1)S(1)}, u32[]{:S(2)}, u32[]{:S(2)}) collective-permute-start(bf16[64,512]{1,0:T(8,128)(2,1)S(1)} %get-tuple-element.37), channel_id=1, source_target_pairs={{0,1},{1,0},{2,3},{3,2},{4,5},{5,4},{6,7},{7,6},{8,9},{9,8},{10,11... | collective-permute-start | bytes 196616 | tf_op jit(solution)/shard_map/ppermute | solution.py:57
  155.6 6.2 %collective-permute-start.5 = (bf16[64,512]{1,0:T(8,128)(2,1)S(1)}, bf16[64,512]{1,0:T(8,128)(2,1)S(1)}, u32[]{:S(2)}, u32[]{:S(2)}) collective-permute-start(bf16[64,512]{1,0:T(8,128)(2,1)S(1)} %squeeze.55), channel_id=1, source_target_pairs={{0,1},{1,0},{2,3},{3,2},{4,5},{5,4},{6,7},{7,6},{8,9},{9,8},{10,11... | collective-permute-start | bytes 196616 | tf_op jit(solution)/shard_map/ppermute | solution.py:57
  166.4 6.6 %copy-start.7 = (s32[1,1,2]{2,1,0:T(1,128)S(1)}, s32[1,1,2]{2,1,0:T(1,128)}, u32[]{:S(2)}) copy-start(s32[1,1,2]{2,1,0:T(1,128)} %param.21) | copy-start | bytes 28
  166.4 6.7 %copy-start.2 = (bf16[1,1,16,16,1024]{4,3,2,1,0:T(8,128)(2,1)S(1)}, bf16[1,1,16,16,1024]{4,3,2,1,0:T(8,128)(2,1)}, u32[]{:S(2)}) copy-start(bf16[1,1,16,16,1024]{4,3,2,1,0:T(8,128)(2,1)} %param.20) | copy-start | bytes 1572868
  166.4 6.8 %copy-start.3 = (bf16[1,2,16,1024]{3,2,1,0:T(8,128)(2,1)S(1)}, bf16[1,2,16,1024]{3,2,1,0:T(8,128)(2,1)}, u32[]{:S(2)}) copy-start(bf16[1,2,16,1024]{3,2,1,0:T(8,128)(2,1)} %reduce-scatter.2.cloned.1.call-done) | copy-start | bytes 196612
  167.5 18.9 %all-to-all-start.2 = ((bf16[8,128,512]{1,2,0:T(8,128)(2,1)}), bf16[8,128,512]{1,2,0:T(8,128)(2,1)S(1)}, u32[]{:S(2)}, u32[]{:S(2)}) async-start(bf16[8,128,512]{1,2,0:T(8,128)(2,1)} %pad_maximum_fusion), calls=%async_computation.3 | async-start | bytes 2097152 | tf_op jit(solution)/shard_map/all_to_all | solution.py:265
Sparse Core Ops, SparseCore 0:
  37.1 48.7 reduce-scatter.1
Sparse Core Ops, SparseCore 1:
  39.5 83.0 all-gather.3

commit v3 on v2

--- a/solution.py
+++ b/solution.py
@@ -139,22 +139,31 @@
     )(queries, near, far, qpos, kpos)
 
 
+def pages_kernel(page_ref, dest_ref, slot_ref, cache_ref, send_ref):
+    groups, moves = send_ref.shape[:2]
+    free = cache_ref.shape[0] - moves
+    leaving = [cache_ref[page_ref[move]] for move in range(moves)]
+    for group in range(groups):
+        for slot in range(moves):
+            page = jnp.zeros_like(leaving[0])
+            for move in range(moves):
+                here = (dest_ref[move] == group) & (slot_ref[move] == free + slot)
+                page = jnp.where(here, leaving[move], page)
+            send_ref[group, slot] = page
+
+
 def pages_to_send(cache_pages, move_page, move_dest, move_slot):
     pages = cache_pages[0, 0]
-    page_count = pages.shape[0]
-    moves = move_page.shape[2]
-    groups = lax.axis_size(REP)
-    leave_ids = move_page[0, 0]
-    dest_ids = move_dest[0, 0]
-    slot_ids = move_slot[0, 0] - (page_count - moves)
-    slots = jnp.arange(moves, dtype=jnp.int32)
-    leaving = jnp.take(pages, leave_ids, axis=0)
-    to_dest = dest_ids[None, :] == jnp.arange(groups, dtype=jnp.int32)[:, None]
-    chosen = to_dest[:, None, :] & (slot_ids[None, :] == slots[:, None])[None]
-    send = jnp.zeros((groups, moves) + pages.shape[1:], pages.dtype)
-    for move in range(moves):
-        send = jnp.where(chosen[:, :, move, None, None], leaving[move][None, None], send)
-    return send
+    shape = (lax.axis_size(REP), move_page.shape[2]) + pages.shape[1:]
+    scalars = pl.BlockSpec(memory_space=pltpu.SMEM)
+    vector = pl.BlockSpec(memory_space=pltpu.VMEM)
+    return pl.pallas_call(
+        pages_kernel,
+        in_specs=[scalars, scalars, scalars, vector],
+        out_specs=vector,
+        out_shape=jax.ShapeDtypeStruct(shape, pages.dtype),
+        name="pages_to_send",
+    )(move_page[0, 0], move_dest[0, 0], move_slot[0, 0], pages)
 
 
 def settle_pages(cache_pages, move_page, arrived):
@@ -198,20 +207,21 @@
     key_cols = lax.dynamic_slice_in_dim(key_matrix, kv_first, HEAD_SIZE, 1)
     value_cols = lax.dynamic_slice_in_dim(value_matrix, kv_first, HEAD_SIZE, 1)
     half_near = spread(jnp.where(mine == 0, key_cols, value_cols), CHIPS).reshape(-1, HEAD_SIZE)
-    weights = jnp.stack([w_query, w_out.T])
-    weights = lax.all_gather(weights, "zh", axis=0)
+    weights = lax.all_gather(jnp.stack([w_query, w_out.T]), "zh", axis=0)
     weights, leave = lax.optimization_barrier((weights, move_page))
-    weights = lax.all_gather(weights, "y", axis=0)
+    wq_near = weights[:, 0].reshape(rows_z * piece, -1)
+    wo_near = weights[:, 1].reshape(rows_z * piece, -1)
+    wq_near = lax.all_gather(wq_near, "y", axis=0, tiled=True)
+
+    x_near, x_far = split_norm(hidden_in.reshape(2 * span, width), norm_gain, core)
     send_pages = pages_to_send(cache_pages, leave, move_dest, move_slot)
     arrived = lax.psum_scatter(send_pages, REP, scatter_dimension=0, tiled=True)
-    weights, arrived = lax.optimization_barrier((weights, arrived))
-    wq_near = weights[:, :, 0].reshape(rows_y * rows_z * piece, -1)
-    wo_near = weights[:, :, 1].reshape(rows_y * rows_z * piece, -1)
-    wq_far = swap_core(wq_near)
-
-    x_near, x_far = split_norm(hidden_in.reshape(2 * span, width), norm_gain, core)
-    half_near, x_near, x_far = lax.optimization_barrier((half_near, x_near, x_far))
+    half_near, x_near, x_far, wo_near = lax.optimization_barrier(
+        (half_near, x_near, x_far, wo_near)
+    )
+    wo_near = lax.all_gather(wo_near, "y", axis=0, tiled=True)
     half_far = swap_core(half_near)
+    x_chip = jnp.concatenate([x_near, swap_core(x_far)], axis=0)
 
     own_pair = lax.dynamic_slice_in_dim(pair_of_device, place, 1, 1)[:, 0]
     blocks = jnp.stack([own_pair, 2 * cycle - 1 - own_pair], axis=1)
@@ -228,18 +238,17 @@
         jnp.concatenate([kept, other], axis=1),
         jnp.concatenate([other, kept], axis=1),
     )
+    kv, x_chip = lax.optimization_barrier((kv, x_chip))
     near = spread(kv, CHIPS).reshape(-1, 2 * HEAD_SIZE)
-    far = swap_core(near)
-
-    query = matmul(x_near, wq_near) + matmul(x_far, wq_far)
+    wq_near, arrived = lax.optimization_barrier((wq_near, arrived))
+    query = matmul(x_chip, wq_near)
+    query = query[: 2 * span] + swap_core(query[2 * span :])
     query = apply_rotation(
         query.reshape(2 * span, heads_here, HEAD_SIZE), cosine_table, sine_table
     ).astype(jnp.bfloat16)
     query = query.reshape(2, span, heads_here * HEAD_SIZE)
     q_mine = lax.dynamic_index_in_dim(query, mine, 0, False)
     q_pair = swap_x(lax.dynamic_index_in_dim(query, 1 - mine, 0, False))
-
-    wo_far = swap_core(wo_near)
 
     pairs = lax.dynamic_index_in_dim(pair_of_device, mine, 0, False).reshape(-1, 2)
     pairs = jnp.where(core == 0, pairs, pairs[:, ::-1]).T.reshape(-1)
@@ -249,10 +258,14 @@
     my_len = lax.dynamic_index_in_dim(prompt_len, mine, 0, False)
     my_qpos = jnp.where(my_qpos < my_len, my_qpos, -1)
     all_q = jnp.stack([q_mine, q_pair]).reshape(-1, HEAD_SIZE)
+    near, all_q = lax.optimization_barrier((near, all_q))
+    far = swap_core(near)
     all_qpos = jnp.broadcast_to(my_qpos[None, :, None], (2, span, heads_here)).reshape(-1, 1)
     context = attend(all_q, near, far, all_qpos, kpos).reshape(2, span, heads_here * HEAD_SIZE)
+    c_pair = swap_x(context[1])
+    wo_near, c_pair = lax.optimization_barrier((wo_near, c_pair))
     c_mine = context[0]
-    c_pair = swap_x(context[1])
+    wo_far = swap_core(wo_near)
     context = jnp.concatenate(
         [jnp.where(mine == 0, c_mine, c_pair), jnp.where(mine == 0, c_pair, c_mine)], axis=0
     )

time: 196 us -> 178 us (0.908)
  the two profiles are of different devices: /device:TPU:24 before, /device:TPU:1 now
where the time goes in v3:
time: 178 us; the launch traced here: 177 us
  starting transfers between devices  59.3 us (33%)
  waiting for transfers between devices  47.5 us (27%)
  blocking collectives  21.3 us (12%)
  between operations  16 us (9%)
  Pallas kernels  12 us (7%)
  matrix products  8.09 us (5%)
  local copies, waits for them, and re-layouts  6.78 us (4%)
  other arithmetic  6.14 us (3%)
    ppermute x5, starting transfers between devices, swap_core(): return lax.ppermute(value, 'core', [(0, 1), (1, 0)])  26.3 us
    all_to_all x2, waiting for transfers between devices, spread(): return lax.all_to_all(copies, axes, split_axis=0, concat_axis=0, tiled=True)  25.1 us
    all_gather x1, blocking collectives, on_device(): weights = lax.all_gather(jnp.stack([w_query, w_out.T]), 'zh', axis=0)  21.3 us
    all_to_all x2, starting transfers between devices, spread(): return lax.all_to_all(copies, axes, split_axis=0, concat_axis=0, tiled=True)  16 us
    all_to_all x1, waiting for transfers between devices, on_device(): terms = lax.all_to_all(send, REP, split_axis=0, concat_axis=0, tiled=True)  13.9 us
    ppermute x3, starting transfers between devices, swap_x(): lax.ppermute(value, 'x', [(i, i ^ 1) for i in range(lax.axis_size('x'))])  9.28 us
    all_to_all x1, starting transfers between devices, on_device(): terms = lax.all_to_all(send, REP, split_axis=0, concat_axis=0, tiled=True)  7.59 us
    pallas_call x1, Pallas kernels, attend(): pl.pallas_call(attend_kernel, grid=(rows // tile,), in_specs=[pl.BlockSpe...  6.15 us
  transfers between devices with their start and end apart: 14, of which 8 were waited for; matrix products, arithmetic and copies ran while one was open for 10% of the time, Pallas kernels for 6%

profile of v3, /device:TPU:1, one launch (start us, length us, event | category | flops | bytes accessed | tf_op | source)
XLA Modules:
  0.0 177.1 jit_solution(10135595697017888827)
XLA Ops:
  8.9 21.3 %all-gather = bf16[8,64,512]{2,1,0:T(8,128)(2,1)S(1)} all-gather(bf16[2,64,512]{2,1,0:T(8,128)(2,1)S(1)} %pad_maximum_fusion.2), channel_id=2, replica_groups=mesh['y'=8,'zh'=4,'core'=2,'zl'=2,'x'=4] {'zh'}, dimensions={0}, use_global_device_ids=true | all-gather | bytes 655360 | tf_op jit(solution)/shard_map/all_gather | solution.py:210
  30.3 1.9 %pages_to_send.1 = bf16[8,2,16,1024]{3,2,1,0:T(8,128)(2,1)} custom-call(s32[2]{0:T(128)} %bitcast.90, s32[2]{0:T(128)} %bitcast.88, s32[2]{0:T(128)} %bitcast.89, bf16[16,16,1024]{2,1,0:T(8,128)(2,1)} %bitcast.75), custom_call_target="tpu_custom_call" | custom-call | tf_op jit(solution)/shard_map/pages_to_send/pallas_call | solution.py:160
  34.8 9.3 %all-to-all-start = ((bf16[32,64,128]{2,1,0:T(8,128)(2,1)}), bf16[32,64,128]{2,1,0:T(8,128)(2,1)S(1)}, u32[]{:S(2)}, u32[]{:S(2)}) async-start(bf16[32,64,128]{2,1,0:T(8,128)(2,1)} %broadcast_in_dim.20), calls=%async_computation | async-start | bytes 1048576 | tf_op jit(solution)/shard_map/all_to_all | solution.py:49
  44.8 3.9 %split_norm.1 = (bf16[128,2048]{1,0:T(8,128)(2,1)}, bf16[128,2048]{1,0:T(8,128)(2,1)}) custom-call(s32[1]{0:T(128)} %bitcast.1.core_ref, bf16[128,4096]{1,0:T(8,128)(2,1)} %bitcast.77, bf16[1,4096]{1,0:T(2,128)(2,1)} %broadcast_in_dim.21.gain_ref), custom_call_target="tpu_custom_call" | custom-call | tf_op jit(solution)/shard_map/split_norm/pallas_call | solution.py:81
  48.9 9.4 %all-to-all-done = bf16[32,64,128]{2,1,0:T(8,128)(2,1)S(1)} async-done(((bf16[32,64,128]{2,1,0:T(8,128)(2,1)}), bf16[32,64,128]{2,1,0:T(8,128)(2,1)S(1)}, u32[]{:S(2)}, u32[]{:S(2)}) %all-to-all-start) | async-done | bytes 524320 | tf_op jit(solution)/shard_map/all_to_all | solution.py:49
  58.2 10.2 %collective-permute-start = (bf16[2048,128]{1,0:T(8,128)(2,1)S(1)}, bf16[2048,128]{1,0:T(8,128)(2,1)S(1)}, u32[]{:S(2)}, u32[]{:S(2)}) collective-permute-start(bf16[2048,128]{1,0:T(8,128)(2,1)S(1)} %bitcast.73), channel_id=1, source_target_pairs={{0,8},{8,0},{1,9},{9,1},{2,10},{10,2},{3,11},{11,3},{4,12},{12,4},... | collective-permute-start | bytes 1572872 | tf_op jit(solution)/shard_map/ppermute | solution.py:53
  68.6 1.9 %collective-permute-start.2 = (bf16[128,2048]{1,0:T(8,128)(2,1)}, bf16[128,2048]{1,0:T(8,128)(2,1)S(1)}, u32[]{:S(2)}, u32[]{:S(2)}) collective-permute-start(bf16[128,2048]{1,0:T(8,128)(2,1)} %get-tuple-element.24), channel_id=1, source_target_pairs={{0,8},{8,0},{1,9},{9,1},{2,10},{10,2},{3,11},{11,3},{4,12},{12,4},... | collective-permute-start | bytes 1572872 | tf_op jit(solution)/shard_map/ppermute | solution.py:53
  73.7 3.2 %collective-permute-start.1 = (bf16[64,128]{1,0:T(8,128)(2,1)S(1)}, bf16[64,128]{1,0:T(8,128)(2,1)S(1)}, u32[]{:S(2)}, u32[]{:S(2)}) collective-permute-start(bf16[64,128]{1,0:T(8,128)(2,1)S(1)} %get-tuple-element.57), channel_id=1, source_target_pairs={{0,1},{1,0},{2,3},{3,2},{4,5},{5,4},{6,7},{7,6},{8,9},{9,8},{10,11... | collective-permute-start | bytes 49160 | tf_op jit(solution)/shard_map/ppermute | solution.py:57
  77.0 1.6 collective-permute-done.1
  79.8 6.7 %all-to-all-start.1 = ((bf16[32,64,256]{2,1,0:T(8,128)(2,1)}), bf16[32,64,256]{2,1,0:T(8,128)(2,1)S(1)}, u32[]{:S(2)}, u32[]{:S(2)}) async-start(bf16[32,64,256]{2,1,0:T(8,128)(2,1)} %broadcast_in_dim.24), calls=%async_computation.1 | async-start | bytes 2097152 | tf_op jit(solution)/shard_map/all_to_all | solution.py:49
  86.5 2.3 %fusion.17 = f32[256,512]{1,0:T(8,128)S(1)} fusion(bf16[256,2048]{1,0:T(8,128)(2,1)S(1)} %pad_maximum_fusion, bf16[2048,512]{1,0:T(8,128)(2,1)} %all-gather.6.cloned.1.call-done), kind=kOutput, calls=%fused_computation.61 | convolution fusion | flops 536870912 | bytes 3670016 | tf_op jit(solution)/shard_map/dot_general | solution.py:43
  88.9 3.5 %collective-permute-start.3 = (f32[128,512]{1,0:T(8,128)S(1)}, f32[128,512]{1,0:T(8,128)S(1)}, u32[]{:S(2)}, u32[]{:S(2)}) collective-permute-start(f32[128,512]{1,0:T(8,128)S(1)} %slice.59), channel_id=1, source_target_pairs={{0,8},{8,0},{1,9},{9,1},{2,10},{10,2},{3,11},{11,3},{4,12},{12,4},... | collective-permute-start | bytes 786440 | tf_op jit(solution)/shard_map/ppermute | solution.py:53
  94.2 3.1 %collective-permute-start.4 = (bf16[64,512]{1,0:T(8,128)(2,1)S(1)}, bf16[64,512]{1,0:T(8,128)(2,1)S(1)}, u32[]{:S(2)}, u32[]{:S(2)}) collective-permute-start(bf16[64,512]{1,0:T(8,128)(2,1)S(1)} %get-tuple-element.53), channel_id=1, source_target_pairs={{0,1},{1,0},{2,3},{3,2},{4,5},{5,4},{6,7},{7,6},{8,9},{9,8},{10,11... | collective-permute-start | bytes 196616 | tf_op jit(solution)/shard_map/ppermute | solution.py:57
  97.6 2.0 %collective-permute-done.4 = bf16[64,512]{1,0:T(8,128)(2,1)S(1)} collective-permute-done((bf16[64,512]{1,0:T(8,128)(2,1)S(1)}, bf16[64,512]{1,0:T(8,128)(2,1)S(1)}, u32[]{:S(2)}, u32[]{:S(2)}) %collective-permute-start.4) | collective-permute-done | bytes 65568 | tf_op jit(solution)/shard_map/ppermute | solution.py:57
  99.6 15.7 %all-to-all-done.1 = bf16[32,64,256]{2,1,0:T(8,128)(2,1)S(1)} async-done(((bf16[32,64,256]{2,1,0:T(8,128)(2,1)}), bf16[32,64,256]{2,1,0:T(8,128)(2,1)S(1)}, u32[]{:S(2)}, u32[]{:S(2)}) %all-to-all-start.1) | async-done | bytes 1048608 | tf_op jit(solution)/shard_map/all_to_all | solution.py:49
  115.4 7.7 %collective-permute-start.5 = (bf16[2048,256]{1,0:T(8,128)(2,1)S(1)}, bf16[2048,256]{1,0:T(8,128)(2,1)S(1)}, u32[]{:S(2)}, u32[]{:S(2)}) collective-permute-start(bf16[2048,256]{1,0:T(8,128)(2,1)S(1)} %bitcast.68), channel_id=1, source_target_pairs={{0,8},{8,0},{1,9},{9,1},{2,10},{10,2},{3,11},{11,3},{4,12},{12,4},... | collective-permute-start | bytes 3145736 | tf_op jit(solution)/shard_map/ppermute | solution.py:53
  125.4 6.2 %attend.1 = bf16[512,128]{1,0:T(8,128)(2,1)S(1)} custom-call(bf16[512,128]{1,0:T(8,128)(2,1)S(1)} %reshape.296.q_ref, bf16[2048,256]{1,0:T(8,128)(2,1)S(1)} %bitcast.69, bf16[2048,256]{1,0:T(8,128)(2,1)S(1)} %collective-permute-done.5.far_ref, s32[512,1]{1,0:T(8,128)S(1)} %reshape.306.qpos_ref, s32[1,4096]{1,0:T(1,128)S(1)} %add.127.kpos_ref), custom_call_target="tpu_custom_call" | custom-call | tf_op jit(solution)/shard_map/attend/pallas_call | solution.py:125
  131.7 3.0 %collective-permute-start.6 = (bf16[64,512]{1,0:T(8,128)(2,1)S(1)}, bf16[64,512]{1,0:T(8,128)(2,1)S(1)}, u32[]{:S(2)}, u32[]{:S(2)}) collective-permute-start(bf16[64,512]{1,0:T(8,128)(2,1)S(1)} %squeeze.61), channel_id=1, source_target_pairs={{0,1},{1,0},{2,3},{3,2},{4,5},{5,4},{6,7},{7,6},{8,9},{9,8},{10,11... | collective-permute-start | bytes 196616 | tf_op jit(solution)/shard_map/ppermute | solution.py:57
  134.7 2.4 %collective-permute-done.6 = bf16[64,512]{1,0:T(8,128)(2,1)S(1)} collective-permute-done((bf16[64,512]{1,0:T(8,128)(2,1)S(1)}, bf16[64,512]{1,0:T(8,128)(2,1)S(1)}, u32[]{:S(2)}, u32[]{:S(2)}) %collective-permute-start.6) | collective-permute-done | bytes 65568 | tf_op jit(solution)/shard_map/ppermute | solution.py:57
  137.1 3.0 %collective-permute-start.7 = (bf16[2048,512]{1,0:T(8,128)(2,1)}, bf16[2048,512]{1,0:T(8,128)(2,1)S(1)}, u32[]{:S(2)}, u32[]{:S(2)}) collective-permute-start(bf16[2048,512]{1,0:T(8,128)(2,1)} %all-gather.4.cloned.1.call-done), channel_id=1, source_target_pairs={{0,8},{8,0},{1,9},{9,1},{2,10},{10,2},{3,11},{11,3},{4,12},{12,4},... | collective-permute-start | bytes 6291464 | tf_op jit(solution)/shard_map/ppermute | solution.py:53
  140.2 2.3 %fusion = bf16[8,128,256]{1,2,0:T(8,128)(2,1)S(1)} fusion(bf16[8,256,512]{2,1,0:T(8,128)(2,1)} %bitcast.71, bf16[64,512]{1,0:T(8,128)(2,1)S(1)} %get-tuple-element.49, bf16[64,512]{1,0:T(8,128)(2,1)S(1)} %get-tuple-element.48), kind=kOutput, calls=%fused_computation.2 | convolution fusion | flops 268959744 | bytes 2752512 | tf_op jit(solution)/shard_map/td,gnd->gtn/dot_general | solution.py:275
  142.4 1.6 collective-permute-done.7
  145.9 7.6 %all-to-all-start.2 = ((bf16[8,128,512]{1,2,0:T(8,128)(2,1)}), bf16[8,128,512]{1,2,0:T(8,128)(2,1)S(1)}, u32[]{:S(2)}, u32[]{:S(2)}) async-start(bf16[8,128,512]{1,2,0:T(8,128)(2,1)} %pad_maximum_fusion.1), calls=%async_computation.3 | async-start | bytes 2097152 | tf_op jit(solution)/shard_map/all_to_all | solution.py:278
  154.5 13.9 %all-to-all-done.2 = bf16[8,128,512]{1,2,0:T(8,128)(2,1)S(1)} async-done(((bf16[8,128,512]{1,2,0:T(8,128)(2,1)}), bf16[8,128,512]{1,2,0:T(8,128)(2,1)S(1)}, u32[]{:S(2)}, u32[]{:S(2)}) %all-to-all-start.2) | async-done | bytes 1048608 | tf_op jit(solution)/shard_map/all_to_all | solution.py:278
  (90 shorter events, 17.5 us)
Async XLA Ops:
  8.0 78.5 %reduce-scatter.2.cloned.1.call-start = ((), (), s32[]{:S(2)}) async-start(), calls=%async_computation.6 | async-start | bytes 589824 | tf_op jit(solution)/shard_map/reduce_scatter | solution.py:218
  30.3 13.9 %copy-start.3 = (bf16[4096]{0:T(1024)(128)(2,1)S(1)}, bf16[4096]{0:T(1024)(128)(2,1)}, u32[]{:S(2)}) copy-start(bf16[4096]{0:T(1024)(128)(2,1)} %param.13) | copy-start | bytes 24580
  32.2 16.5 %copy-start.4 = (s32[2,64]{1,0:T(2,128)S(1)}, s32[2,64]{1,0:T(2,128)}, u32[]{:S(2)}) copy-start(s32[2,64]{1,0:T(2,128)} %param.19) | copy-start | bytes 1540
  32.2 54.3 %all-gather.6.cloned.1.call-start = ((), (), s32[]{:S(2)}) async-start(), calls=%async_computation.5 | async-start | bytes 2359296 | tf_op jit(solution)/shard_map/all_gather | solution.py:214
  34.8 23.4 %all-to-all-start = ((bf16[32,64,128]{2,1,0:T(8,128)(2,1)}), bf16[32,64,128]{2,1,0:T(8,128)(2,1)S(1)}, u32[]{:S(2)}, u32[]{:S(2)}) async-start(bf16[32,64,128]{2,1,0:T(8,128)(2,1)} %broadcast_in_dim.20), calls=%async_computation | async-start | bytes 1048576 | tf_op jit(solution)/shard_map/all_to_all | solution.py:49
  44.1 90.5 %all-gather.4.cloned.1.call-start = ((), (), s32[]{:S(2)}) async-start(), calls=%async_computation.4 | async-start | bytes 2359296 | tf_op jit(solution)/shard_map/all_gather | solution.py:222
  48.7 28.2 %copy-start = (bf16[128,2048]{1,0:T(8,128)(2,1)S(1)}, bf16[128,2048]{1,0:T(8,128)(2,1)}, u32[]{:S(2)}) copy-start(bf16[128,2048]{1,0:T(8,128)(2,1)} %get-tuple-element.22) | copy-start | bytes 1572868
  58.2 13.7 %collective-permute-start = (bf16[2048,128]{1,0:T(8,128)(2,1)S(1)}, bf16[2048,128]{1,0:T(8,128)(2,1)S(1)}, u32[]{:S(2)}, u32[]{:S(2)}) collective-permute-start(bf16[2048,128]{1,0:T(8,128)(2,1)S(1)} %bitcast.73), channel_id=1, source_target_pairs={{0,8},{8,0},{1,9},{9,1},{2,10},{10,2},{3,11},{11,3},{4,12},{12,4},... | collective-permute-start | bytes 1572872 | tf_op jit(solution)/shard_map/ppermute | solution.py:53
  68.6 8.3 %collective-permute-start.2 = (bf16[128,2048]{1,0:T(8,128)(2,1)}, bf16[128,2048]{1,0:T(8,128)(2,1)S(1)}, u32[]{:S(2)}, u32[]{:S(2)}) collective-permute-start(bf16[128,2048]{1,0:T(8,128)(2,1)} %get-tuple-element.24), channel_id=1, source_target_pairs={{0,8},{8,0},{1,9},{9,1},{2,10},{10,2},{3,11},{11,3},{4,12},{12,4},... | collective-permute-start | bytes 1572872 | tf_op jit(solution)/shard_map/ppermute | solution.py:53
  73.7 4.9 %collective-permute-start.1 = (bf16[64,128]{1,0:T(8,128)(2,1)S(1)}, bf16[64,128]{1,0:T(8,128)(2,1)S(1)}, u32[]{:S(2)}, u32[]{:S(2)}) collective-permute-start(bf16[64,128]{1,0:T(8,128)(2,1)S(1)} %get-tuple-element.57), channel_id=1, source_target_pairs={{0,1},{1,0},{2,3},{3,2},{4,5},{5,4},{6,7},{7,6},{8,9},{9,8},{10,11... | collective-permute-start | bytes 49160 | tf_op jit(solution)/shard_map/ppermute | solution.py:57
  79.8 35.6 %all-to-all-start.1 = ((bf16[32,64,256]{2,1,0:T(8,128)(2,1)}), bf16[32,64,256]{2,1,0:T(8,128)(2,1)S(1)}, u32[]{:S(2)}, u32[]{:S(2)}) async-start(bf16[32,64,256]{2,1,0:T(8,128)(2,1)} %broadcast_in_dim.24), calls=%async_computation.1 | async-start | bytes 2097152 | tf_op jit(solution)/shard_map/all_to_all | solution.py:49
  88.9 34.8 %copy-start.6 = (s32[2]{0:T(128)S(1)}, s32[2]{0:T(128)}, u32[]{:S(2)}) copy-start(s32[2]{0:T(128)} %param.18) | copy-start | bytes 28
  88.9 4.6 %collective-permute-start.3 = (f32[128,512]{1,0:T(8,128)S(1)}, f32[128,512]{1,0:T(8,128)S(1)}, u32[]{:S(2)}, u32[]{:S(2)}) collective-permute-start(f32[128,512]{1,0:T(8,128)S(1)} %slice.59), channel_id=1, source_target_pairs={{0,8},{8,0},{1,9},{9,1},{2,10},{10,2},{3,11},{11,3},{4,12},{12,4},... | collective-permute-start | bytes 786440 | tf_op jit(solution)/shard_map/ppermute | solution.py:53
  94.2 5.3 %collective-permute-start.4 = (bf16[64,512]{1,0:T(8,128)(2,1)S(1)}, bf16[64,512]{1,0:T(8,128)(2,1)S(1)}, u32[]{:S(2)}, u32[]{:S(2)}) collective-permute-start(bf16[64,512]{1,0:T(8,128)(2,1)S(1)} %get-tuple-element.53), channel_id=1, source_target_pairs={{0,1},{1,0},{2,3},{3,2},{4,5},{5,4},{6,7},{7,6},{8,9},{9,8},{10,11... | collective-permute-start | bytes 196616 | tf_op jit(solution)/shard_map/ppermute | solution.py:57
  115.4 10.0 %collective-permute-start.5 = (bf16[2048,256]{1,0:T(8,128)(2,1)S(1)}, bf16[2048,256]{1,0:T(8,128)(2,1)S(1)}, u32[]{:S(2)}, u32[]{:S(2)}) collective-permute-start(bf16[2048,256]{1,0:T(8,128)(2,1)S(1)} %bitcast.68), channel_id=1, source_target_pairs={{0,8},{8,0},{1,9},{9,1},{2,10},{10,2},{3,11},{11,3},{4,12},{12,4},... | collective-permute-start | bytes 3145736 | tf_op jit(solution)/shard_map/ppermute | solution.py:53
  131.7 5.4 %collective-permute-start.6 = (bf16[64,512]{1,0:T(8,128)(2,1)S(1)}, bf16[64,512]{1,0:T(8,128)(2,1)S(1)}, u32[]{:S(2)}, u32[]{:S(2)}) collective-permute-start(bf16[64,512]{1,0:T(8,128)(2,1)S(1)} %squeeze.61), channel_id=1, source_target_pairs={{0,1},{1,0},{2,3},{3,2},{4,5},{5,4},{6,7},{7,6},{8,9},{9,8},{10,11... | collective-permute-start | bytes 196616 | tf_op jit(solution)/shard_map/ppermute | solution.py:57
  137.1 7.0 %collective-permute-start.7 = (bf16[2048,512]{1,0:T(8,128)(2,1)}, bf16[2048,512]{1,0:T(8,128)(2,1)S(1)}, u32[]{:S(2)}, u32[]{:S(2)}) collective-permute-start(bf16[2048,512]{1,0:T(8,128)(2,1)} %all-gather.4.cloned.1.call-done), channel_id=1, source_target_pairs={{0,8},{8,0},{1,9},{9,1},{2,10},{10,2},{3,11},{11,3},{4,12},{12,4},... | collective-permute-start | bytes 6291464 | tf_op jit(solution)/shard_map/ppermute | solution.py:53
  144.7 8.7 %copy-start.5 = (s32[1,1,2]{2,1,0:T(1,128)S(1)}, s32[1,1,2]{2,1,0:T(1,128)}, u32[]{:S(2)}) copy-start(s32[1,1,2]{2,1,0:T(1,128)} %param.21) | copy-start | bytes 28
  144.8 8.8 %copy-start.1 = (bf16[1,1,16,16,1024]{4,3,2,1,0:T(8,128)(2,1)S(1)}, bf16[1,1,16,16,1024]{4,3,2,1,0:T(8,128)(2,1)}, u32[]{:S(2)}) copy-start(bf16[1,1,16,16,1024]{4,3,2,1,0:T(8,128)(2,1)} %param.20) | copy-start | bytes 1572868
  144.8 8.9 %copy-start.2 = (bf16[1,2,16,1024]{3,2,1,0:T(8,128)(2,1)S(1)}, bf16[1,2,16,1024]{3,2,1,0:T(8,128)(2,1)}, u32[]{:S(2)}) copy-start(bf16[1,2,16,1024]{3,2,1,0:T(8,128)(2,1)} %reduce-scatter.2.cloned.1.call-done) | copy-start | bytes 196612
  145.9 22.5 %all-to-all-start.2 = ((bf16[8,128,512]{1,2,0:T(8,128)(2,1)}), bf16[8,128,512]{1,2,0:T(8,128)(2,1)S(1)}, u32[]{:S(2)}, u32[]{:S(2)}) async-start(bf16[8,128,512]{1,2,0:T(8,128)(2,1)} %pad_maximum_fusion.1), calls=%async_computation.3 | async-start | bytes 2097152 | tf_op jit(solution)/shard_map/all_to_all | solution.py:278
Sparse Core Ops, SparseCore 0:
  32.3 47.5 reduce-scatter.1
Sparse Core Ops, SparseCore 1:
  34.8 46.6 all-gather.5
  83.3 50.8 all-gather.3

commit v4 on v3

--- a/solution.py
+++ b/solution.py
@@ -206,22 +206,25 @@
 
     key_cols = lax.dynamic_slice_in_dim(key_matrix, kv_first, HEAD_SIZE, 1)
     value_cols = lax.dynamic_slice_in_dim(value_matrix, kv_first, HEAD_SIZE, 1)
-    half_near = spread(jnp.where(mine == 0, key_cols, value_cols), CHIPS).reshape(-1, HEAD_SIZE)
-    weights = lax.all_gather(jnp.stack([w_query, w_out.T]), "zh", axis=0)
+    half_near = jnp.where(mine == 0, key_cols, value_cols)
+    weights = jnp.concatenate([w_query, w_out.T, half_near], axis=1)
+    weights = lax.all_gather(weights, "zh", axis=0, tiled=True)
     weights, leave = lax.optimization_barrier((weights, move_page))
-    wq_near = weights[:, 0].reshape(rows_z * piece, -1)
-    wo_near = weights[:, 1].reshape(rows_z * piece, -1)
+    cols = w_query.shape[1]
+    wq_near, wo_near = weights[:, :cols], weights[:, cols : 2 * cols]
+    half_near = spread(weights[:, 2 * cols :], "y").reshape(-1, HEAD_SIZE)
     wq_near = lax.all_gather(wq_near, "y", axis=0, tiled=True)
 
     x_near, x_far = split_norm(hidden_in.reshape(2 * span, width), norm_gain, core)
     send_pages = pages_to_send(cache_pages, leave, move_dest, move_slot)
     arrived = lax.psum_scatter(send_pages, REP, scatter_dimension=0, tiled=True)
+    x_other = swap_core(x_far)
     half_near, x_near, x_far, wo_near = lax.optimization_barrier(
         (half_near, x_near, x_far, wo_near)
     )
     wo_near = lax.all_gather(wo_near, "y", axis=0, tiled=True)
     half_far = swap_core(half_near)
-    x_chip = jnp.concatenate([x_near, swap_core(x_far)], axis=0)
+    x_chip = jnp.concatenate([x_near, x_other], axis=0)
 
     own_pair = lax.dynamic_slice_in_dim(pair_of_device, place, 1, 1)[:, 0]
     blocks = jnp.stack([own_pair, 2 * cycle - 1 - own_pair], axis=1)
@@ -263,23 +266,24 @@
     all_qpos = jnp.broadcast_to(my_qpos[None, :, None], (2, span, heads_here)).reshape(-1, 1)
     context = attend(all_q, near, far, all_qpos, kpos).reshape(2, span, heads_here * HEAD_SIZE)
     c_pair = swap_x(context[1])
-    wo_near, c_pair = lax.optimization_barrier((wo_near, c_pair))
     c_mine = context[0]
-    wo_far = swap_core(wo_near)
     context = jnp.concatenate(
         [jnp.where(mine == 0, c_mine, c_pair), jnp.where(mine == 0, c_pair, c_mine)], axis=0
     )
-
-    def partial(weight):
-        weight = weight.reshape(rows_y, rows_z * piece, -1)
-        return jnp.einsum("td,gnd->gtn", context, weight, preferred_element_type=jnp.float32)
-
-    send = jnp.concatenate([partial(wo_near), partial(wo_far)], axis=2).astype(jnp.bfloat16)
+    context = jnp.concatenate([context, swap_core(context)], axis=0)
+    context, wo_near = lax.optimization_barrier((context, wo_near))
+    send = jnp.einsum(
+        "td,gnd->gtn",
+        context,
+        wo_near.reshape(rows_y, rows_z * piece, -1),
+        preferred_element_type=jnp.float32,
+    ).astype(jnp.bfloat16)
     terms = lax.all_to_all(send, REP, split_axis=0, concat_axis=0, tiled=True)
     summed = jnp.sum(terms.astype(jnp.float32), axis=0).astype(jnp.bfloat16)
-    summed = summed.reshape(2 * span, 2, rows_z, piece)
-    first = jnp.where(core == 0, summed[:, 0], summed[:, 1])
-    second = jnp.where(core == 0, summed[:, 1], summed[:, 0])
+    near_cols = summed[: 2 * span].reshape(2 * span, rows_z, piece)
+    far_cols = swap_core(summed[2 * span :]).reshape(2 * span, rows_z, piece)
+    first = jnp.where(core == 0, near_cols, far_cols)
+    second = jnp.where(core == 0, far_cols, near_cols)
     attn_out = jnp.stack([first, second], axis=2).reshape(2, 1, 2, blk, -1)
     new_cache = settle_pages(cache_pages, move_page, arrived)
     return (attn_out, new_cache)

time: 178 us -> 170 us (0.955)
  waiting for transfers between devices: 47.5 us -> 39.7 us
    all_to_all x2, waiting for transfers between devices: 25.1 us -> 16.6 us  [spread(): return lax.all_to_all(copies, axes, split_axis=0, concat_axis=0, tiled=True)]
    all_to_all x2, starting transfers between devices: 16 us -> 10.8 us  [spread(): return lax.all_to_all(copies, axes, split_axis=0, concat_axis=0, tiled=True)]
    ppermute x5 -> x6, starting transfers between devices: 26.3 us -> 30.6 us  [swap_core(): return lax.ppermute(value, 'core', [(0, 1), (1, 0)])]
  transfers between devices with their start and end apart: 14 -> 15, of which waited for: 8 -> 10; matrix products, arithmetic and copies ran while one was open for 10% -> 8% of each run, Pallas kernels for 6% -> 6%
where the time goes in v4:
time: 170 us; the launch traced here: 169 us
  starting transfers between devices  58.8 us (35%)
  waiting for transfers between devices  39.7 us (23%)
  blocking collectives  22 us (13%)
  between operations  16 us (9%)
  Pallas kernels  11.9 us (7%)
  matrix products  8.48 us (5%)
  local copies, waits for them, and re-layouts  6.76 us (4%)
  other arithmetic  5.08 us (3%)
    ppermute x6, starting transfers between devices, swap_core(): return lax.ppermute(value, 'core', [(0, 1), (1, 0)])  30.6 us
    all_gather x1, blocking collectives, on_device(): weights = lax.all_gather(weights, 'zh', axis=0, tiled=True)  22 us
    all_to_all x2, waiting for transfers between devices, spread(): return lax.all_to_all(copies, axes, split_axis=0, concat_axis=0, tiled=True)  16.6 us
    all_to_all x1, waiting for transfers between devices, on_device(): terms = lax.all_to_all(send, REP, split_axis=0, concat_axis=0, tiled=True)  14.8 us
    all_to_all x2, starting transfers between devices, spread(): return lax.all_to_all(copies, axes, split_axis=0, concat_axis=0, tiled=True)  10.8 us
    ppermute x3, starting transfers between devices, swap_x(): lax.ppermute(value, 'x', [(i, i ^ 1) for i in range(lax.axis_size('x'))])  9.54 us
    all_to_all x1, starting transfers between devices, on_device(): terms = lax.all_to_all(send, REP, split_axis=0, concat_axis=0, tiled=True)  7.75 us
    pallas_call x1, Pallas kernels, attend(): pl.pallas_call(attend_kernel, grid=(rows // tile,), in_specs=[pl.BlockSpe...  6.07 us
  transfers between devices with their start and end apart: 15, of which 10 were waited for; matrix products, arithmetic and copies ran while one was open for 8% of the time, Pallas kernels for 6%

profile of v4, /device:TPU:1, one launch (start us, length us, event | category | flops | bytes accessed | tf_op | source)
XLA Modules:
  0.0 168.7 jit_solution(14443633987066532461)
XLA Ops:
  9.7 22.0 %all_gather.9 = bf16[256,1152]{1,0:T(8,128)(2,1)S(1)} all-gather(bf16[64,1152]{1,0:T(8,128)(2,1)S(1)} %pad_maximum_fusion.2), channel_id=1, replica_groups=mesh['y'=8,'zh'=4,'core'=2,'zl'=2,'x'=4] {'zh'}, dimensions={0}, use_global_device_ids=true | all-gather | bytes 737280 | tf_op jit(solution)/shard_map/all_gather | solution.py:211
  31.7 1.9 %pages_to_send.1 = bf16[8,2,16,1024]{3,2,1,0:T(8,128)(2,1)} custom-call(s32[2]{0:T(128)} %bitcast.70, s32[2]{0:T(128)} %bitcast.68, s32[2]{0:T(128)} %bitcast.69, bf16[16,16,1024]{2,1,0:T(8,128)(2,1)} %bitcast.57), custom_call_target="tpu_custom_call" | custom-call | tf_op jit(solution)/shard_map/pages_to_send/pallas_call | solution.py:160
  35.5 6.8 %all-to-all-start = ((bf16[8,256,128]{2,1,0:T(8,128)(2,1)}), bf16[8,256,128]{2,1,0:T(8,128)(2,1)S(1)}, u32[]{:S(2)}, u32[]{:S(2)}) async-start(bf16[8,256,128]{2,1,0:T(8,128)(2,1)} %broadcast_in_dim.20), calls=%async_computation | async-start | bytes 1048576 | tf_op jit(solution)/shard_map/all_to_all | solution.py:49
  43.0 3.9 %split_norm.1 = (bf16[128,2048]{1,0:T(8,128)(2,1)}, bf16[128,2048]{1,0:T(8,128)(2,1)}) custom-call(s32[1]{0:T(128)} %bitcast.2.core_ref, bf16[128,4096]{1,0:T(8,128)(2,1)} %bitcast.59, bf16[1,4096]{1,0:T(2,128)(2,1)} %broadcast_in_dim.21.gain_ref), custom_call_target="tpu_custom_call" | custom-call | tf_op jit(solution)/shard_map/split_norm/pallas_call | solution.py:81
  46.9 4.1 %collective-permute-start.2 = (bf16[128,2048]{1,0:T(8,128)(2,1)}, bf16[128,2048]{1,0:T(8,128)(2,1)S(1)}, u32[]{:S(2)}, u32[]{:S(2)}) collective-permute-start(bf16[128,2048]{1,0:T(8,128)(2,1)} %get-tuple-element.23), channel_id=1, source_target_pairs={{0,8},{8,0},{1,9},{9,1},{2,10},{10,2},{3,11},{11,3},{4,12},{12,4},... | collective-permute-start | bytes 1572872 | tf_op jit(solution)/shard_map/ppermute | solution.py:53
  51.2 6.8 %all-to-all-done = bf16[8,256,128]{2,1,0:T(8,128)(2,1)S(1)} async-done(((bf16[8,256,128]{2,1,0:T(8,128)(2,1)}), bf16[8,256,128]{2,1,0:T(8,128)(2,1)S(1)}, u32[]{:S(2)}, u32[]{:S(2)}) %all-to-all-start) | async-done | bytes 524320 | tf_op jit(solution)/shard_map/all_to_all | solution.py:49
  58.0 7.5 %collective-permute-start = (bf16[2048,128]{1,0:T(8,128)(2,1)S(1)}, bf16[2048,128]{1,0:T(8,128)(2,1)S(1)}, u32[]{:S(2)}, u32[]{:S(2)}) collective-permute-start(bf16[2048,128]{1,0:T(8,128)(2,1)S(1)} %bitcast.54), channel_id=1, source_target_pairs={{0,8},{8,0},{1,9},{9,1},{2,10},{10,2},{3,11},{11,3},{4,12},{12,4},... | collective-permute-start | bytes 1572872 | tf_op jit(solution)/shard_map/ppermute | solution.py:53
  65.6 1.4 fusion.14
  68.8 3.1 %collective-permute-start.1 = (bf16[64,128]{1,0:T(8,128)(2,1)S(1)}, bf16[64,128]{1,0:T(8,128)(2,1)S(1)}, u32[]{:S(2)}, u32[]{:S(2)}) collective-permute-start(bf16[64,128]{1,0:T(8,128)(2,1)S(1)} %get-tuple-element.55), channel_id=1, source_target_pairs={{0,1},{1,0},{2,3},{3,2},{4,5},{5,4},{6,7},{7,6},{8,9},{9,8},{10,11... | collective-permute-start | bytes 49160 | tf_op jit(solution)/shard_map/ppermute | solution.py:57
  72.1 1.7 collective-permute-done.1
  74.9 3.9 %all-to-all-start.1 = ((bf16[32,64,256]{2,1,0:T(8,128)(2,1)}), bf16[32,64,256]{2,1,0:T(8,128)(2,1)S(1)}, u32[]{:S(2)}, u32[]{:S(2)}) async-start(bf16[32,64,256]{2,1,0:T(8,128)(2,1)} %broadcast_in_dim.24), calls=%async_computation.1 | async-start | bytes 2097152 | tf_op jit(solution)/shard_map/all_to_all | solution.py:49
  80.0 2.3 %fusion.15 = f32[256,512]{1,0:T(8,128)S(1)} fusion(bf16[256,2048]{1,0:T(8,128)(2,1)S(1)} %pad_maximum_fusion, bf16[2048,512]{1,0:T(8,128)(2,1)} %all-gather.3.cloned.1.call-done), kind=kOutput, calls=%fused_computation.58 | convolution fusion | flops 536870912 | bytes 3670016 | tf_op jit(solution)/shard_map/dot_general | solution.py:43
  82.4 7.4 %collective-permute-start.3 = (f32[128,512]{1,0:T(8,128)S(1)}, f32[128,512]{1,0:T(8,128)S(1)}, u32[]{:S(2)}, u32[]{:S(2)}) collective-permute-start(f32[128,512]{1,0:T(8,128)S(1)} %slice.61), channel_id=1, source_target_pairs={{0,8},{8,0},{1,9},{9,1},{2,10},{10,2},{3,11},{11,3},{4,12},{12,4},... | collective-permute-start | bytes 786440 | tf_op jit(solution)/shard_map/ppermute | solution.py:53
  91.6 3.3 %collective-permute-start.4 = (bf16[64,512]{1,0:T(8,128)(2,1)S(1)}, bf16[64,512]{1,0:T(8,128)(2,1)S(1)}, u32[]{:S(2)}, u32[]{:S(2)}) collective-permute-start(bf16[64,512]{1,0:T(8,128)(2,1)S(1)} %get-tuple-element.51), channel_id=1, source_target_pairs={{0,1},{1,0},{2,3},{3,2},{4,5},{5,4},{6,7},{7,6},{8,9},{9,8},{10,11... | collective-permute-start | bytes 196616 | tf_op jit(solution)/shard_map/ppermute | solution.py:57
  97.1 9.8 %all-to-all-done.1 = bf16[32,64,256]{2,1,0:T(8,128)(2,1)S(1)} async-done(((bf16[32,64,256]{2,1,0:T(8,128)(2,1)}), bf16[32,64,256]{2,1,0:T(8,128)(2,1)S(1)}, u32[]{:S(2)}, u32[]{:S(2)}) %all-to-all-start.1) | async-done | bytes 1048608 | tf_op jit(solution)/shard_map/all_to_all | solution.py:49
  106.8 5.5 %collective-permute-start.5 = (bf16[2048,256]{1,0:T(8,128)(2,1)S(1)}, bf16[2048,256]{1,0:T(8,128)(2,1)S(1)}, u32[]{:S(2)}, u32[]{:S(2)}) collective-permute-start(bf16[2048,256]{1,0:T(8,128)(2,1)S(1)} %bitcast.52), channel_id=1, source_target_pairs={{0,8},{8,0},{1,9},{9,1},{2,10},{10,2},{3,11},{11,3},{4,12},{12,4},... | collective-permute-start | bytes 3145736 | tf_op jit(solution)/shard_map/ppermute | solution.py:53
  114.6 6.1 %attend.1 = bf16[512,128]{1,0:T(8,128)(2,1)S(1)} custom-call(bf16[512,128]{1,0:T(8,128)(2,1)S(1)} %reshape.292.q_ref, bf16[2048,256]{1,0:T(8,128)(2,1)S(1)} %bitcast.53, bf16[2048,256]{1,0:T(8,128)(2,1)S(1)} %collective-permute-done.5.far_ref, s32[512,1]{1,0:T(8,128)S(1)} %reshape.299.qpos_ref, s32[1,4096]{1,0:T(1,128)S(1)} %add.127.kpos_ref), custom_call_target="tpu_custom_call" | custom-call | tf_op jit(solution)/shard_map/attend/pallas_call | solution.py:125
  120.8 3.2 %collective-permute-start.6 = (bf16[64,512]{1,0:T(8,128)(2,1)S(1)}, bf16[64,512]{1,0:T(8,128)(2,1)S(1)}, u32[]{:S(2)}, u32[]{:S(2)}) collective-permute-start(bf16[64,512]{1,0:T(8,128)(2,1)S(1)} %squeeze.58), channel_id=1, source_target_pairs={{0,1},{1,0},{2,3},{3,2},{4,5},{5,4},{6,7},{7,6},{8,9},{9,8},{10,11... | collective-permute-start | bytes 196616 | tf_op jit(solution)/shard_map/ppermute | solution.py:57
  124.0 1.8 %collective-permute-done.6 = bf16[64,512]{1,0:T(8,128)(2,1)S(1)} collective-permute-done((bf16[64,512]{1,0:T(8,128)(2,1)S(1)}, bf16[64,512]{1,0:T(8,128)(2,1)S(1)}, u32[]{:S(2)}, u32[]{:S(2)}) %collective-permute-start.6) | collective-permute-done | bytes 65568 | tf_op jit(solution)/shard_map/ppermute | solution.py:57
  125.8 3.4 %collective-permute-start.7 = (bf16[128,512]{1,0:T(8,128)(2,1)S(1)}, bf16[128,512]{1,0:T(8,128)(2,1)S(1)}, u32[]{:S(2)}, u32[]{:S(2)}) collective-permute-start(bf16[128,512]{1,0:T(8,128)(2,1)S(1)} %pad_maximum_fusion.5), channel_id=1, source_target_pairs={{0,8},{8,0},{1,9},{9,1},{2,10},{10,2},{3,11},{11,3},{4,12},{12,4},... | collective-permute-start | bytes 393224 | tf_op jit(solution)/shard_map/ppermute | solution.py:53
  130.3 3.4 %fusion = bf16[8,256,256]{1,2,0:T(8,128)(2,1)} fusion(bf16[8,256,512]{2,1,0:T(8,128)(2,1)} %bitcast.56, bf16[256,512]{1,0:T(8,128)(2,1)S(1)} %pad_maximum_fusion.1), kind=kOutput, calls=%fused_computation.1 | convolution fusion | flops 537395200 | bytes 3407872 | tf_op jit(solution)/shard_map/td,gnd->gtn/dot_general | solution.py:275
  133.7 7.7 %all-to-all-start.2 = ((bf16[8,256,256]{1,2,0:T(8,128)(2,1)}), bf16[8,256,256]{1,2,0:T(8,128)(2,1)S(1)}, u32[]{:S(2)}, u32[]{:S(2)}) async-start(bf16[8,256,256]{1,2,0:T(8,128)(2,1)} %fusion), calls=%async_computation.3 | async-start | bytes 2097152 | tf_op jit(solution)/shard_map/all_to_all | solution.py:281
  141.6 14.8 %all-to-all-done.2 = bf16[8,256,256]{1,2,0:T(8,128)(2,1)S(1)} async-done(((bf16[8,256,256]{1,2,0:T(8,128)(2,1)}), bf16[8,256,256]{1,2,0:T(8,128)(2,1)S(1)}, u32[]{:S(2)}, u32[]{:S(2)}) %all-to-all-start.2) | async-done | bytes 1048608 | tf_op jit(solution)/shard_map/all_to_all | solution.py:281
  156.5 2.7 %collective-permute-start.8 = (bf16[128,256]{0,1:T(8,128)(2,1)S(1)}, bf16[128,256]{0,1:T(8,128)(2,1)S(1)}, u32[]{:S(2)}, u32[]{:S(2)}) collective-permute-start(bf16[128,256]{0,1:T(8,128)(2,1)S(1)} %slice.67), channel_id=1, source_target_pairs={{0,8},{8,0},{1,9},{9,1},{2,10},{10,2},{3,11},{11,3},{4,12},{12,4},... | collective-permute-start | bytes 196616 | tf_op jit(solution)/shard_map/ppermute | solution.py:53
  (94 shorter events, 18.2 us)
Async XLA Ops:
  8.0 71.4 %reduce-scatter.2.cloned.1.call-start = ((), (), s32[]{:S(2)}) async-start(), calls=%async_computation.5 | async-start | bytes 589824 | tf_op jit(solution)/shard_map/reduce_scatter | solution.py:220
  31.7 10.6 %copy-start.3 = (bf16[4096]{0:T(1024)(128)(2,1)S(1)}, bf16[4096]{0:T(1024)(128)(2,1)}, u32[]{:S(2)}) copy-start(bf16[4096]{0:T(1024)(128)(2,1)} %param.13) | copy-start | bytes 24580
  33.7 17.3 %copy-start.4 = (s32[2,64]{1,0:T(2,128)S(1)}, s32[2,64]{1,0:T(2,128)}, u32[]{:S(2)}) copy-start(s32[2,64]{1,0:T(2,128)} %param.19) | copy-start | bytes 1540
  33.7 46.4 %all-gather.3.cloned.1.call-start = ((), (), s32[]{:S(2)}) async-start(), calls=%async_computation.4 | async-start | bytes 2359296 | tf_op jit(solution)/shard_map/all_gather | solution.py:216
  35.5 22.5 %all-to-all-start = ((bf16[8,256,128]{2,1,0:T(8,128)(2,1)}), bf16[8,256,128]{2,1,0:T(8,128)(2,1)S(1)}, u32[]{:S(2)}, u32[]{:S(2)}) async-start(bf16[8,256,128]{2,1,0:T(8,128)(2,1)} %broadcast_in_dim.20), calls=%async_computation | async-start | bytes 1048576 | tf_op jit(solution)/shard_map/all_to_all | solution.py:49
  46.9 25.1 %copy-start = (bf16[128,2048]{1,0:T(8,128)(2,1)S(1)}, bf16[128,2048]{1,0:T(8,128)(2,1)}, u32[]{:S(2)}) copy-start(bf16[128,2048]{1,0:T(8,128)(2,1)} %get-tuple-element.21) | copy-start | bytes 1572868
  46.9 25.1 %collective-permute-start.2 = (bf16[128,2048]{1,0:T(8,128)(2,1)}, bf16[128,2048]{1,0:T(8,128)(2,1)S(1)}, u32[]{:S(2)}, u32[]{:S(2)}) collective-permute-start(bf16[128,2048]{1,0:T(8,128)(2,1)} %get-tuple-element.23), channel_id=1, source_target_pairs={{0,8},{8,0},{1,9},{9,1},{2,10},{10,2},{3,11},{11,3},{4,12},{12,4},... | collective-permute-start | bytes 1572872 | tf_op jit(solution)/shard_map/ppermute | solution.py:53
  58.0 9.1 %collective-permute-start = (bf16[2048,128]{1,0:T(8,128)(2,1)S(1)}, bf16[2048,128]{1,0:T(8,128)(2,1)S(1)}, u32[]{:S(2)}, u32[]{:S(2)}) collective-permute-start(bf16[2048,128]{1,0:T(8,128)(2,1)S(1)} %bitcast.54), channel_id=1, source_target_pairs={{0,8},{8,0},{1,9},{9,1},{2,10},{10,2},{3,11},{11,3},{4,12},{12,4},... | collective-permute-start | bytes 1572872 | tf_op jit(solution)/shard_map/ppermute | solution.py:53
  68.8 4.9 %collective-permute-start.1 = (bf16[64,128]{1,0:T(8,128)(2,1)S(1)}, bf16[64,128]{1,0:T(8,128)(2,1)S(1)}, u32[]{:S(2)}, u32[]{:S(2)}) collective-permute-start(bf16[64,128]{1,0:T(8,128)(2,1)S(1)} %get-tuple-element.55), channel_id=1, source_target_pairs={{0,1},{1,0},{2,3},{3,2},{4,5},{5,4},{6,7},{7,6},{8,9},{9,8},{10,11... | collective-permute-start | bytes 49160 | tf_op jit(solution)/shard_map/ppermute | solution.py:57
  74.9 32.0 %all-to-all-start.1 = ((bf16[32,64,256]{2,1,0:T(8,128)(2,1)}), bf16[32,64,256]{2,1,0:T(8,128)(2,1)S(1)}, u32[]{:S(2)}, u32[]{:S(2)}) async-start(bf16[32,64,256]{2,1,0:T(8,128)(2,1)} %broadcast_in_dim.24), calls=%async_computation.1 | async-start | bytes 2097152 | tf_op jit(solution)/shard_map/all_to_all | solution.py:49
  78.8 51.5 %all-gather.5.cloned.1.call-start = ((), (), s32[]{:S(2)}) async-start(), calls=%async_computation.6 | async-start | bytes 2359296 | tf_op jit(solution)/shard_map/all_gather | solution.py:225
  82.3 12.6 %copy-start.6 = (s32[2]{0:T(128)S(1)}, s32[2]{0:T(128)}, u32[]{:S(2)}) copy-start(s32[2]{0:T(128)} %param.18) | copy-start | bytes 28
  82.4 8.5 %collective-permute-start.3 = (f32[128,512]{1,0:T(8,128)S(1)}, f32[128,512]{1,0:T(8,128)S(1)}, u32[]{:S(2)}, u32[]{:S(2)}) collective-permute-start(f32[128,512]{1,0:T(8,128)S(1)} %slice.61), channel_id=1, source_target_pairs={{0,8},{8,0},{1,9},{9,1},{2,10},{10,2},{3,11},{11,3},{4,12},{12,4},... | collective-permute-start | bytes 786440 | tf_op jit(solution)/shard_map/ppermute | solution.py:53
  91.6 5.3 %collective-permute-start.4 = (bf16[64,512]{1,0:T(8,128)(2,1)S(1)}, bf16[64,512]{1,0:T(8,128)(2,1)S(1)}, u32[]{:S(2)}, u32[]{:S(2)}) collective-permute-start(bf16[64,512]{1,0:T(8,128)(2,1)S(1)} %get-tuple-element.51), channel_id=1, source_target_pairs={{0,1},{1,0},{2,3},{3,2},{4,5},{5,4},{6,7},{7,6},{8,9},{9,8},{10,11... | collective-permute-start | bytes 196616 | tf_op jit(solution)/shard_map/ppermute | solution.py:57
  106.8 7.8 %collective-permute-start.5 = (bf16[2048,256]{1,0:T(8,128)(2,1)S(1)}, bf16[2048,256]{1,0:T(8,128)(2,1)S(1)}, u32[]{:S(2)}, u32[]{:S(2)}) collective-permute-start(bf16[2048,256]{1,0:T(8,128)(2,1)S(1)} %bitcast.52), channel_id=1, source_target_pairs={{0,8},{8,0},{1,9},{9,1},{2,10},{10,2},{3,11},{11,3},{4,12},{12,4},... | collective-permute-start | bytes 3145736 | tf_op jit(solution)/shard_map/ppermute | solution.py:53
  120.8 5.0 %collective-permute-start.6 = (bf16[64,512]{1,0:T(8,128)(2,1)S(1)}, bf16[64,512]{1,0:T(8,128)(2,1)S(1)}, u32[]{:S(2)}, u32[]{:S(2)}) collective-permute-start(bf16[64,512]{1,0:T(8,128)(2,1)S(1)} %squeeze.58), channel_id=1, source_target_pairs={{0,1},{1,0},{2,3},{3,2},{4,5},{5,4},{6,7},{7,6},{8,9},{9,8},{10,11... | collective-permute-start | bytes 196616 | tf_op jit(solution)/shard_map/ppermute | solution.py:57
  125.8 4.4 %collective-permute-start.7 = (bf16[128,512]{1,0:T(8,128)(2,1)S(1)}, bf16[128,512]{1,0:T(8,128)(2,1)S(1)}, u32[]{:S(2)}, u32[]{:S(2)}) collective-permute-start(bf16[128,512]{1,0:T(8,128)(2,1)S(1)} %pad_maximum_fusion.5), channel_id=1, source_target_pairs={{0,8},{8,0},{1,9},{9,1},{2,10},{10,2},{3,11},{11,3},{4,12},{12,4},... | collective-permute-start | bytes 393224 | tf_op jit(solution)/shard_map/ppermute | solution.py:53
  130.3 11.2 %copy-start.5 = (s32[1,1,2]{2,1,0:T(1,128)S(1)}, s32[1,1,2]{2,1,0:T(1,128)}, u32[]{:S(2)}) copy-start(s32[1,1,2]{2,1,0:T(1,128)} %param.21) | copy-start | bytes 28
  130.3 11.2 %copy-start.1 = (bf16[1,1,16,16,1024]{4,3,2,1,0:T(8,128)(2,1)S(1)}, bf16[1,1,16,16,1024]{4,3,2,1,0:T(8,128)(2,1)}, u32[]{:S(2)}) copy-start(bf16[1,1,16,16,1024]{4,3,2,1,0:T(8,128)(2,1)} %param.20) | copy-start | bytes 1572868
  133.7 25.6 %copy-start.2 = (bf16[1,2,16,1024]{3,2,1,0:T(8,128)(2,1)S(1)}, bf16[1,2,16,1024]{3,2,1,0:T(8,128)(2,1)}, u32[]{:S(2)}) copy-start(bf16[1,2,16,1024]{3,2,1,0:T(8,128)(2,1)} %reduce-scatter.2.cloned.1.call-done) | copy-start | bytes 196612
  133.7 22.7 %all-to-all-start.2 = ((bf16[8,256,256]{1,2,0:T(8,128)(2,1)}), bf16[8,256,256]{1,2,0:T(8,128)(2,1)S(1)}, u32[]{:S(2)}, u32[]{:S(2)}) async-start(bf16[8,256,256]{1,2,0:T(8,128)(2,1)} %fusion), calls=%async_computation.3 | async-start | bytes 2097152 | tf_op jit(solution)/shard_map/all_to_all | solution.py:281
  156.5 3.6 %collective-permute-start.8 = (bf16[128,256]{0,1:T(8,128)(2,1)S(1)}, bf16[128,256]{0,1:T(8,128)(2,1)S(1)}, u32[]{:S(2)}, u32[]{:S(2)}) collective-permute-start(bf16[128,256]{0,1:T(8,128)(2,1)S(1)} %slice.67), channel_id=1, source_target_pairs={{0,8},{8,0},{1,9},{9,1},{2,10},{10,2},{3,11},{11,3},{4,12},{12,4},... | collective-permute-start | bytes 196616 | tf_op jit(solution)/shard_map/ppermute | solution.py:53
Sparse Core Ops, SparseCore 0:
  33.8 39.9 reduce-scatter.1
Sparse Core Ops, SparseCore 1:
  36.2 43.7 all-gather.2
  82.0 45.4 all-gather.4

commit v5 on v3

--- a/solution.py
+++ b/solution.py
@@ -206,22 +206,21 @@
 
     key_cols = lax.dynamic_slice_in_dim(key_matrix, kv_first, HEAD_SIZE, 1)
     value_cols = lax.dynamic_slice_in_dim(value_matrix, kv_first, HEAD_SIZE, 1)
-    half_near = spread(jnp.where(mine == 0, key_cols, value_cols), CHIPS).reshape(-1, HEAD_SIZE)
-    weights = lax.all_gather(jnp.stack([w_query, w_out.T]), "zh", axis=0)
+    half_near = jnp.where(mine == 0, key_cols, value_cols)
+    weights = jnp.concatenate([w_query, w_out.T, half_near], axis=1)
+    weights = lax.all_gather(weights, "zh", axis=0, tiled=True)
     weights, leave = lax.optimization_barrier((weights, move_page))
-    wq_near = weights[:, 0].reshape(rows_z * piece, -1)
-    wo_near = weights[:, 1].reshape(rows_z * piece, -1)
-    wq_near = lax.all_gather(wq_near, "y", axis=0, tiled=True)
+    cols = w_query.shape[1]
+    half_near = spread(weights[:, 2 * cols :], "y").reshape(-1, HEAD_SIZE)
+    weights = lax.all_gather(weights[:, : 2 * cols], "y", axis=0, tiled=True)
 
     x_near, x_far = split_norm(hidden_in.reshape(2 * span, width), norm_gain, core)
     send_pages = pages_to_send(cache_pages, leave, move_dest, move_slot)
     arrived = lax.psum_scatter(send_pages, REP, scatter_dimension=0, tiled=True)
-    half_near, x_near, x_far, wo_near = lax.optimization_barrier(
-        (half_near, x_near, x_far, wo_near)
-    )
-    wo_near = lax.all_gather(wo_near, "y", axis=0, tiled=True)
+    x_other = swap_core(x_far)
+    half_near, x_near, x_far = lax.optimization_barrier((half_near, x_near, x_far))
     half_far = swap_core(half_near)
-    x_chip = jnp.concatenate([x_near, swap_core(x_far)], axis=0)
+    x_chip = jnp.concatenate([x_near, x_other], axis=0)
 
     own_pair = lax.dynamic_slice_in_dim(pair_of_device, place, 1, 1)[:, 0]
     blocks = jnp.stack([own_pair, 2 * cycle - 1 - own_pair], axis=1)
@@ -240,15 +239,21 @@
     )
     kv, x_chip = lax.optimization_barrier((kv, x_chip))
     near = spread(kv, CHIPS).reshape(-1, 2 * HEAD_SIZE)
-    wq_near, arrived = lax.optimization_barrier((wq_near, arrived))
-    query = matmul(x_chip, wq_near)
+    weights, arrived = lax.optimization_barrier((weights, arrived))
+    query = matmul(x_chip, weights[:, :cols])
+    query, weights = lax.optimization_barrier((query, weights))
+    wo_near = weights[:, cols:]
+    wo_far = swap_core(wo_near)
     query = query[: 2 * span] + swap_core(query[2 * span :])
     query = apply_rotation(
         query.reshape(2 * span, heads_here, HEAD_SIZE), cosine_table, sine_table
     ).astype(jnp.bfloat16)
     query = query.reshape(2, span, heads_here * HEAD_SIZE)
     q_mine = lax.dynamic_index_in_dim(query, mine, 0, False)
-    q_pair = swap_x(lax.dynamic_index_in_dim(query, 1 - mine, 0, False))
+    q_send = lax.dynamic_index_in_dim(query, 1 - mine, 0, False)
+    near, q_send = lax.optimization_barrier((near, q_send))
+    far = swap_core(near)
+    q_pair = swap_x(q_send)
 
     pairs = lax.dynamic_index_in_dim(pair_of_device, mine, 0, False).reshape(-1, 2)
     pairs = jnp.where(core == 0, pairs, pairs[:, ::-1]).T.reshape(-1)
@@ -258,14 +263,10 @@
     my_len = lax.dynamic_index_in_dim(prompt_len, mine, 0, False)
     my_qpos = jnp.where(my_qpos < my_len, my_qpos, -1)
     all_q = jnp.stack([q_mine, q_pair]).reshape(-1, HEAD_SIZE)
-    near, all_q = lax.optimization_barrier((near, all_q))
-    far = swap_core(near)
     all_qpos = jnp.broadcast_to(my_qpos[None, :, None], (2, span, heads_here)).reshape(-1, 1)
     context = attend(all_q, near, far, all_qpos, kpos).reshape(2, span, heads_here * HEAD_SIZE)
     c_pair = swap_x(context[1])
-    wo_near, c_pair = lax.optimization_barrier((wo_near, c_pair))
     c_mine = context[0]
-    wo_far = swap_core(wo_near)
     context = jnp.concatenate(
         [jnp.where(mine == 0, c_mine, c_pair), jnp.where(mine == 0, c_pair, c_mine)], axis=0
     )

time: 178 us -> 187 us (1.051); the launches traced: 177 us -> 184 us
  waiting for transfers between devices: 47.5 us -> 66.7 us
  starting transfers between devices: 59.3 us -> 42.1 us
  local copies, waits for them, and re-layouts: 6.78 us -> 9.79 us
    all_gather x2 -> x1, waiting for transfers between devices: 0.05 us -> 44.1 us  [on_device(): weights = lax.all_gather(weights[:, :2 * cols], 'y', axis=0, tiled=True)]
    all_to_all x2, waiting for transfers between devices: 25.1 us -> 6.82 us  [spread(): return lax.all_to_all(copies, axes, split_axis=0, concat_axis=0, tiled=True)]
    ppermute x5, starting transfers between devices: 26.3 us -> 15.9 us  [swap_core(): return lax.ppermute(value, 'core', [(0, 1), (1, 0)])]
    all_to_all x2, starting transfers between devices: 16 us -> 11.3 us  [spread(): return lax.all_to_all(copies, axes, split_axis=0, concat_axis=0, tiled=True)]
    all_to_all x1, waiting for transfers between devices: 13.9 us -> 10.5 us  [on_device(): terms = lax.all_to_all(send, REP, split_axis=0, concat_axis=0, tiled=True)]
    slice x1 -> x3, local copies, waits for them, and re-layouts: 0.83 us -> 3.94 us  [the longest x1 3.08 us: on_device(): wo_near = weights[:, cols:]]
    ppermute x5, waiting for transfers between devices: 2.43 us -> 0.01 us  [swap_core(): return lax.ppermute(value, 'core', [(0, 1), (1, 0)])]
    all_to_all x1, starting transfers between devices: 7.59 us -> 5.55 us  [on_device(): terms = lax.all_to_all(send, REP, split_axis=0, concat_axis=0, tiled=True)]
  transfers between devices with their start and end apart: 14 -> 13, of which waited for: 8 -> 6; matrix products, arithmetic and copies ran while one was open for 10% -> 11% of each run, Pallas kernels for 6% -> 5%
where the time goes in v5:
time: 187 us; the launch traced here: 184 us
  waiting for transfers between devices  66.7 us (36%)
  starting transfers between devices  42.1 us (23%)
  blocking collectives  22 us (12%)
  between operations  16 us (9%)
  Pallas kernels  11.7 us (6%)
  local copies, waits for them, and re-layouts  9.79 us (5%)
  matrix products  9.68 us (5%)
  other arithmetic  6.15 us (3%)
    all_gather x1, waiting for transfers between devices, on_device(): weights = lax.all_gather(weights[:, :2 * cols], 'y', axis=0, tiled=True)  44.1 us
    all_gather x1, blocking collectives, on_device(): weights = lax.all_gather(weights, 'zh', axis=0, tiled=True)  22 us
    ppermute x5, starting transfers between devices, swap_core(): return lax.ppermute(value, 'core', [(0, 1), (1, 0)])  15.9 us
    all_to_all x2, starting transfers between devices, spread(): return lax.all_to_all(copies, axes, split_axis=0, concat_axis=0, tiled=True)  11.3 us
    all_to_all x1, waiting for transfers between devices, on_device(): terms = lax.all_to_all(send, REP, split_axis=0, concat_axis=0, tiled=True)  10.5 us
    ppermute x3, starting transfers between devices, swap_x(): lax.ppermute(value, 'x', [(i, i ^ 1) for i in range(lax.axis_size('x'))])  9.31 us
    all_to_all x2, waiting for transfers between devices, spread(): return lax.all_to_all(copies, axes, split_axis=0, concat_axis=0, tiled=True)  6.82 us
    pallas_call x1, Pallas kernels, attend(): pl.pallas_call(attend_kernel, grid=(rows // tile,), in_specs=[pl.BlockSpe...  5.87 us
  transfers between devices with their start and end apart: 13, of which 6 were waited for; matrix products, arithmetic and copies ran while one was open for 11% of the time, Pallas kernels for 5%

profile of v5, /device:TPU:1, one launch (start us, length us, event | category | flops | bytes accessed | tf_op | source)
XLA Modules:
  0.0 184.1 jit_solution(12062799533913879369)
XLA Ops:
  9.7 22.0 %all_gather.6 = bf16[256,1152]{1,0:T(8,128)(2,1)S(1)} all-gather(bf16[64,1152]{1,0:T(8,128)(2,1)S(1)} %pad_maximum_fusion.2), channel_id=1, replica_groups=mesh['y'=8,'zh'=4,'core'=2,'zl'=2,'x'=4] {'zh'}, dimensions={0}, use_global_device_ids=true | all-gather | bytes 737280 | tf_op jit(solution)/shard_map/all_gather | solution.py:211
  31.8 1.9 %pages_to_send.1 = bf16[8,2,16,1024]{3,2,1,0:T(8,128)(2,1)} custom-call(s32[2]{0:T(128)} %bitcast.77, s32[2]{0:T(128)} %bitcast.75, s32[2]{0:T(128)} %bitcast.76, bf16[16,16,1024]{2,1,0:T(8,128)(2,1)} %bitcast.65), custom_call_target="tpu_custom_call" | custom-call | tf_op jit(solution)/shard_map/pages_to_send/pallas_call | solution.py:160
  35.5 6.8 %all-to-all-start = ((bf16[8,256,128]{2,1,0:T(8,128)(2,1)}), bf16[8,256,128]{2,1,0:T(8,128)(2,1)S(1)}, u32[]{:S(2)}, u32[]{:S(2)}) async-start(bf16[8,256,128]{2,1,0:T(8,128)(2,1)} %broadcast_in_dim.20), calls=%async_computation | async-start | bytes 1048576 | tf_op jit(solution)/shard_map/all_to_all | solution.py:49
  43.0 3.9 %split_norm.1 = (bf16[128,2048]{1,0:T(8,128)(2,1)}, bf16[128,2048]{1,0:T(8,128)(2,1)}) custom-call(s32[1]{0:T(128)} %bitcast.2.core_ref, bf16[128,4096]{1,0:T(8,128)(2,1)} %bitcast.67, bf16[1,4096]{1,0:T(2,128)(2,1)} %broadcast_in_dim.21.gain_ref), custom_call_target="tpu_custom_call" | custom-call | tf_op jit(solution)/shard_map/split_norm/pallas_call | solution.py:81
  46.9 4.1 %collective-permute-start.2 = (bf16[128,2048]{1,0:T(8,128)(2,1)}, bf16[128,2048]{1,0:T(8,128)(2,1)S(1)}, u32[]{:S(2)}, u32[]{:S(2)}) collective-permute-start(bf16[128,2048]{1,0:T(8,128)(2,1)} %get-tuple-element.22), channel_id=1, source_target_pairs={{0,8},{8,0},{1,9},{9,1},{2,10},{10,2},{3,11},{11,3},{4,12},{12,4},... | collective-permute-start | bytes 1572872 | tf_op jit(solution)/shard_map/ppermute | solution.py:53
  51.2 6.8 %all-to-all-done = bf16[8,256,128]{2,1,0:T(8,128)(2,1)S(1)} async-done(((bf16[8,256,128]{2,1,0:T(8,128)(2,1)}), bf16[8,256,128]{2,1,0:T(8,128)(2,1)S(1)}, u32[]{:S(2)}, u32[]{:S(2)}) %all-to-all-start) | async-done | bytes 524320 | tf_op jit(solution)/shard_map/all_to_all | solution.py:49
  58.0 4.9 %collective-permute-start = (bf16[2048,128]{1,0:T(8,128)(2,1)S(1)}, bf16[2048,128]{1,0:T(8,128)(2,1)S(1)}, u32[]{:S(2)}, u32[]{:S(2)}) collective-permute-start(bf16[2048,128]{1,0:T(8,128)(2,1)S(1)} %bitcast.63), channel_id=1, source_target_pairs={{0,8},{8,0},{1,9},{9,1},{2,10},{10,2},{3,11},{11,3},{4,12},{12,4},... | collective-permute-start | bytes 1572872 | tf_op jit(solution)/shard_map/ppermute | solution.py:53
  66.3 3.1 %collective-permute-start.1 = (bf16[64,128]{1,0:T(8,128)(2,1)S(1)}, bf16[64,128]{1,0:T(8,128)(2,1)S(1)}, u32[]{:S(2)}, u32[]{:S(2)}) collective-permute-start(bf16[64,128]{1,0:T(8,128)(2,1)S(1)} %get-tuple-element.51), channel_id=1, source_target_pairs={{0,1},{1,0},{2,3},{3,2},{4,5},{5,4},{6,7},{7,6},{8,9},{9,8},{10,11... | collective-permute-start | bytes 49160 | tf_op jit(solution)/shard_map/ppermute | solution.py:57
  69.5 1.7 collective-permute-done.1
  72.3 4.5 %all-to-all-start.1 = ((bf16[32,64,256]{2,1,0:T(8,128)(2,1)}), bf16[32,64,256]{2,1,0:T(8,128)(2,1)S(1)}, u32[]{:S(2)}, u32[]{:S(2)}) async-start(bf16[32,64,256]{2,1,0:T(8,128)(2,1)} %broadcast_in_dim.24), calls=%async_computation.2 | async-start | bytes 2097152 | tf_op jit(solution)/shard_map/all_to_all | solution.py:49
  76.8 44.1 %all-gather.2.cloned.1.call-done = bf16[2048,1024]{1,0:T(8,128)(2,1)} async-done(((bf16[256,1024]{1,0:T(8,128)(2,1)}), bf16[2048,1024]{1,0:T(8,128)(2,1)}) %all-gather.2.cloned.1.call-update) | async-done | bytes 4194320 | tf_op jit(solution)/shard_map/all_gather | solution.py:215
  121.0 2.3 %fusion = f32[256,512]{1,0:T(8,128)S(1)} fusion(bf16[256,2048]{1,0:T(8,128)(2,1)S(1)} %pad_maximum_fusion, bf16[2048,1024]{1,0:T(8,128)(2,1)} %all-gather.2.cloned.1.call-done), kind=kOutput, calls=%fused_computation | convolution fusion | flops 536870912 | bytes 3670016 | tf_op jit(solution)/shard_map/dot_general | solution.py:43
  123.3 2.4 %collective-permute-start.3 = (f32[128,512]{1,0:T(8,128)S(1)}, f32[128,512]{1,0:T(8,128)S(1)}, u32[]{:S(2)}, u32[]{:S(2)}) collective-permute-start(f32[128,512]{1,0:T(8,128)S(1)} %slice.56), channel_id=1, source_target_pairs={{0,8},{8,0},{1,9},{9,1},{2,10},{10,2},{3,11},{11,3},{4,12},{12,4},... | collective-permute-start | bytes 786440 | tf_op jit(solution)/shard_map/ppermute | solution.py:53
  126.2 3.1 %slice.54 = bf16[2048,512]{1,0:T(8,128)(2,1)} slice(bf16[2048,1024]{1,0:T(8,128)(2,1)} %all-gather.2.cloned.1.call-done), slice={[0:2048], [512:1024]} | slice | bytes 4194304 | tf_op jit(solution)/shard_map/slice | solution.py:245
  129.3 2.1 %collective-permute-start.7 = (bf16[2048,512]{1,0:T(8,128)(2,1)}, bf16[2048,512]{1,0:T(8,128)(2,1)}, u32[]{:S(2)}, u32[]{:S(2)}) collective-permute-start(bf16[2048,512]{1,0:T(8,128)(2,1)} %slice.54), channel_id=1, source_target_pairs={{0,8},{8,0},{1,9},{9,1},{2,10},{10,2},{3,11},{11,3},{4,12},{12,4},... | collective-permute-start | bytes 6291464 | tf_op jit(solution)/shard_map/ppermute | solution.py:53
  132.1 2.4 %collective-permute-start.5 = (bf16[2048,256]{1,0:T(8,128)(2,1)S(1)}, bf16[2048,256]{1,0:T(8,128)(2,1)S(1)}, u32[]{:S(2)}, u32[]{:S(2)}) collective-permute-start(bf16[2048,256]{1,0:T(8,128)(2,1)S(1)} %bitcast.61), channel_id=1, source_target_pairs={{0,8},{8,0},{1,9},{9,1},{2,10},{10,2},{3,11},{11,3},{4,12},{12,4},... | collective-permute-start | bytes 3145736 | tf_op jit(solution)/shard_map/ppermute | solution.py:53
  135.9 3.1 %collective-permute-start.4 = (bf16[64,512]{1,0:T(8,128)(2,1)S(1)}, bf16[64,512]{1,0:T(8,128)(2,1)S(1)}, u32[]{:S(2)}, u32[]{:S(2)}) collective-permute-start(bf16[64,512]{1,0:T(8,128)(2,1)S(1)} %get-tuple-element.29), channel_id=1, source_target_pairs={{0,1},{1,0},{2,3},{3,2},{4,5},{5,4},{6,7},{7,6},{8,9},{9,8},{10,11... | collective-permute-start | bytes 196616 | tf_op jit(solution)/shard_map/ppermute | solution.py:57
  141.5 5.9 %attend.1 = bf16[512,128]{1,0:T(8,128)(2,1)S(1)} custom-call(bf16[512,128]{1,0:T(8,128)(2,1)S(1)} %reshape.297.q_ref, bf16[2048,256]{1,0:T(8,128)(2,1)S(1)} %bitcast.62, bf16[2048,256]{1,0:T(8,128)(2,1)S(1)} %collective-permute-done.5.far_ref, s32[512,1]{1,0:T(8,128)S(1)} %reshape.305.qpos_ref, s32[1,4096]{1,0:T(1,128)S(1)} %add.127.kpos_ref), custom_call_target="tpu_custom_call" | custom-call | tf_op jit(solution)/shard_map/attend/pallas_call | solution.py:125
  147.5 3.1 %collective-permute-start.6 = (bf16[64,512]{1,0:T(8,128)(2,1)S(1)}, bf16[64,512]{1,0:T(8,128)(2,1)S(1)}, u32[]{:S(2)}, u32[]{:S(2)}) collective-permute-start(bf16[64,512]{1,0:T(8,128)(2,1)S(1)} %squeeze.62), channel_id=1, source_target_pairs={{0,1},{1,0},{2,3},{3,2},{4,5},{5,4},{6,7},{7,6},{8,9},{9,8},{10,11... | collective-permute-start | bytes 196616 | tf_op jit(solution)/shard_map/ppermute | solution.py:57
  150.7 1.8 collective-permute-done.6
  152.5 2.3 %fusion.2 = bf16[8,128,256]{1,2,0:T(8,128)(2,1)S(1)} fusion(bf16[8,256,512]{2,1,0:T(8,128)(2,1)} %bitcast.13, bf16[64,512]{1,0:T(8,128)(2,1)S(1)} %get-tuple-element.43, bf16[64,512]{1,0:T(8,128)(2,1)S(1)} %get-tuple-element.42), kind=kOutput, calls=%fused_computation.4 | convolution fusion | flops 268959744 | bytes 2752512 | tf_op jit(solution)/shard_map/td,gnd->gtn/dot_general | solution.py:276
  154.8 2.3 %fusion.3 = bf16[8,128,256]{1,2,0:T(8,128)(2,1)S(1)} fusion(bf16[8,256,512]{2,1,0:T(8,128)(2,1)} %bitcast.22, bf16[64,512]{1,0:T(8,128)(2,1)S(1)} %get-tuple-element.43, bf16[64,512]{1,0:T(8,128)(2,1)S(1)} %get-tuple-element.42), kind=kOutput, calls=%fused_computation.5 | convolution fusion | flops 268959744 | bytes 2752512 | tf_op jit(solution)/shard_map/td,gnd->gtn/dot_general | solution.py:276
  158.3 5.6 %all-to-all-start.2 = ((bf16[8,128,512]{1,2,0:T(8,128)(2,1)}), bf16[8,128,512]{1,2,0:T(8,128)(2,1)S(1)}, u32[]{:S(2)}, u32[]{:S(2)}) async-start(bf16[8,128,512]{1,2,0:T(8,128)(2,1)} %pad_maximum_fusion.1), calls=%async_computation.3 | async-start | bytes 2097152 | tf_op jit(solution)/shard_map/all_to_all | solution.py:279
  164.9 10.5 %all-to-all-done.2 = bf16[8,128,512]{1,2,0:T(8,128)(2,1)S(1)} async-done(((bf16[8,128,512]{1,2,0:T(8,128)(2,1)}), bf16[8,128,512]{1,2,0:T(8,128)(2,1)S(1)}, u32[]{:S(2)}, u32[]{:S(2)}) %all-to-all-start.2) | async-done | bytes 1048608 | tf_op jit(solution)/shard_map/all_to_all | solution.py:279
  (89 shorter events, 17.4 us)
Async XLA Ops:
  8.0 68.8 %reduce-scatter.2.cloned.1.call-start = ((), (), s32[]{:S(2)}) async-start(), calls=%async_computation.5 | async-start | bytes 589824 | tf_op jit(solution)/shard_map/reduce_scatter | solution.py:219
  33.7 8.7 %copy-start.3 = (bf16[4096]{0:T(1024)(128)(2,1)S(1)}, bf16[4096]{0:T(1024)(128)(2,1)}, u32[]{:S(2)}) copy-start(bf16[4096]{0:T(1024)(128)(2,1)} %param.13) | copy-start | bytes 24580
  33.7 17.3 %copy-start.4 = (s32[2,64]{1,0:T(2,128)S(1)}, s32[2,64]{1,0:T(2,128)}, u32[]{:S(2)}) copy-start(s32[2,64]{1,0:T(2,128)} %param.19) | copy-start | bytes 1540
  33.7 87.3 %all-gather.2.cloned.1.call-start = ((), (), s32[]{:S(2)}) async-start(), calls=%async_computation.4 | async-start | bytes 4718592 | tf_op jit(solution)/shard_map/all_gather | solution.py:215
  35.5 22.5 %all-to-all-start = ((bf16[8,256,128]{2,1,0:T(8,128)(2,1)}), bf16[8,256,128]{2,1,0:T(8,128)(2,1)S(1)}, u32[]{:S(2)}, u32[]{:S(2)}) async-start(bf16[8,256,128]{2,1,0:T(8,128)(2,1)} %broadcast_in_dim.20), calls=%async_computation | async-start | bytes 1048576 | tf_op jit(solution)/shard_map/all_to_all | solution.py:49
  46.9 22.5 %copy-start = (bf16[128,2048]{1,0:T(8,128)(2,1)S(1)}, bf16[128,2048]{1,0:T(8,128)(2,1)}, u32[]{:S(2)}) copy-start(bf16[128,2048]{1,0:T(8,128)(2,1)} %get-tuple-element.20) | copy-start | bytes 1572868
  46.9 22.5 %collective-permute-start.2 = (bf16[128,2048]{1,0:T(8,128)(2,1)}, bf16[128,2048]{1,0:T(8,128)(2,1)S(1)}, u32[]{:S(2)}, u32[]{:S(2)}) collective-permute-start(bf16[128,2048]{1,0:T(8,128)(2,1)} %get-tuple-element.22), channel_id=1, source_target_pairs={{0,8},{8,0},{1,9},{9,1},{2,10},{10,2},{3,11},{11,3},{4,12},{12,4},... | collective-permute-start | bytes 1572872 | tf_op jit(solution)/shard_map/ppermute | solution.py:53
  58.0 6.5 %collective-permute-start = (bf16[2048,128]{1,0:T(8,128)(2,1)S(1)}, bf16[2048,128]{1,0:T(8,128)(2,1)S(1)}, u32[]{:S(2)}, u32[]{:S(2)}) collective-permute-start(bf16[2048,128]{1,0:T(8,128)(2,1)S(1)} %bitcast.63), channel_id=1, source_target_pairs={{0,8},{8,0},{1,9},{9,1},{2,10},{10,2},{3,11},{11,3},{4,12},{12,4},... | collective-permute-start | bytes 1572872 | tf_op jit(solution)/shard_map/ppermute | solution.py:53
  66.3 4.9 %collective-permute-start.1 = (bf16[64,128]{1,0:T(8,128)(2,1)S(1)}, bf16[64,128]{1,0:T(8,128)(2,1)S(1)}, u32[]{:S(2)}, u32[]{:S(2)}) collective-permute-start(bf16[64,128]{1,0:T(8,128)(2,1)S(1)} %get-tuple-element.51), channel_id=1, source_target_pairs={{0,1},{1,0},{2,3},{3,2},{4,5},{5,4},{6,7},{7,6},{8,9},{9,8},{10,11... | collective-permute-start | bytes 49160 | tf_op jit(solution)/shard_map/ppermute | solution.py:57
  72.3 59.8 %all-to-all-start.1 = ((bf16[32,64,256]{2,1,0:T(8,128)(2,1)}), bf16[32,64,256]{2,1,0:T(8,128)(2,1)S(1)}, u32[]{:S(2)}, u32[]{:S(2)}) async-start(bf16[32,64,256]{2,1,0:T(8,128)(2,1)} %broadcast_in_dim.24), calls=%async_computation.2 | async-start | bytes 2097152 | tf_op jit(solution)/shard_map/all_to_all | solution.py:49
  123.3 8.1 %collective-permute-start.3 = (f32[128,512]{1,0:T(8,128)S(1)}, f32[128,512]{1,0:T(8,128)S(1)}, u32[]{:S(2)}, u32[]{:S(2)}) collective-permute-start(f32[128,512]{1,0:T(8,128)S(1)} %slice.56), channel_id=1, source_target_pairs={{0,8},{8,0},{1,9},{9,1},{2,10},{10,2},{3,11},{11,3},{4,12},{12,4},... | collective-permute-start | bytes 786440 | tf_op jit(solution)/shard_map/ppermute | solution.py:53
  129.3 5.8 %copy-start.6 = (s32[2]{0:T(128)S(1)}, s32[2]{0:T(128)}, u32[]{:S(2)}) copy-start(s32[2]{0:T(128)} %param.18) | copy-start | bytes 28
  129.3 25.6 %collective-permute-start.7 = (bf16[2048,512]{1,0:T(8,128)(2,1)}, bf16[2048,512]{1,0:T(8,128)(2,1)}, u32[]{:S(2)}, u32[]{:S(2)}) collective-permute-start(bf16[2048,512]{1,0:T(8,128)(2,1)} %slice.54), channel_id=1, source_target_pairs={{0,8},{8,0},{1,9},{9,1},{2,10},{10,2},{3,11},{11,3},{4,12},{12,4},... | collective-permute-start | bytes 6291464 | tf_op jit(solution)/shard_map/ppermute | solution.py:53
  132.1 9.5 %collective-permute-start.5 = (bf16[2048,256]{1,0:T(8,128)(2,1)S(1)}, bf16[2048,256]{1,0:T(8,128)(2,1)S(1)}, u32[]{:S(2)}, u32[]{:S(2)}) collective-permute-start(bf16[2048,256]{1,0:T(8,128)(2,1)S(1)} %bitcast.61), channel_id=1, source_target_pairs={{0,8},{8,0},{1,9},{9,1},{2,10},{10,2},{3,11},{11,3},{4,12},{12,4},... | collective-permute-start | bytes 3145736 | tf_op jit(solution)/shard_map/ppermute | solution.py:53
  135.9 5.6 %collective-permute-start.4 = (bf16[64,512]{1,0:T(8,128)(2,1)S(1)}, bf16[64,512]{1,0:T(8,128)(2,1)S(1)}, u32[]{:S(2)}, u32[]{:S(2)}) collective-permute-start(bf16[64,512]{1,0:T(8,128)(2,1)S(1)} %get-tuple-element.29), channel_id=1, source_target_pairs={{0,1},{1,0},{2,3},{3,2},{4,5},{5,4},{6,7},{7,6},{8,9},{9,8},{10,11... | collective-permute-start | bytes 196616 | tf_op jit(solution)/shard_map/ppermute | solution.py:57
  147.5 5.0 %collective-permute-start.6 = (bf16[64,512]{1,0:T(8,128)(2,1)S(1)}, bf16[64,512]{1,0:T(8,128)(2,1)S(1)}, u32[]{:S(2)}, u32[]{:S(2)}) collective-permute-start(bf16[64,512]{1,0:T(8,128)(2,1)S(1)} %squeeze.62), channel_id=1, source_target_pairs={{0,1},{1,0},{2,3},{3,2},{4,5},{5,4},{6,7},{7,6},{8,9},{9,8},{10,11... | collective-permute-start | bytes 196616 | tf_op jit(solution)/shard_map/ppermute | solution.py:57
  157.2 6.7 %copy-start.5 = (s32[1,1,2]{2,1,0:T(1,128)S(1)}, s32[1,1,2]{2,1,0:T(1,128)}, u32[]{:S(2)}) copy-start(s32[1,1,2]{2,1,0:T(1,128)} %param.21) | copy-start | bytes 28
  157.2 6.8 %copy-start.1 = (bf16[1,1,16,16,1024]{4,3,2,1,0:T(8,128)(2,1)S(1)}, bf16[1,1,16,16,1024]{4,3,2,1,0:T(8,128)(2,1)}, u32[]{:S(2)}) copy-start(bf16[1,1,16,16,1024]{4,3,2,1,0:T(8,128)(2,1)} %param.20) | copy-start | bytes 1572868
  157.2 6.8 %copy-start.2 = (bf16[1,2,16,1024]{3,2,1,0:T(8,128)(2,1)S(1)}, bf16[1,2,16,1024]{3,2,1,0:T(8,128)(2,1)}, u32[]{:S(2)}) copy-start(bf16[1,2,16,1024]{3,2,1,0:T(8,128)(2,1)} %reduce-scatter.2.cloned.1.call-done) | copy-start | bytes 196612
  158.3 17.1 %all-to-all-start.2 = ((bf16[8,128,512]{1,2,0:T(8,128)(2,1)}), bf16[8,128,512]{1,2,0:T(8,128)(2,1)S(1)}, u32[]{:S(2)}, u32[]{:S(2)}) async-start(bf16[8,128,512]{1,2,0:T(8,128)(2,1)} %pad_maximum_fusion.1), calls=%async_computation.3 | async-start | bytes 2097152 | tf_op jit(solution)/shard_map/all_to_all | solution.py:279
Sparse Core Ops, SparseCore 0:
  33.8 41.1 reduce-scatter.1
Sparse Core Ops, SparseCore 1:
  36.8 84.1 all-gather.1

commit v6 on v4

--- a/solution.py
+++ b/solution.py
@@ -12,8 +12,8 @@
 HEADS_PER_KV = 8
 
 CTX = ("y", "zh", "core")
-REP = ("zl", "x")
-CHIPS = ("y", "zh")
+REP = ("zl", "xh", "xe")
+SOURCES = ("y", "zh", "xe")
 
 rope_base = 5000000.0
 neg_fill = -1e30
@@ -43,10 +43,8 @@
     return jnp.dot(left, right, preferred_element_type=jnp.float32)
 
 
-def spread(block, axes):
-    size = lax.axis_size(axes)
-    copies = jnp.broadcast_to(block[None], (size,) + block.shape)
-    return lax.all_to_all(copies, axes, split_axis=0, concat_axis=0, tiled=True)
+def exchange(blocks, axes):
+    return lax.all_to_all(blocks, axes, split_axis=0, concat_axis=0, tiled=True)
 
 
 def swap_core(value):
@@ -54,7 +52,7 @@
 
 
 def swap_x(value):
-    return lax.ppermute(value, "x", [(i, i ^ 1) for i in range(lax.axis_size("x"))])
+    return lax.ppermute(value, "xe", [(0, 1), (1, 0)])
 
 
 def norm_kernel(core_ref, hidden_ref, gain_ref, near_ref, far_ref):
@@ -93,12 +91,12 @@
 
 
 def attend_kernel(q_ref, near_ref, far_ref, qpos_ref, kpos_ref, out_ref):
-    half = near_ref.shape[0]
+    half = near_ref.shape[0] * near_ref.shape[2]
     queries = q_ref[...]
     scores = []
     masks = []
     for part, ref in enumerate((near_ref, far_ref)):
-        keys = ref[:, :HEAD_SIZE]
+        keys = ref[:, 0].reshape(half, HEAD_SIZE)
         raw = lax.dot_general(
             queries, keys, (((1,), (1,)), ((), ())), preferred_element_type=jnp.float32
         )
@@ -115,20 +113,20 @@
     for raw, allowed, ref in zip(scores, masks, (near_ref, far_ref)):
         weights = jnp.where(allowed, jnp.exp(raw - top), 0.0)
         total = total + jnp.sum(weights, axis=-1, keepdims=True)
-        acc = acc + matmul(weights.astype(jnp.bfloat16), ref[:, HEAD_SIZE:])
+        acc = acc + matmul(weights.astype(jnp.bfloat16), ref[:, 1].reshape(half, HEAD_SIZE))
     out_ref[...] = (acc / jnp.maximum(total, 1.0)).astype(jnp.bfloat16)
 
 
 def attend(queries, near, far, qpos, kpos):
-    rows, half = queries.shape[0], near.shape[0]
+    rows, half = queries.shape[0], near.shape[0] * near.shape[2]
     tile = min(rows, 128)
     return pl.pallas_call(
         attend_kernel,
         grid=(rows // tile,),
         in_specs=[
             pl.BlockSpec((tile, HEAD_SIZE), lambda i: (i, 0)),
-            pl.BlockSpec((half, 2 * HEAD_SIZE), lambda i: (0, 0)),
-            pl.BlockSpec((half, 2 * HEAD_SIZE), lambda i: (0, 0)),
+            pl.BlockSpec(near.shape, lambda i: (0, 0, 0, 0)),
+            pl.BlockSpec(far.shape, lambda i: (0, 0, 0, 0)),
             pl.BlockSpec((tile, 1), lambda i: (i, 0)),
             pl.BlockSpec((1, 2 * half), lambda i: (0, 0)),
         ],
@@ -196,7 +194,7 @@
     rank = lax.axis_index(REP)
     core = lax.axis_index("core")
     rows_y, rows_z = lax.axis_size("y"), lax.axis_size("zh")
-    mine = lax.axis_index("x") % 2
+    mine = lax.axis_index("xe")
     blk = hidden_in.shape[3]
     span = 2 * blk
     width = hidden_in.shape[4]
@@ -212,7 +210,9 @@
     weights, leave = lax.optimization_barrier((weights, move_page))
     cols = w_query.shape[1]
     wq_near, wo_near = weights[:, :cols], weights[:, cols : 2 * cols]
-    half_near = spread(weights[:, 2 * cols :], "y").reshape(-1, HEAD_SIZE)
+    half_near = weights[:, 2 * cols :]
+    half_near = exchange(jnp.broadcast_to(half_near[None], (rows_y,) + half_near.shape), "y")
+    half_near = half_near.reshape(-1, HEAD_SIZE)
     wq_near = lax.all_gather(wq_near, "y", axis=0, tiled=True)
 
     x_near, x_far = split_norm(hidden_in.reshape(2 * span, width), norm_gain, core)
@@ -234,16 +234,12 @@
     half = matmul(x_near, half_near) + matmul(x_far, half_far)
     keys = apply_rotation(half[:, None, :], cosine_table, sine_table)[:, 0]
     half = jnp.where(mine == 0, keys, half).astype(jnp.bfloat16).reshape(2, span, HEAD_SIZE)
-    kept = lax.dynamic_index_in_dim(half, mine, 0, False)
-    other = swap_x(lax.dynamic_index_in_dim(half, 1 - mine, 0, False))
-    kv = jnp.where(
-        mine == 0,
-        jnp.concatenate([kept, other], axis=1),
-        jnp.concatenate([other, kept], axis=1),
-    )
-    kv, x_chip = lax.optimization_barrier((kv, x_chip))
-    near = spread(kv, CHIPS).reshape(-1, 2 * HEAD_SIZE)
-    wq_near, arrived = lax.optimization_barrier((wq_near, arrived))
+    half, x_chip = lax.optimization_barrier((half, x_chip))
+    chips = rows_y * rows_z
+    blocks = jnp.broadcast_to(half[None], (chips,) + half.shape)
+    near = exchange(blocks.reshape(2 * chips, span, HEAD_SIZE), SOURCES)
+    near = near.reshape(chips, 2, span, HEAD_SIZE)
+
     query = matmul(x_chip, wq_near)
     query = query[: 2 * span] + swap_core(query[2 * span :])
     query = apply_rotation(
@@ -261,7 +257,7 @@
     my_len = lax.dynamic_index_in_dim(prompt_len, mine, 0, False)
     my_qpos = jnp.where(my_qpos < my_len, my_qpos, -1)
     all_q = jnp.stack([q_mine, q_pair]).reshape(-1, HEAD_SIZE)
-    near, all_q = lax.optimization_barrier((near, all_q))
+    near, all_q, arrived = lax.optimization_barrier((near, all_q, arrived))
     far = swap_core(near)
     all_qpos = jnp.broadcast_to(my_qpos[None, :, None], (2, span, heads_here)).reshape(-1, 1)
     context = attend(all_q, near, far, all_qpos, kpos).reshape(2, span, heads_here * HEAD_SIZE)
@@ -291,7 +287,7 @@
 
 def solution(mesh):
     ctx, rep = mesh.devices.shape
-    fine = Mesh(mesh.devices.reshape(rep, ctx // rep // 2, 2, 2, rep // 2), CTX + REP)
+    fine = Mesh(mesh.devices.reshape(rep, ctx // rep // 2, 2, 2, rep // 4, 2), CTX + REP)
     return jax.shard_map(
         on_device,
         mesh=fine,

time: 170 us -> 168 us (0.988)
  matrix products: 8.48 us -> 6.37 us
  waiting for transfers between devices: 39.7 us -> 38 us
    all_to_all x2, waiting for transfers between devices: 16.6 us -> 5.55 us  [exchange(): return lax.all_to_all(blocks, axes, split_axis=0, concat_axis=0, tiled=True)]
    ppermute x6, starting transfers between devices: 30.6 us -> 39.5 us  [swap_core(): return lax.ppermute(value, 'core', [(0, 1), (1, 0)])]
    all_gather x1, waiting for transfers between devices: 0.63 us -> 8.53 us  [on_device(): wq_near = lax.all_gather(wq_near, 'y', axis=0, tiled=True)]
    all_gather x1, waiting for transfers between devices: 0.03 us -> 5.63 us  [on_device(): wo_near = lax.all_gather(wo_near, 'y', axis=0, tiled=True)]
    ppermute x3 -> x2, starting transfers between devices: 9.54 us -> 4.16 us  [swap_x(): return lax.ppermute(value, 'xe', [(0, 1), (1, 0)])]
    all_to_all x1, waiting for transfers between devices: 14.8 us -> 9.38 us  [on_device(): terms = lax.all_to_all(send, REP, split_axis=0, concat_axis=0, tiled=True)]
    all_to_all x1, starting transfers between devices: 7.75 us -> 5.07 us  [on_device(): terms = lax.all_to_all(send, REP, split_axis=0, concat_axis=0, tiled=True)]
    dot_general x3, matrix products: 5.1 us -> 2.99 us  [matmul(): return jnp.dot(left, right, preferred_element_type=jnp.float32)]
  transfers between devices with their start and end apart: 15 -> 14, of which waited for: 10 -> 9; matrix products, arithmetic and copies ran while one was open for 8% -> 7% of each run, Pallas kernels for 6% -> 7%
where the time goes in v6:
time: 168 us
  starting transfers between devices  60.3 us (36%)
  waiting for transfers between devices  38 us (23%)
  blocking collectives  22 us (13%)
  between operations  16 us (10%)
  Pallas kernels  11.7 us (7%)
  local copies, waits for them, and re-layouts  6.86 us (4%)
  matrix products  6.37 us (4%)
  other arithmetic  6.32 us (4%)
    ppermute x6, starting transfers between devices, swap_core(): return lax.ppermute(value, 'core', [(0, 1), (1, 0)])  39.5 us
    all_gather x1, blocking collectives, on_device(): weights = lax.all_gather(weights, 'zh', axis=0, tiled=True)  22 us
    all_to_all x2, starting transfers between devices, exchange(): return lax.all_to_all(blocks, axes, split_axis=0, concat_axis=0, tiled=True)  11.5 us
    all_to_all x1, waiting for transfers between devices, on_device(): terms = lax.all_to_all(send, REP, split_axis=0, concat_axis=0, tiled=True)  9.38 us
    all_gather x1, waiting for transfers between devices, on_device(): wq_near = lax.all_gather(wq_near, 'y', axis=0, tiled=True)  8.53 us
    pallas_call x1, Pallas kernels, attend(): pl.pallas_call(attend_kernel, grid=(rows // tile,), in_specs=[pl.BlockSpe...  5.9 us
    ppermute x2, waiting for transfers between devices, swap_x(): return lax.ppermute(value, 'xe', [(0, 1), (1, 0)])  5.72 us
    all_gather x1, waiting for transfers between devices, on_device(): wo_near = lax.all_gather(wo_near, 'y', axis=0, tiled=True)  5.63 us
  transfers between devices with their start and end apart: 14, of which 9 were waited for; matrix products, arithmetic and copies ran while one was open for 7% of the time, Pallas kernels for 7%

profile of v6, /device:TPU:1, one launch (start us, length us, event | category | flops | bytes accessed | tf_op | source)
XLA Modules:
  0.0 167.6 jit_solution(18354148904551863143)
XLA Ops:
  9.7 22.0 %all_gather.9 = bf16[256,1152]{1,0:T(8,128)(2,1)S(1)} all-gather(bf16[64,1152]{1,0:T(8,128)(2,1)S(1)} %pad_maximum_fusion.2), channel_id=1, replica_groups=mesh['y'=8,'zh'=4,'core'=2,'zl'=2,'xh'=2,'xe'=2] {'zh'}, dimensions={0}, use_global_device_ids=true | all-gather | bytes 737280 | tf_op jit(solution)/shard_map/all_gather | solution.py:209
  33.5 6.8 %all-to-all-start = ((bf16[8,256,128]{2,1,0:T(8,128)(2,1)}), bf16[8,256,128]{2,1,0:T(8,128)(2,1)S(1)}, u32[]{:S(2)}, u32[]{:S(2)}) async-start(bf16[8,256,128]{2,1,0:T(8,128)(2,1)} %broadcast_in_dim.20), calls=%async_computation | async-start | bytes 1048576 | tf_op jit(solution)/shard_map/all_to_all | solution.py:47
  41.0 3.9 %split_norm.1 = (bf16[128,2048]{1,0:T(8,128)(2,1)}, bf16[128,2048]{1,0:T(8,128)(2,1)}) custom-call(s32[1]{0:T(128)} %bitcast.2.core_ref, bf16[128,4096]{1,0:T(8,128)(2,1)} %bitcast.56, bf16[1,4096]{1,0:T(2,128)(2,1)} %broadcast_in_dim.21.gain_ref), custom_call_target="tpu_custom_call" | custom-call | tf_op jit(solution)/shard_map/split_norm/pallas_call | solution.py:79
  44.9 4.1 %collective-permute-start.1 = (bf16[128,2048]{1,0:T(8,128)(2,1)}, bf16[128,2048]{1,0:T(8,128)(2,1)}, u32[]{:S(2)}, u32[]{:S(2)}) collective-permute-start(bf16[128,2048]{1,0:T(8,128)(2,1)} %get-tuple-element.22), channel_id=1, source_target_pairs={{0,8},{8,0},{1,9},{9,1},{2,10},{10,2},{3,11},{11,3},{4,12},{12,4},... | collective-permute-start | bytes 1572872 | tf_op jit(solution)/shard_map/ppermute | solution.py:51
  49.0 1.9 %pages_to_send.1 = bf16[8,2,16,1024]{3,2,1,0:T(8,128)(2,1)} custom-call(s32[2]{0:T(128)} %bitcast.67, s32[2]{0:T(128)} %bitcast.65, s32[2]{0:T(128)} %bitcast.66, bf16[16,16,1024]{2,1,0:T(8,128)(2,1)} %bitcast.54), custom_call_target="tpu_custom_call" | custom-call | tf_op jit(solution)/shard_map/pages_to_send/pallas_call | solution.py:158
  51.2 5.5 %all-to-all-done = bf16[8,256,128]{2,1,0:T(8,128)(2,1)S(1)} async-done(((bf16[8,256,128]{2,1,0:T(8,128)(2,1)}), bf16[8,256,128]{2,1,0:T(8,128)(2,1)S(1)}, u32[]{:S(2)}, u32[]{:S(2)}) %all-to-all-start) | async-done | bytes 524320 | tf_op jit(solution)/shard_map/all_to_all | solution.py:47
  56.8 7.5 %collective-permute-start = (bf16[2048,128]{1,0:T(8,128)(2,1)S(1)}, bf16[2048,128]{1,0:T(8,128)(2,1)S(1)}, u32[]{:S(2)}, u32[]{:S(2)}) collective-permute-start(bf16[2048,128]{1,0:T(8,128)(2,1)S(1)} %bitcast.51), channel_id=1, source_target_pairs={{0,8},{8,0},{1,9},{9,1},{2,10},{10,2},{3,11},{11,3},{4,12},{12,4},... | collective-permute-start | bytes 1572872 | tf_op jit(solution)/shard_map/ppermute | solution.py:51
  64.4 1.3 pad_maximum_fusion
  68.0 4.7 %all-to-all-start.1 = ((bf16[64,64,128]{2,1,0:T(8,128)(2,1)}), bf16[64,64,128]{2,1,0:T(8,128)(2,1)S(1)}, u32[]{:S(2)}, u32[]{:S(2)}) async-start(bf16[64,64,128]{2,1,0:T(8,128)(2,1)} %bitcast.7), calls=%async_computation.1 | async-start | bytes 2097152 | tf_op jit(solution)/shard_map/all_to_all | solution.py:47
  73.5 8.5 %all-gather.3.cloned.1.call-done = bf16[2048,512]{1,0:T(8,128)(2,1)} async-done(((bf16[256,512]{1,0:T(8,128)(2,1)}), bf16[2048,512]{1,0:T(8,128)(2,1)}) %all-gather.3.cloned.1.call-update) | async-done | bytes 2097168 | tf_op jit(solution)/shard_map/all_gather | solution.py:216
  82.0 2.3 %fusion.15 = f32[256,512]{1,0:T(8,128)S(1)} fusion(bf16[256,2048]{1,0:T(8,128)(2,1)S(1)} %pad_maximum_fusion, bf16[2048,512]{1,0:T(8,128)(2,1)} %all-gather.3.cloned.1.call-done), kind=kOutput, calls=%fused_computation.55 | convolution fusion | flops 536870912 | bytes 3670016 | tf_op jit(solution)/shard_map/dot_general | solution.py:43
  84.3 13.2 %collective-permute-start.2 = (f32[128,512]{1,0:T(8,128)S(1)}, f32[128,512]{1,0:T(8,128)S(1)}, u32[]{:S(2)}, u32[]{:S(2)}) collective-permute-start(f32[128,512]{1,0:T(8,128)S(1)} %slice.61), channel_id=1, source_target_pairs={{0,8},{8,0},{1,9},{9,1},{2,10},{10,2},{3,11},{11,3},{4,12},{12,4},... | collective-permute-start | bytes 786440 | tf_op jit(solution)/shard_map/ppermute | solution.py:51
  99.4 2.2 %collective-permute-start.3 = (bf16[64,512]{1,0:T(8,128)(2,1)S(1)}, bf16[64,512]{1,0:T(8,128)(2,1)S(1)}, u32[]{:S(2)}, u32[]{:S(2)}) collective-permute-start(bf16[64,512]{1,0:T(8,128)(2,1)S(1)} %get-tuple-element.49), channel_id=1, source_target_pairs={{0,1},{1,0},{2,3},{3,2},{4,5},{5,4},{6,7},{7,6},{8,9},{9,8},{10,11... | collective-permute-start | bytes 196616 | tf_op jit(solution)/shard_map/ppermute | solution.py:55
  102.5 2.3 %collective-permute-done.3 = bf16[64,512]{1,0:T(8,128)(2,1)S(1)} collective-permute-done((bf16[64,512]{1,0:T(8,128)(2,1)S(1)}, bf16[64,512]{1,0:T(8,128)(2,1)S(1)}, u32[]{:S(2)}, u32[]{:S(2)}) %collective-permute-start.3) | collective-permute-done | bytes 65568 | tf_op jit(solution)/shard_map/ppermute | solution.py:55
  105.0 3.6 %collective-permute-start.4 = (bf16[32,2,64,128]{3,2,1,0:T(8,128)(2,1)S(1)}, bf16[32,2,64,128]{3,2,1,0:T(8,128)(2,1)S(1)}, u32[]{:S(2)}, u32[]{:S(2)}) collective-permute-start(bf16[32,2,64,128]{3,2,1,0:T(8,128)(2,1)S(1)} %bitcast.49), channel_id=1, source_target_pairs={{0,8},{8,0},{1,9},{9,1},{2,10},{10,2},{3,11},{11,3},{4,12},{12,4},... | collective-permute-start | bytes 3145736 | tf_op jit(solution)/shard_map/ppermute | solution.py:51
  110.8 5.9 %attend.1 = bf16[512,128]{1,0:T(8,128)(2,1)S(1)} custom-call(bf16[512,128]{1,0:T(8,128)(2,1)S(1)} %reshape.296.q_ref, bf16[32,2,64,128]{3,2,1,0:T(8,128)(2,1)S(1)} %bitcast.50, bf16[32,2,64,128]{3,2,1,0:T(8,128)(2,1)S(1)} %collective-permute-done.4.far_ref, s32[512,1]{1,0:T(8,128)S(1)} %reshape.303.qpos_ref, s32[1,4096]{1,0:T(1,128)S(1)} %add.123.kpos_ref), custom_call_target="tpu_custom_call" | custom-call | tf_op jit(solution)/shard_map/attend/pallas_call | solution.py:123
  116.8 1.9 %collective-permute-start.5 = (bf16[64,512]{1,0:T(8,128)(2,1)S(1)}, bf16[64,512]{1,0:T(8,128)(2,1)S(1)}, u32[]{:S(2)}, u32[]{:S(2)}) collective-permute-start(bf16[64,512]{1,0:T(8,128)(2,1)S(1)} %squeeze.49), channel_id=1, source_target_pairs={{0,1},{1,0},{2,3},{3,2},{4,5},{5,4},{6,7},{7,6},{8,9},{9,8},{10,11... | collective-permute-start | bytes 196616 | tf_op jit(solution)/shard_map/ppermute | solution.py:55
  118.8 3.4 %collective-permute-done.5 = bf16[64,512]{1,0:T(8,128)(2,1)S(1)} collective-permute-done((bf16[64,512]{1,0:T(8,128)(2,1)S(1)}, bf16[64,512]{1,0:T(8,128)(2,1)S(1)}, u32[]{:S(2)}, u32[]{:S(2)}) %collective-permute-start.5) | collective-permute-done | bytes 65568 | tf_op jit(solution)/shard_map/ppermute | solution.py:55
  122.2 3.0 %collective-permute-start.6 = (bf16[128,512]{1,0:T(8,128)(2,1)S(1)}, bf16[128,512]{1,0:T(8,128)(2,1)S(1)}, u32[]{:S(2)}, u32[]{:S(2)}) collective-permute-start(bf16[128,512]{1,0:T(8,128)(2,1)S(1)} %pad_maximum_fusion.5), channel_id=1, source_target_pairs={{0,8},{8,0},{1,9},{9,1},{2,10},{10,2},{3,11},{11,3},{4,12},{12,4},... | collective-permute-start | bytes 393224 | tf_op jit(solution)/shard_map/ppermute | solution.py:51
  126.3 5.6 %all-gather.5.cloned.1.call-done = bf16[2048,512]{1,0:T(8,128)(2,1)} async-done(((bf16[256,512]{1,0:T(8,128)(2,1)}), bf16[2048,512]{1,0:T(8,128)(2,1)}) %all-gather.5.cloned.1.call-update) | async-done | bytes 2097168 | tf_op jit(solution)/shard_map/all_gather | solution.py:225
  131.9 3.4 %fusion = bf16[8,256,256]{1,2,0:T(8,128)(2,1)} fusion(bf16[8,256,512]{2,1,0:T(8,128)(2,1)} %bitcast.53, bf16[256,512]{1,0:T(8,128)(2,1)S(1)} %pad_maximum_fusion.1), kind=kOutput, calls=%fused_computation.1 | convolution fusion | flops 537395200 | bytes 3407872 | tf_op jit(solution)/shard_map/td,gnd->gtn/dot_general | solution.py:271
  135.3 5.1 %all-to-all-start.2 = ((bf16[8,256,256]{1,2,0:T(8,128)(2,1)}), bf16[8,256,256]{1,2,0:T(8,128)(2,1)S(1)}, u32[]{:S(2)}, u32[]{:S(2)}) async-start(bf16[8,256,256]{1,2,0:T(8,128)(2,1)} %fusion), calls=%async_computation.3 | async-start | bytes 2097152 | tf_op jit(solution)/shard_map/all_to_all | solution.py:277
  140.6 9.4 %all-to-all-done.2 = bf16[8,256,256]{1,2,0:T(8,128)(2,1)S(1)} async-done(((bf16[8,256,256]{1,2,0:T(8,128)(2,1)}), bf16[8,256,256]{1,2,0:T(8,128)(2,1)S(1)}, u32[]{:S(2)}, u32[]{:S(2)}) %all-to-all-start.2) | async-done | bytes 1048608 | tf_op jit(solution)/shard_map/all_to_all | solution.py:277
  150.1 8.1 %collective-permute-start.7 = (bf16[128,256]{0,1:T(8,128)(2,1)S(1)}, bf16[128,256]{0,1:T(8,128)(2,1)S(1)}, u32[]{:S(2)}, u32[]{:S(2)}) collective-permute-start(bf16[128,256]{0,1:T(8,128)(2,1)S(1)} %slice.67), channel_id=1, source_target_pairs={{0,8},{8,0},{1,9},{9,1},{2,10},{10,2},{3,11},{11,3},{4,12},{12,4},... | collective-permute-start | bytes 196616 | tf_op jit(solution)/shard_map/ppermute | solution.py:51
  (92 shorter events, 15.9 us)
Async XLA Ops:
  8.0 74.0 %all-gather.3.cloned.1.call-start = ((), (), s32[]{:S(2)}) async-start(), calls=%async_computation.4 | async-start | bytes 2359296 | tf_op jit(solution)/shard_map/all_gather | solution.py:216
  8.1 32.3 %copy-start.4 = (bf16[4096]{0:T(1024)(128)(2,1)S(1)}, bf16[4096]{0:T(1024)(128)(2,1)}, u32[]{:S(2)}) copy-start(bf16[4096]{0:T(1024)(128)(2,1)} %param.13) | copy-start | bytes 24580
  32.6 18.3 %copy-start.5 = (s32[2,64]{1,0:T(2,128)S(1)}, s32[2,64]{1,0:T(2,128)}, u32[]{:S(2)}) copy-start(s32[2,64]{1,0:T(2,128)} %param.19) | copy-start | bytes 1540
  33.5 23.3 %all-to-all-start = ((bf16[8,256,128]{2,1,0:T(8,128)(2,1)}), bf16[8,256,128]{2,1,0:T(8,128)(2,1)S(1)}, u32[]{:S(2)}, u32[]{:S(2)}) async-start(bf16[8,256,128]{2,1,0:T(8,128)(2,1)} %broadcast_in_dim.20), calls=%async_computation | async-start | bytes 1048576 | tf_op jit(solution)/shard_map/all_to_all | solution.py:47
  40.3 64.6 %reduce-scatter.2.cloned.1.call-start = ((), (), s32[]{:S(2)}) async-start(), calls=%async_computation.5 | async-start | bytes 589824 | tf_op jit(solution)/shard_map/reduce_scatter | solution.py:220
  44.9 20.8 %copy-start = (bf16[128,2048]{1,0:T(8,128)(2,1)S(1)}, bf16[128,2048]{1,0:T(8,128)(2,1)}, u32[]{:S(2)}) copy-start(bf16[128,2048]{1,0:T(8,128)(2,1)} %get-tuple-element.20) | copy-start | bytes 1572868
  44.9 19.5 %collective-permute-start.1 = (bf16[128,2048]{1,0:T(8,128)(2,1)}, bf16[128,2048]{1,0:T(8,128)(2,1)}, u32[]{:S(2)}, u32[]{:S(2)}) collective-permute-start(bf16[128,2048]{1,0:T(8,128)(2,1)} %get-tuple-element.22), channel_id=1, source_target_pairs={{0,8},{8,0},{1,9},{9,1},{2,10},{10,2},{3,11},{11,3},{4,12},{12,4},... | collective-permute-start | bytes 1572872 | tf_op jit(solution)/shard_map/ppermute | solution.py:51
  50.9 15.1 %copy-start.2 = (bf16[128,2048]{1,0:T(8,128)(2,1)S(1)}, bf16[128,2048]{1,0:T(8,128)(2,1)}, u32[]{:S(2)}) copy-start(bf16[128,2048]{1,0:T(8,128)(2,1)} %get-tuple-element.22) | copy-start | bytes 1572868
  56.8 9.3 %collective-permute-start = (bf16[2048,128]{1,0:T(8,128)(2,1)S(1)}, bf16[2048,128]{1,0:T(8,128)(2,1)S(1)}, u32[]{:S(2)}, u32[]{:S(2)}) collective-permute-start(bf16[2048,128]{1,0:T(8,128)(2,1)S(1)} %bitcast.51), channel_id=1, source_target_pairs={{0,8},{8,0},{1,9},{9,1},{2,10},{10,2},{3,11},{11,3},{4,12},{12,4},... | collective-permute-start | bytes 1572872 | tf_op jit(solution)/shard_map/ppermute | solution.py:51
  68.0 36.9 %all-to-all-start.1 = ((bf16[64,64,128]{2,1,0:T(8,128)(2,1)}), bf16[64,64,128]{2,1,0:T(8,128)(2,1)S(1)}, u32[]{:S(2)}, u32[]{:S(2)}) async-start(bf16[64,64,128]{2,1,0:T(8,128)(2,1)} %bitcast.7), calls=%async_computation.1 | async-start | bytes 2097152 | tf_op jit(solution)/shard_map/all_to_all | solution.py:47
  72.7 59.2 %all-gather.5.cloned.1.call-start = ((), (), s32[]{:S(2)}) async-start(), calls=%async_computation.6 | async-start | bytes 2359296 | tf_op jit(solution)/shard_map/all_gather | solution.py:225
  84.3 17.6 %copy-start.7 = (s32[2]{0:T(128)S(1)}, s32[2]{0:T(128)}, u32[]{:S(2)}) copy-start(s32[2]{0:T(128)} %param.18) | copy-start | bytes 28
  84.3 14.3 %collective-permute-start.2 = (f32[128,512]{1,0:T(8,128)S(1)}, f32[128,512]{1,0:T(8,128)S(1)}, u32[]{:S(2)}, u32[]{:S(2)}) collective-permute-start(f32[128,512]{1,0:T(8,128)S(1)} %slice.61), channel_id=1, source_target_pairs={{0,8},{8,0},{1,9},{9,1},{2,10},{10,2},{3,11},{11,3},{4,12},{12,4},... | collective-permute-start | bytes 786440 | tf_op jit(solution)/shard_map/ppermute | solution.py:51
  99.4 5.4 %collective-permute-start.3 = (bf16[64,512]{1,0:T(8,128)(2,1)S(1)}, bf16[64,512]{1,0:T(8,128)(2,1)S(1)}, u32[]{:S(2)}, u32[]{:S(2)}) collective-permute-start(bf16[64,512]{1,0:T(8,128)(2,1)S(1)} %get-tuple-element.49), channel_id=1, source_target_pairs={{0,1},{1,0},{2,3},{3,2},{4,5},{5,4},{6,7},{7,6},{8,9},{9,8},{10,11... | collective-permute-start | bytes 196616 | tf_op jit(solution)/shard_map/ppermute | solution.py:55
  105.0 5.8 %collective-permute-start.4 = (bf16[32,2,64,128]{3,2,1,0:T(8,128)(2,1)S(1)}, bf16[32,2,64,128]{3,2,1,0:T(8,128)(2,1)S(1)}, u32[]{:S(2)}, u32[]{:S(2)}) collective-permute-start(bf16[32,2,64,128]{3,2,1,0:T(8,128)(2,1)S(1)} %bitcast.49), channel_id=1, source_target_pairs={{0,8},{8,0},{1,9},{9,1},{2,10},{10,2},{3,11},{11,3},{4,12},{12,4},... | collective-permute-start | bytes 3145736 | tf_op jit(solution)/shard_map/ppermute | solution.py:51
  116.8 5.4 %collective-permute-start.5 = (bf16[64,512]{1,0:T(8,128)(2,1)S(1)}, bf16[64,512]{1,0:T(8,128)(2,1)S(1)}, u32[]{:S(2)}, u32[]{:S(2)}) collective-permute-start(bf16[64,512]{1,0:T(8,128)(2,1)S(1)} %squeeze.49), channel_id=1, source_target_pairs={{0,1},{1,0},{2,3},{3,2},{4,5},{5,4},{6,7},{7,6},{8,9},{9,8},{10,11... | collective-permute-start | bytes 196616 | tf_op jit(solution)/shard_map/ppermute | solution.py:55
  122.2 4.0 %collective-permute-start.6 = (bf16[128,512]{1,0:T(8,128)(2,1)S(1)}, bf16[128,512]{1,0:T(8,128)(2,1)S(1)}, u32[]{:S(2)}, u32[]{:S(2)}) collective-permute-start(bf16[128,512]{1,0:T(8,128)(2,1)S(1)} %pad_maximum_fusion.5), channel_id=1, source_target_pairs={{0,8},{8,0},{1,9},{9,1},{2,10},{10,2},{3,11},{11,3},{4,12},{12,4},... | collective-permute-start | bytes 393224 | tf_op jit(solution)/shard_map/ppermute | solution.py:51
  131.9 8.5 %copy-start.6 = (s32[1,1,2]{2,1,0:T(1,128)S(1)}, s32[1,1,2]{2,1,0:T(1,128)}, u32[]{:S(2)}) copy-start(s32[1,1,2]{2,1,0:T(1,128)} %param.21) | copy-start | bytes 28
  131.9 8.6 %copy-start.1 = (bf16[1,1,16,16,1024]{4,3,2,1,0:T(8,128)(2,1)S(1)}, bf16[1,1,16,16,1024]{4,3,2,1,0:T(8,128)(2,1)}, u32[]{:S(2)}) copy-start(bf16[1,1,16,16,1024]{4,3,2,1,0:T(8,128)(2,1)} %param.20) | copy-start | bytes 1572868
  135.3 22.9 %copy-start.3 = (bf16[1,2,16,1024]{3,2,1,0:T(8,128)(2,1)S(1)}, bf16[1,2,16,1024]{3,2,1,0:T(8,128)(2,1)}, u32[]{:S(2)}) copy-start(bf16[1,2,16,1024]{3,2,1,0:T(8,128)(2,1)} %reduce-scatter.2.cloned.1.call-done) | copy-start | bytes 196612
  135.3 14.7 %all-to-all-start.2 = ((bf16[8,256,256]{1,2,0:T(8,128)(2,1)}), bf16[8,256,256]{1,2,0:T(8,128)(2,1)S(1)}, u32[]{:S(2)}, u32[]{:S(2)}) async-start(bf16[8,256,256]{1,2,0:T(8,128)(2,1)} %fusion), calls=%async_computation.3 | async-start | bytes 2097152 | tf_op jit(solution)/shard_map/all_to_all | solution.py:277
  150.1 9.0 %collective-permute-start.7 = (bf16[128,256]{0,1:T(8,128)(2,1)S(1)}, bf16[128,256]{0,1:T(8,128)(2,1)S(1)}, u32[]{:S(2)}, u32[]{:S(2)}) collective-permute-start(bf16[128,256]{0,1:T(8,128)(2,1)S(1)} %slice.67), channel_id=1, source_target_pairs={{0,8},{8,0},{1,9},{9,1},{2,10},{10,2},{3,11},{11,3},{4,12},{12,4},... | collective-permute-start | bytes 196616 | tf_op jit(solution)/shard_map/ppermute | solution.py:51
Sparse Core Ops, SparseCore 0:
  32.7 49.2 all-gather.2
  84.1 47.7 all-gather.4
Sparse Core Ops, SparseCore 1:
  51.0 43.4 reduce-scatter.1

commit v7 on v4

--- a/solution.py
+++ b/solution.py
@@ -88,6 +88,7 @@
         ],
         out_specs=(half_spec, half_spec),
         out_shape=(half, half),
+        compiler_params=pltpu.CompilerParams(vmem_limit_bytes=12 << 20),
         name="split_norm",
     )(core.reshape(1), hidden, gain[None])
 
@@ -139,6 +140,60 @@
     )(queries, near, far, qpos, kpos)
 
 
+def project_kernel(context_ref, weight_ref, out_ref):
+    out_ref[0] = lax.dot_general(
+        context_ref[...],
+        weight_ref[...],
+        (((1,), (1,)), ((), ())),
+        preferred_element_type=jnp.float32,
+    ).astype(jnp.bfloat16)
+
+
+def project(context, weight, groups):
+    rows, width = context.shape
+    cols = weight.shape[0] // groups
+    return pl.pallas_call(
+        project_kernel,
+        grid=(groups,),
+        in_specs=[
+            pl.BlockSpec((rows, width), lambda i: (0, 0)),
+            pl.BlockSpec((cols, width), lambda i: (i, 0)),
+        ],
+        out_specs=pl.BlockSpec((1, rows, cols), lambda i: (i, 0, 0)),
+        out_shape=jax.ShapeDtypeStruct((groups, rows, cols), jnp.bfloat16),
+        name="project",
+    )(context, weight)
+
+
+def weave_kernel(core_ref, near_ref, far_ref, out_ref):
+    core = core_ref[0]
+    lane = lax.broadcasted_iota(jnp.int32, (near_ref.shape[0], 128), 1)
+    for pair in range(near_ref.shape[1] // 128):
+        span = slice(128 * pair, 128 * pair + 128)
+        near = near_ref[:, span].astype(jnp.float32)
+        far = far_ref[:, span].astype(jnp.float32)
+        first = jnp.where(core == 0, near, far)
+        second = jnp.where(core == 0, far, near)
+        low = jnp.where(lane < 64, first, pltpu.roll(second, 64, 1))
+        high = jnp.where(lane < 64, pltpu.roll(first, 64, 1), second)
+        out_ref[:, 256 * pair : 256 * pair + 128] = low.astype(jnp.bfloat16)
+        out_ref[:, 256 * pair + 128 : 256 * pair + 256] = high.astype(jnp.bfloat16)
+
+
+def weave(near, far, core):
+    rows, cols = near.shape
+    half = pl.BlockSpec((rows, cols), lambda i: (0, 0))
+    return pl.pallas_call(
+        weave_kernel,
+        grid=(1,),
+        in_specs=[pl.BlockSpec(memory_space=pltpu.SMEM), half, half],
+        out_specs=pl.BlockSpec((rows, 2 * cols), lambda i: (0, 0)),
+        out_shape=jax.ShapeDtypeStruct((rows, 2 * cols), near.dtype),
+        compiler_params=pltpu.CompilerParams(vmem_limit_bytes=12 << 20),
+        name="weave",
+    )(core.reshape(1), near, far)
+
+
 def pages_kernel(page_ref, dest_ref, slot_ref, cache_ref, send_ref):
     groups, moves = send_ref.shape[:2]
     free = cache_ref.shape[0] - moves
@@ -162,6 +217,7 @@
         in_specs=[scalars, scalars, scalars, vector],
         out_specs=vector,
         out_shape=jax.ShapeDtypeStruct(shape, pages.dtype),
+        compiler_params=pltpu.CompilerParams(vmem_limit_bytes=12 << 20),
         name="pages_to_send",
     )(move_page[0, 0], move_dest[0, 0], move_slot[0, 0], pages)
 
@@ -243,7 +299,6 @@
     )
     kv, x_chip = lax.optimization_barrier((kv, x_chip))
     near = spread(kv, CHIPS).reshape(-1, 2 * HEAD_SIZE)
-    wq_near, arrived = lax.optimization_barrier((wq_near, arrived))
     query = matmul(x_chip, wq_near)
     query = query[: 2 * span] + swap_core(query[2 * span :])
     query = apply_rotation(
@@ -261,7 +316,7 @@
     my_len = lax.dynamic_index_in_dim(prompt_len, mine, 0, False)
     my_qpos = jnp.where(my_qpos < my_len, my_qpos, -1)
     all_q = jnp.stack([q_mine, q_pair]).reshape(-1, HEAD_SIZE)
-    near, all_q = lax.optimization_barrier((near, all_q))
+    near, all_q, arrived = lax.optimization_barrier((near, all_q, arrived))
     far = swap_core(near)
     all_qpos = jnp.broadcast_to(my_qpos[None, :, None], (2, span, heads_here)).reshape(-1, 1)
     context = attend(all_q, near, far, all_qpos, kpos).reshape(2, span, heads_here * HEAD_SIZE)
@@ -272,19 +327,11 @@
     )
     context = jnp.concatenate([context, swap_core(context)], axis=0)
     context, wo_near = lax.optimization_barrier((context, wo_near))
-    send = jnp.einsum(
-        "td,gnd->gtn",
-        context,
-        wo_near.reshape(rows_y, rows_z * piece, -1),
-        preferred_element_type=jnp.float32,
-    ).astype(jnp.bfloat16)
+    send = project(context, wo_near, rows_y)
     terms = lax.all_to_all(send, REP, split_axis=0, concat_axis=0, tiled=True)
     summed = jnp.sum(terms.astype(jnp.float32), axis=0).astype(jnp.bfloat16)
-    near_cols = summed[: 2 * span].reshape(2 * span, rows_z, piece)
-    far_cols = swap_core(summed[2 * span :]).reshape(2 * span, rows_z, piece)
-    first = jnp.where(core == 0, near_cols, far_cols)
-    second = jnp.where(core == 0, far_cols, near_cols)
-    attn_out = jnp.stack([first, second], axis=2).reshape(2, 1, 2, blk, -1)
+    attn_out = weave(summed[: 2 * span], swap_core(summed[2 * span :]), core)
+    attn_out = attn_out.reshape(2, 1, 2, blk, -1)
     new_cache = settle_pages(cache_pages, move_page, arrived)
     return (attn_out, new_cache)
 

time: 170 us -> 171 us (level); the launches traced: 169 us -> 168 us
  matrix products: 8.48 us -> 3.03 us
  Pallas kernels: 11.9 us -> 15.8 us
  other arithmetic: 5.08 us -> 6.97 us
    pallas_call x0 -> x2, Pallas kernels: none -> 7.19 us  [the longest x1 6.43 us: project(): pl.pallas_call(project_kernel, grid=(groups,), in_specs=[pl.BlockSpec((ro...]
    dot_general x1 -> x0, matrix products: 3.38 us -> none  [on_device(): jnp.einsum('td,gnd->gtn', context, wo_near.reshape(rows_y, rows_z * piece...]
    all_to_all x2, waiting for transfers between devices: 16.6 us -> 13.3 us  [spread(): return lax.all_to_all(copies, axes, split_axis=0, concat_axis=0, tiled=True)]
    pallas_call x1, Pallas kernels: 3.9 us -> 1.23 us  [split_norm(): pl.pallas_call(norm_kernel, grid=(rows // tile,), in_specs=[pl.BlockSpec(...]
    dot_general x3, matrix products: 5.1 us -> 3.03 us  [matmul(): return jnp.dot(left, right, preferred_element_type=jnp.float32)]
  transfers between devices with their start and end apart: 15 -> 15, of which waited for: 10 -> 12; matrix products, arithmetic and copies ran while one was open for 8% -> 7% of each run, Pallas kernels for 6% -> 5%
where the time goes in v7:
time: 171 us; the launch traced here: 168 us
  starting transfers between devices  59.8 us (35%)
  waiting for transfers between devices  39 us (23%)
  blocking collectives  22 us (13%)
  between operations  16 us (9%)
  Pallas kernels  15.8 us (9%)
  other arithmetic  6.97 us (4%)
  local copies, waits for them, and re-layouts  5.09 us (3%)
  matrix products  3.03 us (2%)
    ppermute x6, starting transfers between devices, swap_core(): return lax.ppermute(value, 'core', [(0, 1), (1, 0)])  31.9 us
    all_gather x1, blocking collectives, on_device(): weights = lax.all_gather(weights, 'zh', axis=0, tiled=True)  22 us
    all_to_all x1, waiting for transfers between devices, on_device(): terms = lax.all_to_all(send, REP, split_axis=0, concat_axis=0, tiled=True)  14.7 us
    all_to_all x2, waiting for transfers between devices, spread(): return lax.all_to_all(copies, axes, split_axis=0, concat_axis=0, tiled=True)  13.3 us
    all_to_all x2, starting transfers between devices, spread(): return lax.all_to_all(copies, axes, split_axis=0, concat_axis=0, tiled=True)  10.7 us
    ppermute x3, starting transfers between devices, swap_x(): lax.ppermute(value, 'x', [(i, i ^ 1) for i in range(lax.axis_size('x'))])  9.37 us
    all_to_all x1, starting transfers between devices, on_device(): terms = lax.all_to_all(send, REP, split_axis=0, concat_axis=0, tiled=True)  7.72 us
    pallas_call x1, Pallas kernels, project(): pl.pallas_call(project_kernel, grid=(groups,), in_specs=[pl.BlockSpec((ro...  6.43 us
  transfers between devices with their start and end apart: 15, of which 12 were waited for; matrix products, arithmetic and copies ran while one was open for 7% of the time, Pallas kernels for 5%

profile of v7, /device:TPU:1, one launch (start us, length us, event | category | flops | bytes accessed | tf_op | source)
XLA Modules:
  0.0 167.8 jit_solution(2696622363291456507)
XLA Ops:
  9.8 22.0 %all_gather.9 = bf16[256,1152]{1,0:T(8,128)(2,1)S(1)} all-gather(bf16[64,1152]{1,0:T(8,128)(2,1)S(1)} %pad_maximum_fusion.2), channel_id=1, replica_groups=mesh['y'=8,'zh'=4,'core'=2,'zl'=2,'x'=4] {'zh'}, dimensions={0}, use_global_device_ids=true | all-gather | bytes 737280 | tf_op jit(solution)/shard_map/all_gather | solution.py:267
  33.6 6.8 %all-to-all-start = ((bf16[8,256,128]{2,1,0:T(8,128)(2,1)}), bf16[8,256,128]{2,1,0:T(8,128)(2,1)S(1)}, u32[]{:S(2)}, u32[]{:S(2)}) async-start(bf16[8,256,128]{2,1,0:T(8,128)(2,1)} %broadcast_in_dim.20), calls=%async_computation | async-start | bytes 1048576 | tf_op jit(solution)/shard_map/all_to_all | solution.py:49
  40.5 1.2 split_norm.1
  41.8 4.0 %collective-permute-start.2 = (bf16[128,2048]{1,0:T(8,128)(2,1)S(1)}, bf16[128,2048]{1,0:T(8,128)(2,1)}, u32[]{:S(2)}, u32[]{:S(2)}) collective-permute-start(bf16[128,2048]{1,0:T(8,128)(2,1)S(1)} %get-tuple-element.22), channel_id=1, source_target_pairs={{0,8},{8,0},{1,9},{9,1},{2,10},{10,2},{3,11},{11,3},{4,12},{12,4},... | collective-permute-start | bytes 1572872 | tf_op jit(solution)/shard_map/ppermute | solution.py:53
  45.8 1.4 pages_to_send.1
  47.4 8.7 %all-to-all-done = bf16[8,256,128]{2,1,0:T(8,128)(2,1)S(1)} async-done(((bf16[8,256,128]{2,1,0:T(8,128)(2,1)}), bf16[8,256,128]{2,1,0:T(8,128)(2,1)S(1)}, u32[]{:S(2)}, u32[]{:S(2)}) %all-to-all-start) | async-done | bytes 524320 | tf_op jit(solution)/shard_map/all_to_all | solution.py:49
  56.1 7.5 %collective-permute-start = (bf16[2048,128]{1,0:T(8,128)(2,1)S(1)}, bf16[2048,128]{1,0:T(8,128)(2,1)S(1)}, u32[]{:S(2)}, u32[]{:S(2)}) collective-permute-start(bf16[2048,128]{1,0:T(8,128)(2,1)S(1)} %bitcast.54), channel_id=1, source_target_pairs={{0,8},{8,0},{1,9},{9,1},{2,10},{10,2},{3,11},{11,3},{4,12},{12,4},... | collective-permute-start | bytes 1572872 | tf_op jit(solution)/shard_map/ppermute | solution.py:53
  65.8 3.1 %collective-permute-start.1 = (bf16[64,128]{1,0:T(8,128)(2,1)S(1)}, bf16[64,128]{1,0:T(8,128)(2,1)S(1)}, u32[]{:S(2)}, u32[]{:S(2)}) collective-permute-start(bf16[64,128]{1,0:T(8,128)(2,1)S(1)} %get-tuple-element.55), channel_id=1, source_target_pairs={{0,1},{1,0},{2,3},{3,2},{4,5},{5,4},{6,7},{7,6},{8,9},{9,8},{10,11... | collective-permute-start | bytes 49160 | tf_op jit(solution)/shard_map/ppermute | solution.py:57
  71.8 3.9 %all-to-all-start.1 = ((bf16[32,64,256]{2,1,0:T(8,128)(2,1)}), bf16[32,64,256]{2,1,0:T(8,128)(2,1)S(1)}, u32[]{:S(2)}, u32[]{:S(2)}) async-start(bf16[32,64,256]{2,1,0:T(8,128)(2,1)} %broadcast_in_dim.24), calls=%async_computation.1 | async-start | bytes 2097152 | tf_op jit(solution)/shard_map/all_to_all | solution.py:49
  76.5 1.6 all-gather.3.cloned.1.call-done
  78.1 2.3 %fusion.14 = f32[256,512]{1,0:T(8,128)S(1)} fusion(bf16[256,2048]{1,0:T(8,128)(2,1)S(1)} %pad_maximum_fusion, bf16[2048,512]{1,0:T(8,128)(2,1)} %all-gather.3.cloned.1.call-done), kind=kOutput, calls=%fused_computation.53 | convolution fusion | flops 536870912 | bytes 3670016 | tf_op jit(solution)/shard_map/dot_general | solution.py:43
  80.5 9.2 %collective-permute-start.3 = (f32[128,512]{1,0:T(8,128)S(1)}, f32[128,512]{1,0:T(8,128)S(1)}, u32[]{:S(2)}, u32[]{:S(2)}) collective-permute-start(f32[128,512]{1,0:T(8,128)S(1)} %slice.61), channel_id=1, source_target_pairs={{0,8},{8,0},{1,9},{9,1},{2,10},{10,2},{3,11},{11,3},{4,12},{12,4},... | collective-permute-start | bytes 786440 | tf_op jit(solution)/shard_map/ppermute | solution.py:53
  91.5 2.9 %collective-permute-start.4 = (bf16[64,512]{1,0:T(8,128)(2,1)S(1)}, bf16[64,512]{1,0:T(8,128)(2,1)S(1)}, u32[]{:S(2)}, u32[]{:S(2)}) collective-permute-start(bf16[64,512]{1,0:T(8,128)(2,1)S(1)} %get-tuple-element.51), channel_id=1, source_target_pairs={{0,1},{1,0},{2,3},{3,2},{4,5},{5,4},{6,7},{7,6},{8,9},{9,8},{10,11... | collective-permute-start | bytes 196616 | tf_op jit(solution)/shard_map/ppermute | solution.py:57
  95.4 1.6 collective-permute-done.4
  98.0 4.6 %all-to-all-done.1 = bf16[32,64,256]{2,1,0:T(8,128)(2,1)S(1)} async-done(((bf16[32,64,256]{2,1,0:T(8,128)(2,1)}), bf16[32,64,256]{2,1,0:T(8,128)(2,1)S(1)}, u32[]{:S(2)}, u32[]{:S(2)}) %all-to-all-start.1) | async-done | bytes 1048608 | tf_op jit(solution)/shard_map/all_to_all | solution.py:49
  102.7 5.5 %collective-permute-start.5 = (bf16[2048,256]{1,0:T(8,128)(2,1)S(1)}, bf16[2048,256]{1,0:T(8,128)(2,1)S(1)}, u32[]{:S(2)}, u32[]{:S(2)}) collective-permute-start(bf16[2048,256]{1,0:T(8,128)(2,1)S(1)} %bitcast.45), channel_id=1, source_target_pairs={{0,8},{8,0},{1,9},{9,1},{2,10},{10,2},{3,11},{11,3},{4,12},{12,4},... | collective-permute-start | bytes 3145736 | tf_op jit(solution)/shard_map/ppermute | solution.py:53
  110.5 6.0 %attend.1 = bf16[512,128]{1,0:T(8,128)(2,1)S(1)} custom-call(bf16[512,128]{1,0:T(8,128)(2,1)S(1)} %reshape.250.q_ref, bf16[2048,256]{1,0:T(8,128)(2,1)S(1)} %bitcast.46, bf16[2048,256]{1,0:T(8,128)(2,1)S(1)} %collective-permute-done.5.far_ref, s32[512,1]{1,0:T(8,128)S(1)} %reshape.255.qpos_ref, s32[1,4096]{1,0:T(1,128)S(1)} %add.127.kpos_ref), custom_call_target="tpu_custom_call" | custom-call | tf_op jit(solution)/shard_map/attend/pallas_call | solution.py:126
  116.6 3.3 %collective-permute-start.6 = (bf16[64,512]{1,0:T(8,128)(2,1)S(1)}, bf16[64,512]{1,0:T(8,128)(2,1)S(1)}, u32[]{:S(2)}, u32[]{:S(2)}) collective-permute-start(bf16[64,512]{1,0:T(8,128)(2,1)S(1)} %squeeze.58), channel_id=1, source_target_pairs={{0,1},{1,0},{2,3},{3,2},{4,5},{5,4},{6,7},{7,6},{8,9},{9,8},{10,11... | collective-permute-start | bytes 196616 | tf_op jit(solution)/shard_map/ppermute | solution.py:57
  119.9 2.0 %collective-permute-done.6 = bf16[64,512]{1,0:T(8,128)(2,1)S(1)} collective-permute-done((bf16[64,512]{1,0:T(8,128)(2,1)S(1)}, bf16[64,512]{1,0:T(8,128)(2,1)S(1)}, u32[]{:S(2)}, u32[]{:S(2)}) %collective-permute-start.6) | collective-permute-done | bytes 65568 | tf_op jit(solution)/shard_map/ppermute | solution.py:57
  122.0 3.0 %collective-permute-start.7 = (bf16[128,512]{1,0:T(8,128)(2,1)S(1)}, bf16[128,512]{1,0:T(8,128)(2,1)S(1)}, u32[]{:S(2)}, u32[]{:S(2)}) collective-permute-start(bf16[128,512]{1,0:T(8,128)(2,1)S(1)} %pad_maximum_fusion.5), channel_id=1, source_target_pairs={{0,8},{8,0},{1,9},{9,1},{2,10},{10,2},{3,11},{11,3},{4,12},{12,4},... | collective-permute-start | bytes 393224 | tf_op jit(solution)/shard_map/ppermute | solution.py:53
  126.7 6.4 %project.1 = bf16[8,256,256]{2,1,0:T(8,128)(2,1)} custom-call(bf16[256,512]{1,0:T(8,128)(2,1)} %pad_maximum_fusion.1.context_ref, bf16[2048,512]{1,0:T(8,128)(2,1)} %all-gather.5.cloned.1.call-done.weight_ref), custom_call_target="tpu_custom_call" | custom-call | tf_op jit(solution)/shard_map/project/pallas_call | solution.py:155
  133.2 7.7 %all-to-all-start.2 = ((bf16[8,256,256]{2,1,0:T(8,128)(2,1)}), bf16[8,256,256]{2,1,0:T(8,128)(2,1)S(1)}, u32[]{:S(2)}, u32[]{:S(2)}) async-start(bf16[8,256,256]{2,1,0:T(8,128)(2,1)} %project.1), calls=%async_computation.3 | async-start | bytes 2097152 | tf_op jit(solution)/shard_map/all_to_all | solution.py:331
  141.1 14.7 %all-to-all-done.2 = bf16[8,256,256]{2,1,0:T(8,128)(2,1)S(1)} async-done(((bf16[8,256,256]{2,1,0:T(8,128)(2,1)}), bf16[8,256,256]{2,1,0:T(8,128)(2,1)S(1)}, u32[]{:S(2)}, u32[]{:S(2)}) %all-to-all-start.2) | async-done | bytes 1048608 | tf_op jit(solution)/shard_map/all_to_all | solution.py:331
  156.0 2.7 %collective-permute-start.8 = (bf16[128,256]{1,0:T(8,128)(2,1)S(1)}, bf16[128,256]{1,0:T(8,128)(2,1)S(1)}, u32[]{:S(2)}, u32[]{:S(2)}) collective-permute-start(bf16[128,256]{1,0:T(8,128)(2,1)S(1)} %get-tuple-element.44), channel_id=1, source_target_pairs={{0,8},{8,0},{1,9},{9,1},{2,10},{10,2},{3,11},{11,3},{4,12},{12,4},... | collective-permute-start | bytes 196616 | tf_op jit(solution)/shard_map/ppermute | solution.py:53
  (95 shorter events, 19.3 us)
Async XLA Ops:
  8.0 70.1 %all-gather.3.cloned.1.call-start = ((), (), s32[]{:S(2)}) async-start(), calls=%async_computation.4 | async-start | bytes 2359296 | tf_op jit(solution)/shard_map/all_gather | solution.py:272
  8.1 32.4 %copy-start.6 = (bf16[4096]{0:T(1024)(128)(2,1)S(1)}, bf16[4096]{0:T(1024)(128)(2,1)}, u32[]{:S(2)}) copy-start(bf16[4096]{0:T(1024)(128)(2,1)} %param.13) | copy-start | bytes 24580
  8.1 32.4 %copy-start.1 = (bf16[2,1,2,32,4096]{4,3,2,1,0:T(8,128)(2,1)S(1)}, bf16[2,1,2,32,4096]{4,3,2,1,0:T(8,128)(2,1)}, u32[]{:S(2)}) copy-start(bf16[2,1,2,32,4096]{4,3,2,1,0:T(8,128)(2,1)} %param.12) | copy-start | bytes 3145732
  31.9 13.9 %copy-start = (bf16[1,1,16,16,1024]{4,3,2,1,0:T(8,128)(2,1)S(1)}, bf16[1,1,16,16,1024]{4,3,2,1,0:T(8,128)(2,1)}, u32[]{:S(2)}) copy-start(bf16[1,1,16,16,1024]{4,3,2,1,0:T(8,128)(2,1)} %param.20) | copy-start | bytes 1572868
  31.9 13.9 %copy-start.2 = (s32[1,1,2]{2,1,0:T(1,128)S(1)}, s32[1,1,2]{2,1,0:T(1,128)}, u32[]{:S(2)}) copy-start(s32[1,1,2]{2,1,0:T(1,128)} %param.22) | copy-start | bytes 28
  31.9 13.9 %copy-start.3 = (s32[1,1,2]{2,1,0:T(1,128)S(1)}, s32[1,1,2]{2,1,0:T(1,128)}, u32[]{:S(2)}) copy-start(s32[1,1,2]{2,1,0:T(1,128)} %param.23) | copy-start | bytes 28
  31.9 14.0 %copy-start.4 = (s32[1,1,2]{2,1,0:T(1,128)S(1)}, s32[1,1,2]{2,1,0:T(1,128)}, u32[]{:S(2)}) copy-start(s32[1,1,2]{2,1,0:T(1,128)} %param.21) | copy-start | bytes 28
  32.7 14.5 %copy-start.7 = (s32[2,64]{1,0:T(2,128)S(1)}, s32[2,64]{1,0:T(2,128)}, u32[]{:S(2)}) copy-start(s32[2,64]{1,0:T(2,128)} %param.19) | copy-start | bytes 1540
  33.6 22.5 %all-to-all-start = ((bf16[8,256,128]{2,1,0:T(8,128)(2,1)}), bf16[8,256,128]{2,1,0:T(8,128)(2,1)S(1)}, u32[]{:S(2)}, u32[]{:S(2)}) async-start(bf16[8,256,128]{2,1,0:T(8,128)(2,1)} %broadcast_in_dim.20), calls=%async_computation | async-start | bytes 1048576 | tf_op jit(solution)/shard_map/all_to_all | solution.py:49
  40.4 57.6 %reduce-scatter.2.cloned.1.call-start = ((), (), s32[]{:S(2)}) async-start(), calls=%async_computation.5 | async-start | bytes 589824 | tf_op jit(solution)/shard_map/reduce_scatter | solution.py:276
  41.8 27.2 %collective-permute-start.2 = (bf16[128,2048]{1,0:T(8,128)(2,1)S(1)}, bf16[128,2048]{1,0:T(8,128)(2,1)}, u32[]{:S(2)}, u32[]{:S(2)}) collective-permute-start(bf16[128,2048]{1,0:T(8,128)(2,1)S(1)} %get-tuple-element.22), channel_id=1, source_target_pairs={{0,8},{8,0},{1,9},{9,1},{2,10},{10,2},{3,11},{11,3},{4,12},{12,4},... | collective-permute-start | bytes 1572872 | tf_op jit(solution)/shard_map/ppermute | solution.py:53
  56.1 9.0 %collective-permute-start = (bf16[2048,128]{1,0:T(8,128)(2,1)S(1)}, bf16[2048,128]{1,0:T(8,128)(2,1)S(1)}, u32[]{:S(2)}, u32[]{:S(2)}) collective-permute-start(bf16[2048,128]{1,0:T(8,128)(2,1)S(1)} %bitcast.54), channel_id=1, source_target_pairs={{0,8},{8,0},{1,9},{9,1},{2,10},{10,2},{3,11},{11,3},{4,12},{12,4},... | collective-permute-start | bytes 1572872 | tf_op jit(solution)/shard_map/ppermute | solution.py:53
  65.8 4.9 %collective-permute-start.1 = (bf16[64,128]{1,0:T(8,128)(2,1)S(1)}, bf16[64,128]{1,0:T(8,128)(2,1)S(1)}, u32[]{:S(2)}, u32[]{:S(2)}) collective-permute-start(bf16[64,128]{1,0:T(8,128)(2,1)S(1)} %get-tuple-element.55), channel_id=1, source_target_pairs={{0,1},{1,0},{2,3},{3,2},{4,5},{5,4},{6,7},{7,6},{8,9},{9,8},{10,11... | collective-permute-start | bytes 49160 | tf_op jit(solution)/shard_map/ppermute | solution.py:57
  71.8 30.8 %all-to-all-start.1 = ((bf16[32,64,256]{2,1,0:T(8,128)(2,1)}), bf16[32,64,256]{2,1,0:T(8,128)(2,1)S(1)}, u32[]{:S(2)}, u32[]{:S(2)}) async-start(bf16[32,64,256]{2,1,0:T(8,128)(2,1)} %broadcast_in_dim.24), calls=%async_computation.1 | async-start | bytes 2097152 | tf_op jit(solution)/shard_map/all_to_all | solution.py:49
  75.8 51.0 %all-gather.5.cloned.1.call-start = ((), (), s32[]{:S(2)}) async-start(), calls=%async_computation.6 | async-start | bytes 2359296 | tf_op jit(solution)/shard_map/all_gather | solution.py:281
  80.5 14.1 %copy-start.8 = (s32[2]{0:T(128)S(1)}, s32[2]{0:T(128)}, u32[]{:S(2)}) copy-start(s32[2]{0:T(128)} %param.18) | copy-start | bytes 28
  80.5 10.3 %collective-permute-start.3 = (f32[128,512]{1,0:T(8,128)S(1)}, f32[128,512]{1,0:T(8,128)S(1)}, u32[]{:S(2)}, u32[]{:S(2)}) collective-permute-start(f32[128,512]{1,0:T(8,128)S(1)} %slice.61), channel_id=1, source_target_pairs={{0,8},{8,0},{1,9},{9,1},{2,10},{10,2},{3,11},{11,3},{4,12},{12,4},... | collective-permute-start | bytes 786440 | tf_op jit(solution)/shard_map/ppermute | solution.py:53
  91.5 5.4 %collective-permute-start.4 = (bf16[64,512]{1,0:T(8,128)(2,1)S(1)}, bf16[64,512]{1,0:T(8,128)(2,1)S(1)}, u32[]{:S(2)}, u32[]{:S(2)}) collective-permute-start(bf16[64,512]{1,0:T(8,128)(2,1)S(1)} %get-tuple-element.51), channel_id=1, source_target_pairs={{0,1},{1,0},{2,3},{3,2},{4,5},{5,4},{6,7},{7,6},{8,9},{9,8},{10,11... | collective-permute-start | bytes 196616 | tf_op jit(solution)/shard_map/ppermute | solution.py:57
  102.7 7.8 %collective-permute-start.5 = (bf16[2048,256]{1,0:T(8,128)(2,1)S(1)}, bf16[2048,256]{1,0:T(8,128)(2,1)S(1)}, u32[]{:S(2)}, u32[]{:S(2)}) collective-permute-start(bf16[2048,256]{1,0:T(8,128)(2,1)S(1)} %bitcast.45), channel_id=1, source_target_pairs={{0,8},{8,0},{1,9},{9,1},{2,10},{10,2},{3,11},{11,3},{4,12},{12,4},... | collective-permute-start | bytes 3145736 | tf_op jit(solution)/shard_map/ppermute | solution.py:53
  116.6 5.4 %collective-permute-start.6 = (bf16[64,512]{1,0:T(8,128)(2,1)S(1)}, bf16[64,512]{1,0:T(8,128)(2,1)S(1)}, u32[]{:S(2)}, u32[]{:S(2)}) collective-permute-start(bf16[64,512]{1,0:T(8,128)(2,1)S(1)} %squeeze.58), channel_id=1, source_target_pairs={{0,1},{1,0},{2,3},{3,2},{4,5},{5,4},{6,7},{7,6},{8,9},{9,8},{10,11... | collective-permute-start | bytes 196616 | tf_op jit(solution)/shard_map/ppermute | solution.py:57
  122.0 4.0 %collective-permute-start.7 = (bf16[128,512]{1,0:T(8,128)(2,1)S(1)}, bf16[128,512]{1,0:T(8,128)(2,1)S(1)}, u32[]{:S(2)}, u32[]{:S(2)}) collective-permute-start(bf16[128,512]{1,0:T(8,128)(2,1)S(1)} %pad_maximum_fusion.5), channel_id=1, source_target_pairs={{0,8},{8,0},{1,9},{9,1},{2,10},{10,2},{3,11},{11,3},{4,12},{12,4},... | collective-permute-start | bytes 393224 | tf_op jit(solution)/shard_map/ppermute | solution.py:53
  133.2 25.6 %copy-start.5 = (bf16[1,2,16,1024]{3,2,1,0:T(8,128)(2,1)S(1)}, bf16[1,2,16,1024]{3,2,1,0:T(8,128)(2,1)}, u32[]{:S(2)}) copy-start(bf16[1,2,16,1024]{3,2,1,0:T(8,128)(2,1)} %reduce-scatter.2.cloned.1.call-done) | copy-start | bytes 196612
  133.2 22.7 %all-to-all-start.2 = ((bf16[8,256,256]{2,1,0:T(8,128)(2,1)}), bf16[8,256,256]{2,1,0:T(8,128)(2,1)S(1)}, u32[]{:S(2)}, u32[]{:S(2)}) async-start(bf16[8,256,256]{2,1,0:T(8,128)(2,1)} %project.1), calls=%async_computation.3 | async-start | bytes 2097152 | tf_op jit(solution)/shard_map/all_to_all | solution.py:331
  156.0 3.6 %collective-permute-start.8 = (bf16[128,256]{1,0:T(8,128)(2,1)S(1)}, bf16[128,256]{1,0:T(8,128)(2,1)S(1)}, u32[]{:S(2)}, u32[]{:S(2)}) collective-permute-start(bf16[128,256]{1,0:T(8,128)(2,1)S(1)} %get-tuple-element.44), channel_id=1, source_target_pairs={{0,8},{8,0},{1,9},{9,1},{2,10},{10,2},{3,11},{11,3},{4,12},{12,4},... | collective-permute-start | bytes 196616 | tf_op jit(solution)/shard_map/ppermute | solution.py:53
Sparse Core Ops, SparseCore 0:
  32.8 45.2 all-gather.2
  80.2 44.4 all-gather.4
Sparse Core Ops, SparseCore 1:
  47.3 50.6 reduce-scatter.1

commit v8 on v4

--- a/solution.py
+++ b/solution.py
@@ -88,6 +88,7 @@
         ],
         out_specs=(half_spec, half_spec),
         out_shape=(half, half),
+        compiler_params=pltpu.CompilerParams(vmem_limit_bytes=12 << 20),
         name="split_norm",
     )(core.reshape(1), hidden, gain[None])
 
@@ -162,6 +163,7 @@
         in_specs=[scalars, scalars, scalars, vector],
         out_specs=vector,
         out_shape=jax.ShapeDtypeStruct(shape, pages.dtype),
+        compiler_params=pltpu.CompilerParams(vmem_limit_bytes=12 << 20),
         name="pages_to_send",
     )(move_page[0, 0], move_dest[0, 0], move_slot[0, 0], pages)
 
@@ -243,7 +245,6 @@
     )
     kv, x_chip = lax.optimization_barrier((kv, x_chip))
     near = spread(kv, CHIPS).reshape(-1, 2 * HEAD_SIZE)
-    wq_near, arrived = lax.optimization_barrier((wq_near, arrived))
     query = matmul(x_chip, wq_near)
     query = query[: 2 * span] + swap_core(query[2 * span :])
     query = apply_rotation(
@@ -261,7 +262,7 @@
     my_len = lax.dynamic_index_in_dim(prompt_len, mine, 0, False)
     my_qpos = jnp.where(my_qpos < my_len, my_qpos, -1)
     all_q = jnp.stack([q_mine, q_pair]).reshape(-1, HEAD_SIZE)
-    near, all_q = lax.optimization_barrier((near, all_q))
+    near, all_q, arrived = lax.optimization_barrier((near, all_q, arrived))
     far = swap_core(near)
     all_qpos = jnp.broadcast_to(my_qpos[None, :, None], (2, span, heads_here)).reshape(-1, 1)
     context = attend(all_q, near, far, all_qpos, kpos).reshape(2, span, heads_here * HEAD_SIZE)

time: 170 us -> 167 us (0.982); the launches traced: 169 us -> 164 us
  Pallas kernels: 11.9 us -> 8.64 us
    reduce_scatter x1, waiting for transfers between devices: 0.02 us -> 8.3 us  [on_device(): arrived = lax.psum_scatter(send_pages, REP, scatter_dimension=0, tiled=True)]
    all_to_all x2, waiting for transfers between devices: 16.6 us -> 8.79 us  [spread(): return lax.all_to_all(copies, axes, split_axis=0, concat_axis=0, tiled=True)]
    all_to_all x1, waiting for transfers between devices: 14.8 us -> 11.1 us  [on_device(): terms = lax.all_to_all(send, REP, split_axis=0, concat_axis=0, tiled=True)]
    pallas_call x1, Pallas kernels: 3.9 us -> 1.23 us  [split_norm(): pl.pallas_call(norm_kernel, grid=(rows // tile,), in_specs=[pl.BlockSpec(...]
    ppermute x6, starting transfers between devices: 30.6 us -> 32.6 us  [swap_core(): return lax.ppermute(value, 'core', [(0, 1), (1, 0)])]
  transfers between devices with their start and end apart: 15 -> 15, of which waited for: 10 -> 11; matrix products, arithmetic and copies ran while one was open for 8% -> 7% of each run, Pallas kernels for 6% -> 5%
where the time goes in v8:
time: 167 us; the launch traced here: 164 us
  starting transfers between devices  59.7 us (36%)
  waiting for transfers between devices  38.8 us (23%)
  blocking collectives  22 us (13%)
  between operations  16 us (10%)
  Pallas kernels  8.64 us (5%)
  matrix products  7.4 us (4%)
  local copies, waits for them, and re-layouts  6.14 us (4%)
  other arithmetic  5.17 us (3%)
    ppermute x6, starting transfers between devices, swap_core(): return lax.ppermute(value, 'core', [(0, 1), (1, 0)])  32.6 us
    all_gather x1, blocking collectives, on_device(): weights = lax.all_gather(weights, 'zh', axis=0, tiled=True)  22 us
    all_to_all x1, waiting for transfers between devices, on_device(): terms = lax.all_to_all(send, REP, split_axis=0, concat_axis=0, tiled=True)  11.1 us
    all_to_all x2, starting transfers between devices, spread(): return lax.all_to_all(copies, axes, split_axis=0, concat_axis=0, tiled=True)  10.7 us
    ppermute x3, starting transfers between devices, swap_x(): lax.ppermute(value, 'x', [(i, i ^ 1) for i in range(lax.axis_size('x'))])  9.84 us
    all_to_all x2, waiting for transfers between devices, spread(): return lax.all_to_all(copies, axes, split_axis=0, concat_axis=0, tiled=True)  8.79 us
    reduce_scatter x1, waiting for transfers between devices, on_device(): arrived = lax.psum_scatter(send_pages, REP, scatter_dimension=0, tiled=True)  8.3 us
    all_to_all x1, starting transfers between devices, on_device(): terms = lax.all_to_all(send, REP, split_axis=0, concat_axis=0, tiled=True)  6.37 us
  transfers between devices with their start and end apart: 15, of which 11 were waited for; matrix products, arithmetic and copies ran while one was open for 7% of the time, Pallas kernels for 5%

profile of v8, /device:TPU:1, one launch (start us, length us, event | category | flops | bytes accessed | tf_op | source)
XLA Modules:
  0.0 163.9 jit_solution(17025820349540809268)
XLA Ops:
  9.8 22.0 %all_gather.9 = bf16[256,1152]{1,0:T(8,128)(2,1)S(1)} all-gather(bf16[64,1152]{1,0:T(8,128)(2,1)S(1)} %pad_maximum_fusion.2), channel_id=1, replica_groups=mesh['y'=8,'zh'=4,'core'=2,'zl'=2,'x'=4] {'zh'}, dimensions={0}, use_global_device_ids=true | all-gather | bytes 737280 | tf_op jit(solution)/shard_map/all_gather | solution.py:213
  33.6 6.8 %all-to-all-start = ((bf16[8,256,128]{2,1,0:T(8,128)(2,1)}), bf16[8,256,128]{2,1,0:T(8,128)(2,1)}, u32[]{:S(2)}, u32[]{:S(2)}) async-start(bf16[8,256,128]{2,1,0:T(8,128)(2,1)} %broadcast_in_dim.20), calls=%async_computation | async-start | bytes 1048576 | tf_op jit(solution)/shard_map/all_to_all | solution.py:49
  41.8 4.0 %collective-permute-start.2 = (bf16[128,2048]{1,0:T(8,128)(2,1)S(1)}, bf16[128,2048]{1,0:T(8,128)(2,1)S(1)}, u32[]{:S(2)}, u32[]{:S(2)}) collective-permute-start(bf16[128,2048]{1,0:T(8,128)(2,1)S(1)} %get-tuple-element.22), channel_id=1, source_target_pairs={{0,8},{8,0},{1,9},{9,1},{2,10},{10,2},{3,11},{11,3},{4,12},{12,4},... | collective-permute-start | bytes 1572872 | tf_op jit(solution)/shard_map/ppermute | solution.py:53
  45.8 1.4 pages_to_send.1
  47.4 8.8 %all-to-all-done = bf16[8,256,128]{2,1,0:T(8,128)(2,1)} async-done(((bf16[8,256,128]{2,1,0:T(8,128)(2,1)}), bf16[8,256,128]{2,1,0:T(8,128)(2,1)}, u32[]{:S(2)}, u32[]{:S(2)}) %all-to-all-start) | async-done | bytes 524320 | tf_op jit(solution)/shard_map/all_to_all | solution.py:49
  56.2 7.5 %collective-permute-start = (bf16[2048,128]{1,0:T(8,128)(2,1)}, bf16[2048,128]{1,0:T(8,128)(2,1)S(1)}, u32[]{:S(2)}, u32[]{:S(2)}) collective-permute-start(bf16[2048,128]{1,0:T(8,128)(2,1)} %bitcast.1), channel_id=1, source_target_pairs={{0,8},{8,0},{1,9},{9,1},{2,10},{10,2},{3,11},{11,3},{4,12},{12,4},... | collective-permute-start | bytes 1572872 | tf_op jit(solution)/shard_map/ppermute | solution.py:53
  66.1 3.1 %collective-permute-start.1 = (bf16[64,128]{1,0:T(8,128)(2,1)S(1)}, bf16[64,128]{1,0:T(8,128)(2,1)S(1)}, u32[]{:S(2)}, u32[]{:S(2)}) collective-permute-start(bf16[64,128]{1,0:T(8,128)(2,1)S(1)} %get-tuple-element.53), channel_id=1, source_target_pairs={{0,1},{1,0},{2,3},{3,2},{4,5},{5,4},{6,7},{7,6},{8,9},{9,8},{10,11... | collective-permute-start | bytes 49160 | tf_op jit(solution)/shard_map/ppermute | solution.py:57
  69.3 1.7 %collective-permute-done.1 = bf16[64,128]{1,0:T(8,128)(2,1)S(1)} collective-permute-done((bf16[64,128]{1,0:T(8,128)(2,1)S(1)}, bf16[64,128]{1,0:T(8,128)(2,1)S(1)}, u32[]{:S(2)}, u32[]{:S(2)}) %collective-permute-start.1) | collective-permute-done | bytes 16416 | tf_op jit(solution)/shard_map/ppermute | solution.py:57
  72.2 3.9 %all-to-all-start.1 = ((bf16[32,64,256]{2,1,0:T(8,128)(2,1)}), bf16[32,64,256]{2,1,0:T(8,128)(2,1)S(1)}, u32[]{:S(2)}, u32[]{:S(2)}) async-start(bf16[32,64,256]{2,1,0:T(8,128)(2,1)} %broadcast_in_dim.24), calls=%async_computation.1 | async-start | bytes 2097152 | tf_op jit(solution)/shard_map/all_to_all | solution.py:49
  76.9 2.1 %all-gather.3.cloned.1.call-done = bf16[2048,512]{1,0:T(8,128)(2,1)} async-done(((bf16[256,512]{1,0:T(8,128)(2,1)}), bf16[2048,512]{1,0:T(8,128)(2,1)}) %all-gather.3.cloned.1.call-update) | async-done | bytes 2097168 | tf_op jit(solution)/shard_map/all_gather | solution.py:218
  79.0 2.3 %fusion.15 = f32[256,512]{1,0:T(8,128)S(1)} fusion(bf16[256,2048]{1,0:T(8,128)(2,1)S(1)} %pad_maximum_fusion, bf16[2048,512]{1,0:T(8,128)(2,1)} %all-gather.3.cloned.1.call-done), kind=kOutput, calls=%fused_computation.58 | convolution fusion | flops 536870912 | bytes 3670016 | tf_op jit(solution)/shard_map/dot_general | solution.py:43
  81.4 7.4 %collective-permute-start.3 = (f32[128,512]{1,0:T(8,128)S(1)}, f32[128,512]{1,0:T(8,128)S(1)}, u32[]{:S(2)}, u32[]{:S(2)}) collective-permute-start(f32[128,512]{1,0:T(8,128)S(1)} %slice.61), channel_id=1, source_target_pairs={{0,8},{8,0},{1,9},{9,1},{2,10},{10,2},{3,11},{11,3},{4,12},{12,4},... | collective-permute-start | bytes 786440 | tf_op jit(solution)/shard_map/ppermute | solution.py:53
  90.7 3.1 %collective-permute-start.4 = (bf16[64,512]{1,0:T(8,128)(2,1)S(1)}, bf16[64,512]{1,0:T(8,128)(2,1)S(1)}, u32[]{:S(2)}, u32[]{:S(2)}) collective-permute-start(bf16[64,512]{1,0:T(8,128)(2,1)S(1)} %get-tuple-element.49), channel_id=1, source_target_pairs={{0,1},{1,0},{2,3},{3,2},{4,5},{5,4},{6,7},{7,6},{8,9},{9,8},{10,11... | collective-permute-start | bytes 196616 | tf_op jit(solution)/shard_map/ppermute | solution.py:57
  94.7 1.4 collective-permute-done.4
  96.2 8.3 %reduce-scatter.2.cloned.1.call-done = bf16[1,2,16,1024]{3,2,1,0:T(8,128)(2,1)} async-done(((bf16[8,2,16,1024]{3,2,1,0:T(8,128)(2,1)}), bf16[1,2,16,1024]{3,2,1,0:T(8,128)(2,1)}) %reduce-scatter.2.cloned.1.call-update) | async-done | bytes 65552 | tf_op jit(solution)/shard_map/reduce_scatter | solution.py:222
  104.5 4.5 %collective-permute-start.5 = (bf16[2048,256]{1,0:T(8,128)(2,1)S(1)}, bf16[2048,256]{1,0:T(8,128)(2,1)S(1)}, u32[]{:S(2)}, u32[]{:S(2)}) collective-permute-start(bf16[2048,256]{1,0:T(8,128)(2,1)S(1)} %bitcast.52), channel_id=1, source_target_pairs={{0,8},{8,0},{1,9},{9,1},{2,10},{10,2},{3,11},{11,3},{4,12},{12,4},... | collective-permute-start | bytes 3145736 | tf_op jit(solution)/shard_map/ppermute | solution.py:53
  111.3 6.0 %attend.1 = bf16[512,128]{1,0:T(8,128)(2,1)S(1)} custom-call(bf16[512,128]{1,0:T(8,128)(2,1)S(1)} %reshape.292.q_ref, bf16[2048,256]{1,0:T(8,128)(2,1)S(1)} %bitcast.53, bf16[2048,256]{1,0:T(8,128)(2,1)S(1)} %collective-permute-done.5.far_ref, s32[512,1]{1,0:T(8,128)S(1)} %reshape.299.qpos_ref, s32[1,4096]{1,0:T(1,128)S(1)} %add.127.kpos_ref), custom_call_target="tpu_custom_call" | custom-call | tf_op jit(solution)/shard_map/attend/pallas_call | solution.py:126
  117.4 3.6 %collective-permute-start.6 = (bf16[64,512]{1,0:T(8,128)(2,1)S(1)}, bf16[64,512]{1,0:T(8,128)(2,1)S(1)}, u32[]{:S(2)}, u32[]{:S(2)}) collective-permute-start(bf16[64,512]{1,0:T(8,128)(2,1)S(1)} %squeeze.58), channel_id=1, source_target_pairs={{0,1},{1,0},{2,3},{3,2},{4,5},{5,4},{6,7},{7,6},{8,9},{9,8},{10,11... | collective-permute-start | bytes 196616 | tf_op jit(solution)/shard_map/ppermute | solution.py:57
  121.0 2.1 %collective-permute-done.6 = bf16[64,512]{1,0:T(8,128)(2,1)S(1)} collective-permute-done((bf16[64,512]{1,0:T(8,128)(2,1)S(1)}, bf16[64,512]{1,0:T(8,128)(2,1)S(1)}, u32[]{:S(2)}, u32[]{:S(2)}) %collective-permute-start.6) | collective-permute-done | bytes 65568 | tf_op jit(solution)/shard_map/ppermute | solution.py:57
  123.1 2.8 %collective-permute-start.7 = (bf16[128,512]{1,0:T(8,128)(2,1)S(1)}, bf16[128,512]{1,0:T(8,128)(2,1)S(1)}, u32[]{:S(2)}, u32[]{:S(2)}) collective-permute-start(bf16[128,512]{1,0:T(8,128)(2,1)S(1)} %pad_maximum_fusion.5), channel_id=1, source_target_pairs={{0,8},{8,0},{1,9},{9,1},{2,10},{10,2},{3,11},{11,3},{4,12},{12,4},... | collective-permute-start | bytes 393224 | tf_op jit(solution)/shard_map/ppermute | solution.py:53
  127.0 3.3 %fusion = bf16[8,256,256]{1,2,0:T(8,128)(2,1)} fusion(bf16[8,256,512]{2,1,0:T(8,128)(2,1)} %bitcast.61, bf16[256,512]{1,0:T(8,128)(2,1)S(1)} %pad_maximum_fusion.1), kind=kOutput, calls=%fused_computation.1 | convolution fusion | flops 537395200 | bytes 3407872 | tf_op jit(solution)/shard_map/td,gnd->gtn/dot_general | solution.py:276
  130.3 6.4 %all-to-all-start.2 = ((bf16[8,256,256]{1,2,0:T(8,128)(2,1)}), bf16[8,256,256]{1,2,0:T(8,128)(2,1)S(1)}, u32[]{:S(2)}, u32[]{:S(2)}) async-start(bf16[8,256,256]{1,2,0:T(8,128)(2,1)} %fusion), calls=%async_computation.3 | async-start | bytes 2097152 | tf_op jit(solution)/shard_map/all_to_all | solution.py:282
  136.9 11.1 %all-to-all-done.2 = bf16[8,256,256]{1,2,0:T(8,128)(2,1)S(1)} async-done(((bf16[8,256,256]{1,2,0:T(8,128)(2,1)}), bf16[8,256,256]{1,2,0:T(8,128)(2,1)S(1)}, u32[]{:S(2)}, u32[]{:S(2)}) %all-to-all-start.2) | async-done | bytes 1048608 | tf_op jit(solution)/shard_map/all_to_all | solution.py:282
  148.1 6.4 %collective-permute-start.8 = (bf16[128,256]{0,1:T(8,128)(2,1)S(1)}, bf16[128,256]{0,1:T(8,128)(2,1)S(1)}, u32[]{:S(2)}, u32[]{:S(2)}) collective-permute-start(bf16[128,256]{0,1:T(8,128)(2,1)S(1)} %slice.67), channel_id=1, source_target_pairs={{0,8},{8,0},{1,9},{9,1},{2,10},{10,2},{3,11},{11,3},{4,12},{12,4},... | collective-permute-start | bytes 196616 | tf_op jit(solution)/shard_map/ppermute | solution.py:53
  (98 shorter events, 17.8 us)
Async XLA Ops:
  8.0 71.0 %all-gather.3.cloned.1.call-start = ((), (), s32[]{:S(2)}) async-start(), calls=%async_computation.4 | async-start | bytes 2359296 | tf_op jit(solution)/shard_map/all_gather | solution.py:218
  8.1 32.4 %copy-start.6 = (bf16[4096]{0:T(1024)(128)(2,1)S(1)}, bf16[4096]{0:T(1024)(128)(2,1)}, u32[]{:S(2)}) copy-start(bf16[4096]{0:T(1024)(128)(2,1)} %param.13) | copy-start | bytes 24580
  8.1 32.4 %copy-start.1 = (bf16[2,1,2,32,4096]{4,3,2,1,0:T(8,128)(2,1)S(1)}, bf16[2,1,2,32,4096]{4,3,2,1,0:T(8,128)(2,1)}, u32[]{:S(2)}) copy-start(bf16[2,1,2,32,4096]{4,3,2,1,0:T(8,128)(2,1)} %param.12) | copy-start | bytes 3145732
  31.9 13.9 %copy-start = (bf16[1,1,16,16,1024]{4,3,2,1,0:T(8,128)(2,1)S(1)}, bf16[1,1,16,16,1024]{4,3,2,1,0:T(8,128)(2,1)}, u32[]{:S(2)}) copy-start(bf16[1,1,16,16,1024]{4,3,2,1,0:T(8,128)(2,1)} %param.20) | copy-start | bytes 1572868
  31.9 13.9 %copy-start.2 = (s32[1,1,2]{2,1,0:T(1,128)S(1)}, s32[1,1,2]{2,1,0:T(1,128)}, u32[]{:S(2)}) copy-start(s32[1,1,2]{2,1,0:T(1,128)} %param.22) | copy-start | bytes 28
  31.9 13.9 %copy-start.3 = (s32[1,1,2]{2,1,0:T(1,128)S(1)}, s32[1,1,2]{2,1,0:T(1,128)}, u32[]{:S(2)}) copy-start(s32[1,1,2]{2,1,0:T(1,128)} %param.23) | copy-start | bytes 28
  31.9 13.9 %copy-start.4 = (s32[1,1,2]{2,1,0:T(1,128)S(1)}, s32[1,1,2]{2,1,0:T(1,128)}, u32[]{:S(2)}) copy-start(s32[1,1,2]{2,1,0:T(1,128)} %param.21) | copy-start | bytes 28
  32.7 14.5 %copy-start.7 = (s32[2,64]{1,0:T(2,128)S(1)}, s32[2,64]{1,0:T(2,128)}, u32[]{:S(2)}) copy-start(s32[2,64]{1,0:T(2,128)} %param.19) | copy-start | bytes 1540
  33.6 22.6 %all-to-all-start = ((bf16[8,256,128]{2,1,0:T(8,128)(2,1)}), bf16[8,256,128]{2,1,0:T(8,128)(2,1)}, u32[]{:S(2)}, u32[]{:S(2)}) async-start(bf16[8,256,128]{2,1,0:T(8,128)(2,1)} %broadcast_in_dim.20), calls=%async_computation | async-start | bytes 1048576 | tf_op jit(solution)/shard_map/all_to_all | solution.py:49
  40.4 64.1 %reduce-scatter.2.cloned.1.call-start = ((), (), s32[]{:S(2)}) async-start(), calls=%async_computation.5 | async-start | bytes 589824 | tf_op jit(solution)/shard_map/reduce_scatter | solution.py:222
  41.8 27.5 %collective-permute-start.2 = (bf16[128,2048]{1,0:T(8,128)(2,1)S(1)}, bf16[128,2048]{1,0:T(8,128)(2,1)S(1)}, u32[]{:S(2)}, u32[]{:S(2)}) collective-permute-start(bf16[128,2048]{1,0:T(8,128)(2,1)S(1)} %get-tuple-element.22), channel_id=1, source_target_pairs={{0,8},{8,0},{1,9},{9,1},{2,10},{10,2},{3,11},{11,3},{4,12},{12,4},... | collective-permute-start | bytes 1572872 | tf_op jit(solution)/shard_map/ppermute | solution.py:53
  56.2 9.2 %collective-permute-start = (bf16[2048,128]{1,0:T(8,128)(2,1)}, bf16[2048,128]{1,0:T(8,128)(2,1)S(1)}, u32[]{:S(2)}, u32[]{:S(2)}) collective-permute-start(bf16[2048,128]{1,0:T(8,128)(2,1)} %bitcast.1), channel_id=1, source_target_pairs={{0,8},{8,0},{1,9},{9,1},{2,10},{10,2},{3,11},{11,3},{4,12},{12,4},... | collective-permute-start | bytes 1572872 | tf_op jit(solution)/shard_map/ppermute | solution.py:53
  66.1 5.0 %collective-permute-start.1 = (bf16[64,128]{1,0:T(8,128)(2,1)S(1)}, bf16[64,128]{1,0:T(8,128)(2,1)S(1)}, u32[]{:S(2)}, u32[]{:S(2)}) collective-permute-start(bf16[64,128]{1,0:T(8,128)(2,1)S(1)} %get-tuple-element.53), channel_id=1, source_target_pairs={{0,1},{1,0},{2,3},{3,2},{4,5},{5,4},{6,7},{7,6},{8,9},{9,8},{10,11... | collective-permute-start | bytes 49160 | tf_op jit(solution)/shard_map/ppermute | solution.py:57
  72.2 32.3 %all-to-all-start.1 = ((bf16[32,64,256]{2,1,0:T(8,128)(2,1)}), bf16[32,64,256]{2,1,0:T(8,128)(2,1)S(1)}, u32[]{:S(2)}, u32[]{:S(2)}) async-start(bf16[32,64,256]{2,1,0:T(8,128)(2,1)} %broadcast_in_dim.24), calls=%async_computation.1 | async-start | bytes 2097152 | tf_op jit(solution)/shard_map/all_to_all | solution.py:49
  76.2 50.8 %all-gather.5.cloned.1.call-start = ((), (), s32[]{:S(2)}) async-start(), calls=%async_computation.6 | async-start | bytes 2359296 | tf_op jit(solution)/shard_map/all_gather | solution.py:227
  81.4 12.5 %copy-start.8 = (s32[2]{0:T(128)S(1)}, s32[2]{0:T(128)}, u32[]{:S(2)}) copy-start(s32[2]{0:T(128)} %param.18) | copy-start | bytes 28
  81.4 8.5 %collective-permute-start.3 = (f32[128,512]{1,0:T(8,128)S(1)}, f32[128,512]{1,0:T(8,128)S(1)}, u32[]{:S(2)}, u32[]{:S(2)}) collective-permute-start(f32[128,512]{1,0:T(8,128)S(1)} %slice.61), channel_id=1, source_target_pairs={{0,8},{8,0},{1,9},{9,1},{2,10},{10,2},{3,11},{11,3},{4,12},{12,4},... | collective-permute-start | bytes 786440 | tf_op jit(solution)/shard_map/ppermute | solution.py:53
  90.7 5.4 %collective-permute-start.4 = (bf16[64,512]{1,0:T(8,128)(2,1)S(1)}, bf16[64,512]{1,0:T(8,128)(2,1)S(1)}, u32[]{:S(2)}, u32[]{:S(2)}) collective-permute-start(bf16[64,512]{1,0:T(8,128)(2,1)S(1)} %get-tuple-element.49), channel_id=1, source_target_pairs={{0,1},{1,0},{2,3},{3,2},{4,5},{5,4},{6,7},{7,6},{8,9},{9,8},{10,11... | collective-permute-start | bytes 196616 | tf_op jit(solution)/shard_map/ppermute | solution.py:57
  104.5 6.8 %collective-permute-start.5 = (bf16[2048,256]{1,0:T(8,128)(2,1)S(1)}, bf16[2048,256]{1,0:T(8,128)(2,1)S(1)}, u32[]{:S(2)}, u32[]{:S(2)}) collective-permute-start(bf16[2048,256]{1,0:T(8,128)(2,1)S(1)} %bitcast.52), channel_id=1, source_target_pairs={{0,8},{8,0},{1,9},{9,1},{2,10},{10,2},{3,11},{11,3},{4,12},{12,4},... | collective-permute-start | bytes 3145736 | tf_op jit(solution)/shard_map/ppermute | solution.py:53
  117.4 5.7 %collective-permute-start.6 = (bf16[64,512]{1,0:T(8,128)(2,1)S(1)}, bf16[64,512]{1,0:T(8,128)(2,1)S(1)}, u32[]{:S(2)}, u32[]{:S(2)}) collective-permute-start(bf16[64,512]{1,0:T(8,128)(2,1)S(1)} %squeeze.58), channel_id=1, source_target_pairs={{0,1},{1,0},{2,3},{3,2},{4,5},{5,4},{6,7},{7,6},{8,9},{9,8},{10,11... | collective-permute-start | bytes 196616 | tf_op jit(solution)/shard_map/ppermute | solution.py:57
  123.1 3.8 %collective-permute-start.7 = (bf16[128,512]{1,0:T(8,128)(2,1)S(1)}, bf16[128,512]{1,0:T(8,128)(2,1)S(1)}, u32[]{:S(2)}, u32[]{:S(2)}) collective-permute-start(bf16[128,512]{1,0:T(8,128)(2,1)S(1)} %pad_maximum_fusion.5), channel_id=1, source_target_pairs={{0,8},{8,0},{1,9},{9,1},{2,10},{10,2},{3,11},{11,3},{4,12},{12,4},... | collective-permute-start | bytes 393224 | tf_op jit(solution)/shard_map/ppermute | solution.py:53
  130.3 24.2 %copy-start.5 = (bf16[1,2,16,1024]{3,2,1,0:T(8,128)(2,1)S(1)}, bf16[1,2,16,1024]{3,2,1,0:T(8,128)(2,1)}, u32[]{:S(2)}) copy-start(bf16[1,2,16,1024]{3,2,1,0:T(8,128)(2,1)} %reduce-scatter.2.cloned.1.call-done) | copy-start | bytes 196612
  130.3 17.6 %all-to-all-start.2 = ((bf16[8,256,256]{1,2,0:T(8,128)(2,1)}), bf16[8,256,256]{1,2,0:T(8,128)(2,1)S(1)}, u32[]{:S(2)}, u32[]{:S(2)}) async-start(bf16[8,256,256]{1,2,0:T(8,128)(2,1)} %fusion), calls=%async_computation.3 | async-start | bytes 2097152 | tf_op jit(solution)/shard_map/all_to_all | solution.py:282
  148.1 7.3 %collective-permute-start.8 = (bf16[128,256]{0,1:T(8,128)(2,1)S(1)}, bf16[128,256]{0,1:T(8,128)(2,1)S(1)}, u32[]{:S(2)}, u32[]{:S(2)}) collective-permute-start(bf16[128,256]{0,1:T(8,128)(2,1)S(1)} %slice.67), channel_id=1, source_target_pairs={{0,8},{8,0},{1,9},{9,1},{2,10},{10,2},{3,11},{11,3},{4,12},{12,4},... | collective-permute-start | bytes 196616 | tf_op jit(solution)/shard_map/ppermute | solution.py:53
Sparse Core Ops, SparseCore 0:
  32.8 46.1 all-gather.2
  81.1 43.9 all-gather.4
Sparse Core Ops, SparseCore 1:
  47.3 57.1 reduce-scatter.1

commit v9 on v8

--- a/solution.py
+++ b/solution.py
@@ -138,6 +138,33 @@
         compiler_params=pltpu.CompilerParams(vmem_limit_bytes=40 << 20),
         name="attend",
     )(queries, near, far, qpos, kpos)
+
+
+def project_kernel(context_ref, weight_ref, out_ref, turned_ref):
+    @pl.when(pl.program_id(0) == 0)
+    def _():
+        turned_ref[...] = context_ref[...].astype(jnp.float32).T.astype(jnp.bfloat16)
+
+    product = jnp.dot(weight_ref[...], turned_ref[...], preferred_element_type=jnp.float32)
+    out_ref[...] = product.astype(jnp.bfloat16).reshape(out_ref.shape)
+
+
+def project(context, weight, groups):
+    rows, width = context.shape
+    cols = weight.shape[0] // groups
+    step = 2
+    return pl.pallas_call(
+        project_kernel,
+        grid=(groups // step,),
+        in_specs=[
+            pl.BlockSpec((rows, width), lambda i: (0, 0)),
+            pl.BlockSpec((step * cols, width), lambda i: (i, 0)),
+        ],
+        out_specs=pl.BlockSpec((step, cols, rows), lambda i: (i, 0, 0)),
+        out_shape=jax.ShapeDtypeStruct((groups, cols, rows), jnp.bfloat16),
+        scratch_shapes=[pltpu.VMEM((width, rows), jnp.bfloat16)],
+        name="project",
+    )(context, weight)
 
 
 def pages_kernel(page_ref, dest_ref, slot_ref, cache_ref, send_ref):
@@ -273,13 +300,9 @@
     )
     context = jnp.concatenate([context, swap_core(context)], axis=0)
     context, wo_near = lax.optimization_barrier((context, wo_near))
-    send = jnp.einsum(
-        "td,gnd->gtn",
-        context,
-        wo_near.reshape(rows_y, rows_z * piece, -1),
-        preferred_element_type=jnp.float32,
-    ).astype(jnp.bfloat16)
+    send = project(context, wo_near, rows_y)
     terms = lax.all_to_all(send, REP, split_axis=0, concat_axis=0, tiled=True)
+    terms = jnp.swapaxes(terms, 1, 2)
     summed = jnp.sum(terms.astype(jnp.float32), axis=0).astype(jnp.bfloat16)
     near_cols = summed[: 2 * span].reshape(2 * span, rows_z, piece)
     far_cols = swap_core(summed[2 * span :]).reshape(2 * span, rows_z, piece)

time: 167 us -> 169 us (1.012)
  matrix products: 7.4 us -> 3.03 us
  Pallas kernels: 8.64 us -> 13 us
  other arithmetic: 5.17 us -> 7 us
    reduce_scatter x1, waiting for transfers between devices: 8.3 us -> 0.97 us  [on_device(): arrived = lax.psum_scatter(send_pages, REP, scatter_dimension=0, tiled=True)]
    all_to_all x2, waiting for transfers between devices: 8.79 us -> 13.3 us  [spread(): return lax.all_to_all(copies, axes, split_axis=0, concat_axis=0, tiled=True)]
    pallas_call x0 -> x1, Pallas kernels: none -> 4.35 us  [project(): pl.pallas_call(project_kernel, grid=(groups // step,), in_specs=[pl.Block...]
    all_to_all x1, waiting for transfers between devices: 11.1 us -> 14.8 us  [on_device(): terms = lax.all_to_all(send, REP, split_axis=0, concat_axis=0, tiled=True)]
    dot_general x1 -> x0, matrix products: 3.31 us -> none  [on_device(): jnp.einsum('td,gnd->gtn', context, wo_near.reshape(rows_y, rows_z * piece...]
  transfers between devices with their start and end apart: 15 -> 15, of which waited for: 11 -> 12; matrix products, arithmetic and copies ran while one was open for 7% -> 7% of each run, Pallas kernels for 5% -> 5%
where the time goes in v9:
time: 169 us; the launch traced here: 166 us
  starting transfers between devices  59.8 us (35%)
  waiting for transfers between devices  39 us (23%)
  blocking collectives  22 us (13%)
  between operations  16 us (9%)
  Pallas kernels  13 us (8%)
  other arithmetic  7 us (4%)
  local copies, waits for them, and re-layouts  6.14 us (4%)
  matrix products  3.03 us (2%)
    ppermute x6, starting transfers between devices, swap_core(): return lax.ppermute(value, 'core', [(0, 1), (1, 0)])  31.9 us
    all_gather x1, blocking collectives, on_device(): weights = lax.all_gather(weights, 'zh', axis=0, tiled=True)  22 us
    all_to_all x1, waiting for transfers between devices, on_device(): terms = lax.all_to_all(send, REP, split_axis=0, concat_axis=0, tiled=True)  14.8 us
    all_to_all x2, waiting for transfers between devices, spread(): return lax.all_to_all(copies, axes, split_axis=0, concat_axis=0, tiled=True)  13.3 us
    all_to_all x2, starting transfers between devices, spread(): return lax.all_to_all(copies, axes, split_axis=0, concat_axis=0, tiled=True)  10.7 us
    ppermute x3, starting transfers between devices, swap_x(): lax.ppermute(value, 'x', [(i, i ^ 1) for i in range(lax.axis_size('x'))])  9.37 us
    all_to_all x1, starting transfers between devices, on_device(): terms = lax.all_to_all(send, REP, split_axis=0, concat_axis=0, tiled=True)  7.72 us
    pallas_call x1, Pallas kernels, attend(): pl.pallas_call(attend_kernel, grid=(rows // tile,), in_specs=[pl.BlockSpe...  6 us
  transfers between devices with their start and end apart: 15, of which 12 were waited for; matrix products, arithmetic and copies ran while one was open for 7% of the time, Pallas kernels for 5%

profile of v9, /device:TPU:1, one launch (start us, length us, event | category | flops | bytes accessed | tf_op | source)
XLA Modules:
  0.0 166.1 jit_solution(11068748384029103625)
XLA Ops:
  9.8 22.0 %all_gather.9 = bf16[256,1152]{1,0:T(8,128)(2,1)S(1)} all-gather(bf16[64,1152]{1,0:T(8,128)(2,1)S(1)} %pad_maximum_fusion.2), channel_id=1, replica_groups=mesh['y'=8,'zh'=4,'core'=2,'zl'=2,'x'=4] {'zh'}, dimensions={0}, use_global_device_ids=true | all-gather | bytes 737280 | tf_op jit(solution)/shard_map/all_gather | solution.py:240
  33.6 6.8 %all-to-all-start = ((bf16[8,256,128]{2,1,0:T(8,128)(2,1)}), bf16[8,256,128]{2,1,0:T(8,128)(2,1)S(1)}, u32[]{:S(2)}, u32[]{:S(2)}) async-start(bf16[8,256,128]{2,1,0:T(8,128)(2,1)} %broadcast_in_dim.20), calls=%async_computation | async-start | bytes 1048576 | tf_op jit(solution)/shard_map/all_to_all | solution.py:49
  40.5 1.2 split_norm.1
  41.8 4.0 %collective-permute-start.2 = (bf16[128,2048]{1,0:T(8,128)(2,1)S(1)}, bf16[128,2048]{1,0:T(8,128)(2,1)}, u32[]{:S(2)}, u32[]{:S(2)}) collective-permute-start(bf16[128,2048]{1,0:T(8,128)(2,1)S(1)} %get-tuple-element.22), channel_id=1, source_target_pairs={{0,8},{8,0},{1,9},{9,1},{2,10},{10,2},{3,11},{11,3},{4,12},{12,4},... | collective-permute-start | bytes 1572872 | tf_op jit(solution)/shard_map/ppermute | solution.py:53
  45.8 1.4 pages_to_send.1
  47.4 8.7 %all-to-all-done = bf16[8,256,128]{2,1,0:T(8,128)(2,1)S(1)} async-done(((bf16[8,256,128]{2,1,0:T(8,128)(2,1)}), bf16[8,256,128]{2,1,0:T(8,128)(2,1)S(1)}, u32[]{:S(2)}, u32[]{:S(2)}) %all-to-all-start) | async-done | bytes 524320 | tf_op jit(solution)/shard_map/all_to_all | solution.py:49
  56.1 7.5 %collective-permute-start = (bf16[2048,128]{1,0:T(8,128)(2,1)S(1)}, bf16[2048,128]{1,0:T(8,128)(2,1)S(1)}, u32[]{:S(2)}, u32[]{:S(2)}) collective-permute-start(bf16[2048,128]{1,0:T(8,128)(2,1)S(1)} %bitcast.55), channel_id=1, source_target_pairs={{0,8},{8,0},{1,9},{9,1},{2,10},{10,2},{3,11},{11,3},{4,12},{12,4},... | collective-permute-start | bytes 1572872 | tf_op jit(solution)/shard_map/ppermute | solution.py:53
  65.8 3.1 %collective-permute-start.1 = (bf16[64,128]{1,0:T(8,128)(2,1)S(1)}, bf16[64,128]{1,0:T(8,128)(2,1)S(1)}, u32[]{:S(2)}, u32[]{:S(2)}) collective-permute-start(bf16[64,128]{1,0:T(8,128)(2,1)S(1)} %get-tuple-element.53), channel_id=1, source_target_pairs={{0,1},{1,0},{2,3},{3,2},{4,5},{5,4},{6,7},{7,6},{8,9},{9,8},{10,11... | collective-permute-start | bytes 49160 | tf_op jit(solution)/shard_map/ppermute | solution.py:57
  71.8 3.9 %all-to-all-start.1 = ((bf16[32,64,256]{2,1,0:T(8,128)(2,1)}), bf16[32,64,256]{2,1,0:T(8,128)(2,1)S(1)}, u32[]{:S(2)}, u32[]{:S(2)}) async-start(bf16[32,64,256]{2,1,0:T(8,128)(2,1)} %broadcast_in_dim.24), calls=%async_computation.1 | async-start | bytes 2097152 | tf_op jit(solution)/shard_map/all_to_all | solution.py:49
  76.5 1.6 all-gather.3.cloned.1.call-done
  78.1 2.3 %fusion.13 = f32[256,512]{1,0:T(8,128)S(1)} fusion(bf16[256,2048]{1,0:T(8,128)(2,1)S(1)} %pad_maximum_fusion, bf16[2048,512]{1,0:T(8,128)(2,1)} %all-gather.3.cloned.1.call-done), kind=kOutput, calls=%fused_computation.55 | convolution fusion | flops 536870912 | bytes 3670016 | tf_op jit(solution)/shard_map/dot_general | solution.py:43
  80.5 9.2 %collective-permute-start.3 = (f32[128,512]{1,0:T(8,128)S(1)}, f32[128,512]{1,0:T(8,128)S(1)}, u32[]{:S(2)}, u32[]{:S(2)}) collective-permute-start(f32[128,512]{1,0:T(8,128)S(1)} %slice.61), channel_id=1, source_target_pairs={{0,8},{8,0},{1,9},{9,1},{2,10},{10,2},{3,11},{11,3},{4,12},{12,4},... | collective-permute-start | bytes 786440 | tf_op jit(solution)/shard_map/ppermute | solution.py:53
  91.5 2.9 %collective-permute-start.4 = (bf16[64,512]{1,0:T(8,128)(2,1)S(1)}, bf16[64,512]{1,0:T(8,128)(2,1)S(1)}, u32[]{:S(2)}, u32[]{:S(2)}) collective-permute-start(bf16[64,512]{1,0:T(8,128)(2,1)S(1)} %get-tuple-element.49), channel_id=1, source_target_pairs={{0,1},{1,0},{2,3},{3,2},{4,5},{5,4},{6,7},{7,6},{8,9},{9,8},{10,11... | collective-permute-start | bytes 196616 | tf_op jit(solution)/shard_map/ppermute | solution.py:57
  95.4 1.6 collective-permute-done.4
  98.0 4.6 %all-to-all-done.1 = bf16[32,64,256]{2,1,0:T(8,128)(2,1)S(1)} async-done(((bf16[32,64,256]{2,1,0:T(8,128)(2,1)}), bf16[32,64,256]{2,1,0:T(8,128)(2,1)S(1)}, u32[]{:S(2)}, u32[]{:S(2)}) %all-to-all-start.1) | async-done | bytes 1048608 | tf_op jit(solution)/shard_map/all_to_all | solution.py:49
  102.7 5.5 %collective-permute-start.5 = (bf16[2048,256]{1,0:T(8,128)(2,1)S(1)}, bf16[2048,256]{1,0:T(8,128)(2,1)S(1)}, u32[]{:S(2)}, u32[]{:S(2)}) collective-permute-start(bf16[2048,256]{1,0:T(8,128)(2,1)S(1)} %bitcast.46), channel_id=1, source_target_pairs={{0,8},{8,0},{1,9},{9,1},{2,10},{10,2},{3,11},{11,3},{4,12},{12,4},... | collective-permute-start | bytes 3145736 | tf_op jit(solution)/shard_map/ppermute | solution.py:53
  110.5 6.0 %attend.1 = bf16[512,128]{1,0:T(8,128)(2,1)S(1)} custom-call(bf16[512,128]{1,0:T(8,128)(2,1)S(1)} %reshape.289.q_ref, bf16[2048,256]{1,0:T(8,128)(2,1)S(1)} %bitcast.47, bf16[2048,256]{1,0:T(8,128)(2,1)S(1)} %collective-permute-done.5.far_ref, s32[512,1]{1,0:T(8,128)S(1)} %reshape.294.qpos_ref, s32[1,4096]{1,0:T(1,128)S(1)} %add.127.kpos_ref), custom_call_target="tpu_custom_call" | custom-call | tf_op jit(solution)/shard_map/attend/pallas_call | solution.py:126
  116.6 3.3 %collective-permute-start.6 = (bf16[64,512]{1,0:T(8,128)(2,1)S(1)}, bf16[64,512]{1,0:T(8,128)(2,1)S(1)}, u32[]{:S(2)}, u32[]{:S(2)}) collective-permute-start(bf16[64,512]{1,0:T(8,128)(2,1)S(1)} %squeeze.58), channel_id=1, source_target_pairs={{0,1},{1,0},{2,3},{3,2},{4,5},{5,4},{6,7},{7,6},{8,9},{9,8},{10,11... | collective-permute-start | bytes 196616 | tf_op jit(solution)/shard_map/ppermute | solution.py:57
  119.9 2.0 %collective-permute-done.6 = bf16[64,512]{1,0:T(8,128)(2,1)S(1)} collective-permute-done((bf16[64,512]{1,0:T(8,128)(2,1)S(1)}, bf16[64,512]{1,0:T(8,128)(2,1)S(1)}, u32[]{:S(2)}, u32[]{:S(2)}) %collective-permute-start.6) | collective-permute-done | bytes 65568 | tf_op jit(solution)/shard_map/ppermute | solution.py:57
  122.0 3.0 %collective-permute-start.7 = (bf16[128,512]{1,0:T(8,128)(2,1)S(1)}, bf16[128,512]{1,0:T(8,128)(2,1)S(1)}, u32[]{:S(2)}, u32[]{:S(2)}) collective-permute-start(bf16[128,512]{1,0:T(8,128)(2,1)S(1)} %pad_maximum_fusion.5), channel_id=1, source_target_pairs={{0,8},{8,0},{1,9},{9,1},{2,10},{10,2},{3,11},{11,3},{4,12},{12,4},... | collective-permute-start | bytes 393224 | tf_op jit(solution)/shard_map/ppermute | solution.py:53
  126.7 4.3 %project.1 = bf16[8,256,256]{2,1,0:T(8,128)(2,1)} custom-call(bf16[256,512]{1,0:T(8,128)(2,1)} %pad_maximum_fusion.1.context_ref, bf16[2048,512]{1,0:T(8,128)(2,1)} %all-gather.5.cloned.1.call-done.weight_ref), custom_call_target="tpu_custom_call" | custom-call | tf_op jit(solution)/shard_map/project/pallas_call | solution.py:156
  131.1 7.7 %all-to-all-start.2 = ((bf16[8,256,256]{2,1,0:T(8,128)(2,1)}), bf16[8,256,256]{2,1,0:T(8,128)(2,1)S(1)}, u32[]{:S(2)}, u32[]{:S(2)}) async-start(bf16[8,256,256]{2,1,0:T(8,128)(2,1)} %project.1), calls=%async_computation.3 | async-start | bytes 2097152 | tf_op jit(solution)/shard_map/all_to_all | solution.py:304
  139.0 14.8 %all-to-all-done.2 = bf16[8,256,256]{2,1,0:T(8,128)(2,1)S(1)} async-done(((bf16[8,256,256]{2,1,0:T(8,128)(2,1)}), bf16[8,256,256]{2,1,0:T(8,128)(2,1)S(1)}, u32[]{:S(2)}, u32[]{:S(2)}) %all-to-all-start.2) | async-done | bytes 1048608 | tf_op jit(solution)/shard_map/all_to_all | solution.py:304
  153.9 2.7 %collective-permute-start.8 = (bf16[128,256]{0,1:T(8,128)(2,1)S(1)}, bf16[128,256]{0,1:T(8,128)(2,1)S(1)}, u32[]{:S(2)}, u32[]{:S(2)}) collective-permute-start(bf16[128,256]{0,1:T(8,128)(2,1)S(1)} %slice.67), channel_id=1, source_target_pairs={{0,8},{8,0},{1,9},{9,1},{2,10},{10,2},{3,11},{11,3},{4,12},{12,4},... | collective-permute-start | bytes 196616 | tf_op jit(solution)/shard_map/ppermute | solution.py:53
  (98 shorter events, 19.7 us)
Async XLA Ops:
  8.0 70.1 %all-gather.3.cloned.1.call-start = ((), (), s32[]{:S(2)}) async-start(), calls=%async_computation.4 | async-start | bytes 2359296 | tf_op jit(solution)/shard_map/all_gather | solution.py:245
  8.1 32.4 %copy-start.6 = (bf16[4096]{0:T(1024)(128)(2,1)S(1)}, bf16[4096]{0:T(1024)(128)(2,1)}, u32[]{:S(2)}) copy-start(bf16[4096]{0:T(1024)(128)(2,1)} %param.13) | copy-start | bytes 24580
  8.1 32.4 %copy-start.1 = (bf16[2,1,2,32,4096]{4,3,2,1,0:T(8,128)(2,1)S(1)}, bf16[2,1,2,32,4096]{4,3,2,1,0:T(8,128)(2,1)}, u32[]{:S(2)}) copy-start(bf16[2,1,2,32,4096]{4,3,2,1,0:T(8,128)(2,1)} %param.12) | copy-start | bytes 3145732
  31.9 13.9 %copy-start = (bf16[1,1,16,16,1024]{4,3,2,1,0:T(8,128)(2,1)S(1)}, bf16[1,1,16,16,1024]{4,3,2,1,0:T(8,128)(2,1)}, u32[]{:S(2)}) copy-start(bf16[1,1,16,16,1024]{4,3,2,1,0:T(8,128)(2,1)} %param.20) | copy-start | bytes 1572868
  31.9 13.9 %copy-start.2 = (s32[1,1,2]{2,1,0:T(1,128)S(1)}, s32[1,1,2]{2,1,0:T(1,128)}, u32[]{:S(2)}) copy-start(s32[1,1,2]{2,1,0:T(1,128)} %param.22) | copy-start | bytes 28
  31.9 13.9 %copy-start.3 = (s32[1,1,2]{2,1,0:T(1,128)S(1)}, s32[1,1,2]{2,1,0:T(1,128)}, u32[]{:S(2)}) copy-start(s32[1,1,2]{2,1,0:T(1,128)} %param.23) | copy-start | bytes 28
  31.9 14.0 %copy-start.4 = (s32[1,1,2]{2,1,0:T(1,128)S(1)}, s32[1,1,2]{2,1,0:T(1,128)}, u32[]{:S(2)}) copy-start(s32[1,1,2]{2,1,0:T(1,128)} %param.21) | copy-start | bytes 28
  32.7 14.5 %copy-start.7 = (s32[2,64]{1,0:T(2,128)S(1)}, s32[2,64]{1,0:T(2,128)}, u32[]{:S(2)}) copy-start(s32[2,64]{1,0:T(2,128)} %param.19) | copy-start | bytes 1540
  33.6 22.5 %all-to-all-start = ((bf16[8,256,128]{2,1,0:T(8,128)(2,1)}), bf16[8,256,128]{2,1,0:T(8,128)(2,1)S(1)}, u32[]{:S(2)}, u32[]{:S(2)}) async-start(bf16[8,256,128]{2,1,0:T(8,128)(2,1)} %broadcast_in_dim.20), calls=%async_computation | async-start | bytes 1048576 | tf_op jit(solution)/shard_map/all_to_all | solution.py:49
  40.4 57.6 %reduce-scatter.2.cloned.1.call-start = ((), (), s32[]{:S(2)}) async-start(), calls=%async_computation.5 | async-start | bytes 589824 | tf_op jit(solution)/shard_map/reduce_scatter | solution.py:249
  41.8 27.2 %collective-permute-start.2 = (bf16[128,2048]{1,0:T(8,128)(2,1)S(1)}, bf16[128,2048]{1,0:T(8,128)(2,1)}, u32[]{:S(2)}, u32[]{:S(2)}) collective-permute-start(bf16[128,2048]{1,0:T(8,128)(2,1)S(1)} %get-tuple-element.22), channel_id=1, source_target_pairs={{0,8},{8,0},{1,9},{9,1},{2,10},{10,2},{3,11},{11,3},{4,12},{12,4},... | collective-permute-start | bytes 1572872 | tf_op jit(solution)/shard_map/ppermute | solution.py:53
  56.1 9.0 %collective-permute-start = (bf16[2048,128]{1,0:T(8,128)(2,1)S(1)}, bf16[2048,128]{1,0:T(8,128)(2,1)S(1)}, u32[]{:S(2)}, u32[]{:S(2)}) collective-permute-start(bf16[2048,128]{1,0:T(8,128)(2,1)S(1)} %bitcast.55), channel_id=1, source_target_pairs={{0,8},{8,0},{1,9},{9,1},{2,10},{10,2},{3,11},{11,3},{4,12},{12,4},... | collective-permute-start | bytes 1572872 | tf_op jit(solution)/shard_map/ppermute | solution.py:53
  65.8 4.9 %collective-permute-start.1 = (bf16[64,128]{1,0:T(8,128)(2,1)S(1)}, bf16[64,128]{1,0:T(8,128)(2,1)S(1)}, u32[]{:S(2)}, u32[]{:S(2)}) collective-permute-start(bf16[64,128]{1,0:T(8,128)(2,1)S(1)} %get-tuple-element.53), channel_id=1, source_target_pairs={{0,1},{1,0},{2,3},{3,2},{4,5},{5,4},{6,7},{7,6},{8,9},{9,8},{10,11... | collective-permute-start | bytes 49160 | tf_op jit(solution)/shard_map/ppermute | solution.py:57
  71.8 30.8 %all-to-all-start.1 = ((bf16[32,64,256]{2,1,0:T(8,128)(2,1)}), bf16[32,64,256]{2,1,0:T(8,128)(2,1)S(1)}, u32[]{:S(2)}, u32[]{:S(2)}) async-start(bf16[32,64,256]{2,1,0:T(8,128)(2,1)} %broadcast_in_dim.24), calls=%async_computation.1 | async-start | bytes 2097152 | tf_op jit(solution)/shard_map/all_to_all | solution.py:49
  75.8 51.0 %all-gather.5.cloned.1.call-start = ((), (), s32[]{:S(2)}) async-start(), calls=%async_computation.6 | async-start | bytes 2359296 | tf_op jit(solution)/shard_map/all_gather | solution.py:254
  80.5 14.1 %copy-start.8 = (s32[2]{0:T(128)S(1)}, s32[2]{0:T(128)}, u32[]{:S(2)}) copy-start(s32[2]{0:T(128)} %param.18) | copy-start | bytes 28
  80.5 10.3 %collective-permute-start.3 = (f32[128,512]{1,0:T(8,128)S(1)}, f32[128,512]{1,0:T(8,128)S(1)}, u32[]{:S(2)}, u32[]{:S(2)}) collective-permute-start(f32[128,512]{1,0:T(8,128)S(1)} %slice.61), channel_id=1, source_target_pairs={{0,8},{8,0},{1,9},{9,1},{2,10},{10,2},{3,11},{11,3},{4,12},{12,4},... | collective-permute-start | bytes 786440 | tf_op jit(solution)/shard_map/ppermute | solution.py:53
  91.5 5.4 %collective-permute-start.4 = (bf16[64,512]{1,0:T(8,128)(2,1)S(1)}, bf16[64,512]{1,0:T(8,128)(2,1)S(1)}, u32[]{:S(2)}, u32[]{:S(2)}) collective-permute-start(bf16[64,512]{1,0:T(8,128)(2,1)S(1)} %get-tuple-element.49), channel_id=1, source_target_pairs={{0,1},{1,0},{2,3},{3,2},{4,5},{5,4},{6,7},{7,6},{8,9},{9,8},{10,11... | collective-permute-start | bytes 196616 | tf_op jit(solution)/shard_map/ppermute | solution.py:57
  102.7 7.8 %collective-permute-start.5 = (bf16[2048,256]{1,0:T(8,128)(2,1)S(1)}, bf16[2048,256]{1,0:T(8,128)(2,1)S(1)}, u32[]{:S(2)}, u32[]{:S(2)}) collective-permute-start(bf16[2048,256]{1,0:T(8,128)(2,1)S(1)} %bitcast.46), channel_id=1, source_target_pairs={{0,8},{8,0},{1,9},{9,1},{2,10},{10,2},{3,11},{11,3},{4,12},{12,4},... | collective-permute-start | bytes 3145736 | tf_op jit(solution)/shard_map/ppermute | solution.py:53
  116.6 5.4 %collective-permute-start.6 = (bf16[64,512]{1,0:T(8,128)(2,1)S(1)}, bf16[64,512]{1,0:T(8,128)(2,1)S(1)}, u32[]{:S(2)}, u32[]{:S(2)}) collective-permute-start(bf16[64,512]{1,0:T(8,128)(2,1)S(1)} %squeeze.58), channel_id=1, source_target_pairs={{0,1},{1,0},{2,3},{3,2},{4,5},{5,4},{6,7},{7,6},{8,9},{9,8},{10,11... | collective-permute-start | bytes 196616 | tf_op jit(solution)/shard_map/ppermute | solution.py:57
  122.0 4.0 %collective-permute-start.7 = (bf16[128,512]{1,0:T(8,128)(2,1)S(1)}, bf16[128,512]{1,0:T(8,128)(2,1)S(1)}, u32[]{:S(2)}, u32[]{:S(2)}) collective-permute-start(bf16[128,512]{1,0:T(8,128)(2,1)S(1)} %pad_maximum_fusion.5), channel_id=1, source_target_pairs={{0,8},{8,0},{1,9},{9,1},{2,10},{10,2},{3,11},{11,3},{4,12},{12,4},... | collective-permute-start | bytes 393224 | tf_op jit(solution)/shard_map/ppermute | solution.py:53
  131.1 25.6 %copy-start.5 = (bf16[1,2,16,1024]{3,2,1,0:T(8,128)(2,1)S(1)}, bf16[1,2,16,1024]{3,2,1,0:T(8,128)(2,1)}, u32[]{:S(2)}) copy-start(bf16[1,2,16,1024]{3,2,1,0:T(8,128)(2,1)} %reduce-scatter.2.cloned.1.call-done) | copy-start | bytes 196612
  131.1 22.7 %all-to-all-start.2 = ((bf16[8,256,256]{2,1,0:T(8,128)(2,1)}), bf16[8,256,256]{2,1,0:T(8,128)(2,1)S(1)}, u32[]{:S(2)}, u32[]{:S(2)}) async-start(bf16[8,256,256]{2,1,0:T(8,128)(2,1)} %project.1), calls=%async_computation.3 | async-start | bytes 2097152 | tf_op jit(solution)/shard_map/all_to_all | solution.py:304
  153.9 3.6 %collective-permute-start.8 = (bf16[128,256]{0,1:T(8,128)(2,1)S(1)}, bf16[128,256]{0,1:T(8,128)(2,1)S(1)}, u32[]{:S(2)}, u32[]{:S(2)}) collective-permute-start(bf16[128,256]{0,1:T(8,128)(2,1)S(1)} %slice.67), channel_id=1, source_target_pairs={{0,8},{8,0},{1,9},{9,1},{2,10},{10,2},{3,11},{11,3},{4,12},{12,4},... | collective-permute-start | bytes 196616 | tf_op jit(solution)/shard_map/ppermute | solution.py:53
Sparse Core Ops, SparseCore 0:
  32.8 45.2 all-gather.2
  80.2 44.4 all-gather.4
Sparse Core Ops, SparseCore 1:
  47.3 50.6 reduce-scatter.1
